TPU v7x, 32 devices: a whole 2x2x4 slice. The times are simulated.
32 devices in a mesh: rows: 2 (over y), seq: 16 (over z, x, core).
Axes of the slice: x: 2, y: 2, z: 4, core: 2. Of those that a mesh axis runs over, the one named last changes fastest.
Arguments:
- tokens: bfloat16 [2, 2048, 2304], P('rows', 'seq'), may hold values from -6 to 6
- cotangent: bfloat16 [2, 2048, 2304], P('rows', 'seq'), may hold values from -6 to 6
- doc_ids: int32 [2, 2048], P('rows'), may hold values from 0 to 3, as said below
- bit_levels: int32 [7], replicated, may hold values from 0 to 2, as said below
- w_query: int32 [2304, 2048], P(('rows', 'seq')), may hold values from -128 to 127
- w_key: int32 [2304, 1024], P(('rows', 'seq')), may hold values from -128 to 127
- w_value: int32 [2304, 1024], P(('rows', 'seq')), may hold values from -128 to 127
- w_proj: int32 [2304, 2048], P(('rows', 'seq')), may hold values from -128 to 127
- w_gate: int32 [2304, 9216], P(('rows', 'seq')), may hold values from -128 to 127
- w_up: int32 [2304, 9216], P(('rows', 'seq')), may hold values from -128 to 127
- w_down: int32 [2304, 9216], P(('rows', 'seq')), may hold values from -128 to 127
- gain_first: float32 [2304], replicated, may hold values from -0.5 to 0.5
- gain_second: float32 [2304], replicated, may hold values from -0.5 to 0.5
- gain_third: float32 [2304], replicated, may hold values from -0.5 to 0.5
- gain_fourth: float32 [2304], replicated, may hold values from -0.5 to 0.5
Outputs:
- layer_out: bfloat16 [2, 2048, 2304], P('rows', 'seq')
- grad_tokens: float32 [2, 2048, 2304], P('rows', 'seq')
- grad_query: float32 [2304, 2048], P(('rows', 'seq'))
- grad_key: float32 [2304, 1024], P(('rows', 'seq'))
- grad_value: float32 [2304, 1024], P(('rows', 'seq'))
- grad_proj: float32 [2304, 2048], P(('rows', 'seq'))
- grad_gate: float32 [2304, 9216], P(('rows', 'seq'))
- grad_up: float32 [2304, 9216], P(('rows', 'seq'))
- grad_down: float32 [2304, 9216], P(('rows', 'seq'))
- grad_first: float32 [2304], P(('rows', 'seq'))
- grad_second: float32 [2304], P(('rows', 'seq'))
- grad_third: float32 [2304], P(('rows', 'seq'))
- grad_fourth: float32 [2304], P(('rows', 'seq'))
Inputs may be any that keep to these rules, and one draw needn't show every extreme that they name: `doc_ids`: ids never fall along a row. Rows of even index hold one document (id 0); rows of odd index hold up to four, and their last token has id 3. `bit_levels`: level 0 occurs three times, levels 1 and 2 twice each.
All inputs are finite; a program needn't handle non-finite values.
Results may differ from a plain program's by a relative error of at most 0.019.
The roundings to bfloat16 on the way count: a program that leaves them out, or rounds other values in their place, can miss the bound.
Values may be sent and summed in bfloat16 or wider, within the bound.
A program may use at most 448 MiB of HBM per device.

v0:
```python
import math

import jax
import jax.numpy as jnp
from jax import lax
from jax.sharding import PartitionSpec as P

D = 2304
FF = 9216
HEADS = 8
KV_HEADS = 4
HEAD_DIM = 256


softcap = 50.0
epsilon = 1e-06
qk_boost = 1.65


def dequant(levels_int, level_idx, fan_in, boost):
    stride = jnp.where(level_idx == 0, 1, jnp.where(level_idx == 1, 16, 64)).astype(jnp.int32)
    sliced = levels_int // stride * stride + stride // 2
    return sliced.astype(jnp.float32) * (boost / (74.0 * math.sqrt(fan_in)))


def rmsnorm(values, gain_vec):
    return (
        values
        * lax.rsqrt(jnp.mean(values * values, axis=-1, keepdims=True) + epsilon)
        * (1.0 + gain_vec)
    )


def rotate(values, positions, direction):
    half_dim = HEAD_DIM // 2
    frequency = 10000.0 ** (-(2.0 / HEAD_DIM) * jnp.arange(half_dim, dtype=jnp.float32))
    angles = positions.astype(jnp.float32)[:, None] * frequency[None, :]
    cosine = jnp.cos(angles)[:, None, :]
    sine = jnp.sin(angles)[:, None, :] * direction
    front_half = values[..., :half_dim]
    back_half = values[..., half_dim:]
    return jnp.concatenate(
        [front_half * cosine - back_half * sine, back_half * cosine + front_half * sine], axis=-1
    )


def gelu_product(gate_vals, up_vals):
    return jax.nn.gelu(gate_vals, approximate=True) * up_vals


def per_device(
    tokens,
    cotangent,
    doc_ids,
    bit_levels,
    w_query,
    w_key,
    w_value,
    w_proj,
    w_gate,
    w_up,
    w_down,
    gain_first,
    gain_second,
    gain_third,
    gain_fourth,
):
    rows_here = tokens.shape[0]
    seq_block = tokens.shape[1]
    token_count = rows_here * seq_block
    local_rows = w_query.shape[0]
    group_size = HEADS // KV_HEADS
    query_width = HEADS * HEAD_DIM
    key_width = KV_HEADS * HEAD_DIM
    score_scale = HEAD_DIM ** (-0.5)
    offset = lax.axis_index("seq") * seq_block
    positions = offset + jnp.arange(seq_block, dtype=jnp.int32)
    query_docs = lax.dynamic_slice_in_dim(doc_ids, offset, seq_block, 1)
    query_local = dequant(w_query, bit_levels[0], D, qk_boost).astype(jnp.bfloat16)
    key_local = dequant(w_key, bit_levels[1], D, qk_boost).astype(jnp.bfloat16)
    value_local = dequant(w_value, bit_levels[2], D, 1.0).astype(jnp.bfloat16)
    proj_local = dequant(w_proj, bit_levels[3], query_width, 1.0).astype(jnp.bfloat16)
    gate_local = dequant(w_gate, bit_levels[4], D, 1.0).astype(jnp.bfloat16)
    up_local = dequant(w_up, bit_levels[5], D, 1.0).astype(jnp.bfloat16)
    down_local = dequant(w_down, bit_levels[6], FF, 1.0).astype(jnp.bfloat16)
    query_full, key_full, value_full, proj_full = (
        lax.all_gather(query_local, ("rows", "seq"), axis=0, tiled=True),
        lax.all_gather(key_local, ("rows", "seq"), axis=0, tiled=True),
        lax.all_gather(value_local, ("rows", "seq"), axis=0, tiled=True),
        lax.all_gather(proj_local, ("rows", "seq"), axis=0, tiled=True),
    )
    row_groups = lax.axis_size("rows")
    seq_count = lax.axis_size("seq")
    col_width = FF // seq_count
    stacked = jnp.stack([gate_local, up_local, down_local]).reshape(
        3, local_rows, seq_count, col_width
    )
    spread = jnp.concatenate([stacked] * row_groups, axis=2)
    columns_all = lax.all_to_all(
        spread, ("rows", "seq"), split_axis=2, concat_axis=1, tiled=True
    ).reshape(3, D, col_width)
    gate_cols = columns_all[0]
    up_cols = columns_all[1]
    down_cols = columns_all[2]
    flat_tokens = tokens.astype(jnp.float32).reshape(token_count, D)
    normed_low = rmsnorm(flat_tokens, gain_first).astype(jnp.bfloat16)
    query_pre = jnp.dot(normed_low, query_full, preferred_element_type=jnp.float32)
    key_pre = jnp.dot(normed_low, key_full, preferred_element_type=jnp.float32)
    value_low = (
        jnp.dot(normed_low, value_full, preferred_element_type=jnp.float32)
        .astype(jnp.bfloat16)
        .reshape(rows_here, seq_block, KV_HEADS, HEAD_DIM)
    )
    query_rot = (
        rotate(query_pre.reshape(rows_here, seq_block, HEADS, HEAD_DIM), positions, 1.0)
        .astype(jnp.bfloat16)
        .reshape(rows_here, seq_block, KV_HEADS, group_size, HEAD_DIM)
    )
    key_rot = rotate(
        key_pre.reshape(rows_here, seq_block, KV_HEADS, HEAD_DIM), positions, 1.0
    ).astype(jnp.bfloat16)

    def piece_weights(key_piece):
        key_count = key_piece.shape[1]
        key_pos = jnp.arange(key_count, dtype=jnp.int32)
        raw_scores = (
            jnp.einsum(
                "bqgrd,bkgd->bgrqk", query_rot, key_piece, preferred_element_type=jnp.float32
            )
            * score_scale
        )
        allowed = (key_pos[None, :] <= positions[:, None])[None] & (
            doc_ids[:, None, :] == query_docs[:, :, None]
        )
        bent_score = jnp.tanh(raw_scores / softcap)
        weights = jnp.where(allowed[:, None, None], jnp.exp(softcap * bent_score), 0.0)
        return (weights, bent_score)

    key_piece = lax.all_gather(key_rot, "seq", axis=1, tiled=True)
    value_piece = lax.all_gather(value_low, "seq", axis=1, tiled=True)
    weights, bent_score = piece_weights(key_piece)
    summed = jnp.einsum(
        "bgrqk,bkgd->bqgrd",
        weights.astype(jnp.bfloat16),
        value_piece,
        preferred_element_type=jnp.float32,
    )
    totals, summed = (jnp.sum(weights, axis=-1), summed)
    denominator = jnp.transpose(totals, (0, 3, 1, 2))[..., None]
    mixed_out = summed / denominator
    mixed_low = mixed_out.astype(jnp.bfloat16).reshape(token_count, query_width)
    attn_out = jnp.einsum("th,dh->td", mixed_low, proj_full, preferred_element_type=jnp.float32)
    hidden_one = flat_tokens + rmsnorm(attn_out, gain_second)
    mid_low = rmsnorm(hidden_one, gain_third).astype(jnp.bfloat16)
    mid_row = lax.all_gather(mid_low.reshape(rows_here, seq_block, D), "seq", axis=1, tiled=True)
    gate_pre = jnp.einsum("btd,df->btf", mid_row, gate_cols, preferred_element_type=jnp.float32)
    up_pre = jnp.einsum("btd,df->btf", mid_row, up_cols, preferred_element_type=jnp.float32)
    activated = gelu_product(gate_pre, up_pre).astype(jnp.bfloat16)
    ffn_terms = jnp.einsum("btf,df->btd", activated, down_cols, preferred_element_type=jnp.float32)
    ffn_out = lax.psum_scatter(ffn_terms, "seq", scatter_dimension=1, tiled=True).reshape(
        token_count, D
    )
    result = hidden_one + rmsnorm(ffn_out, gain_fourth)
    layer_out = result.astype(jnp.bfloat16).reshape(rows_here, seq_block, D)
    upstream = cotangent.astype(jnp.float32).reshape(token_count, D)
    grad_ffn, fourth_part = jax.vjp(rmsnorm, ffn_out, gain_fourth)[1](upstream)
    grad_ffn_low = grad_ffn.astype(jnp.bfloat16)
    grad_row = lax.all_gather(
        grad_ffn_low.reshape(rows_here, seq_block, D), "seq", axis=1, tiled=True
    )
    grad_act = jnp.einsum("btd,df->btf", grad_row, down_cols, preferred_element_type=jnp.float32)
    grad_gate_pre, grad_up_pre = jax.vjp(gelu_product, gate_pre, up_pre)[1](grad_act)
    grad_gate_low = grad_gate_pre.astype(jnp.bfloat16)
    grad_up_low = grad_up_pre.astype(jnp.bfloat16)
    mid_terms = jnp.einsum(
        "btf,df->btd", grad_gate_low, gate_cols, preferred_element_type=jnp.float32
    ) + jnp.einsum("btf,df->btd", grad_up_low, up_cols, preferred_element_type=jnp.float32)
    grad_mid = lax.psum_scatter(mid_terms, "seq", scatter_dimension=1, tiled=True).reshape(
        token_count, D
    )
    column_terms = jnp.stack(
        [
            jnp.einsum("btd,btf->df", mid_row, grad_gate_low, preferred_element_type=jnp.float32),
            jnp.einsum("btd,btf->df", mid_row, grad_up_low, preferred_element_type=jnp.float32),
            jnp.einsum("btd,btf->df", grad_row, activated, preferred_element_type=jnp.float32),
        ]
    )
    returned = lax.all_to_all(
        column_terms.reshape(3, D, 1, col_width).astype(jnp.bfloat16),
        ("rows", "seq"),
        split_axis=1,
        concat_axis=2,
        tiled=True,
    ).astype(jnp.float32)
    column_sums = jnp.sum(
        returned.reshape(3, local_rows, row_groups, seq_count, col_width), axis=2
    ).reshape(3, local_rows, FF)
    hidden_part, third_part = jax.vjp(rmsnorm, hidden_one, gain_third)[1](grad_mid)
    grad_hidden = upstream + hidden_part
    grad_attn, second_part = jax.vjp(rmsnorm, attn_out, gain_second)[1](grad_hidden)
    grad_attn_low = grad_attn.astype(jnp.bfloat16)
    query_back, key_back, value_back, proj_back = (
        lax.all_gather(query_local, ("rows", "seq"), axis=0, tiled=True),
        lax.all_gather(key_local, ("rows", "seq"), axis=0, tiled=True),
        lax.all_gather(value_local, ("rows", "seq"), axis=0, tiled=True),
        lax.all_gather(proj_local, ("rows", "seq"), axis=0, tiled=True),
    )
    grad_mixed = jnp.dot(grad_attn_low, proj_back, preferred_element_type=jnp.float32).reshape(
        rows_here, seq_block, KV_HEADS, group_size, HEAD_DIM
    )
    grad_summed = (grad_mixed / denominator).astype(jnp.bfloat16)
    delta_rows = jnp.transpose(
        jnp.sum(grad_mixed * mixed_out, axis=-1) / denominator[..., 0], (0, 2, 3, 1)
    )
    key_piece = lax.all_gather(key_rot, "seq", axis=1, tiled=True)
    value_piece = lax.all_gather(value_low, "seq", axis=1, tiled=True)
    key_count = key_piece.shape[1]
    weights, bent_score = piece_weights(key_piece)
    grad_weights = (
        jnp.einsum(
            "bqgrd,bkgd->bgrqk", grad_summed, value_piece, preferred_element_type=jnp.float32
        )
        - delta_rows[..., None]
    )
    grad_raw = (weights * grad_weights * (1.0 - bent_score * bent_score)).astype(jnp.bfloat16)
    grad_queries = (
        jnp.einsum("bgrqk,bkgd->bqgrd", grad_raw, key_piece, preferred_element_type=jnp.float32)
        * score_scale
    )
    key_term = (
        jnp.einsum("bgrqk,bqgrd->bkgd", grad_raw, query_rot, preferred_element_type=jnp.float32)
        * score_scale
    )
    value_term = jnp.einsum(
        "bgrqk,bqgrd->bkgd",
        weights.astype(jnp.bfloat16),
        grad_summed,
        preferred_element_type=jnp.float32,
    )
    key_sums = key_term
    value_sums = value_term
    grad_query_rot, key_sums, value_sums = (grad_queries, key_sums, value_sums)
    grad_key_rot, grad_value_sum = (
        lax.psum_scatter(key_sums, "seq", scatter_dimension=1, tiled=True),
        lax.psum_scatter(value_sums, "seq", scatter_dimension=1, tiled=True),
    )
    grad_query_pre = (
        rotate(grad_query_rot.reshape(rows_here, seq_block, HEADS, HEAD_DIM), positions, -1.0)
        .astype(jnp.bfloat16)
        .reshape(token_count, query_width)
    )
    grad_key_pre = (
        rotate(grad_key_rot, positions, -1.0).astype(jnp.bfloat16).reshape(token_count, key_width)
    )
    grad_value_low = grad_value_sum.astype(jnp.bfloat16).reshape(token_count, key_width)
    grad_in = (
        jnp.einsum("tf,df->td", grad_query_pre, query_back, preferred_element_type=jnp.float32)
        + jnp.einsum("tf,df->td", grad_key_pre, key_back, preferred_element_type=jnp.float32)
        + jnp.einsum("tf,df->td", grad_value_low, value_back, preferred_element_type=jnp.float32)
    )
    tokens_part, first_part = jax.vjp(rmsnorm, flat_tokens, gain_first)[1](grad_in)
    grad_tokens = (grad_hidden + tokens_part).reshape(rows_here, seq_block, D)

    def outer_sum(left_side, right_side):
        return jnp.einsum("td,tf->df", left_side, right_side, preferred_element_type=jnp.float32)

    gain_terms = jnp.stack([first_part, second_part, third_part, fourth_part], axis=1)
    padding = jnp.zeros((D, 124), jnp.float32)
    weight_terms = jnp.concatenate(
        [
            outer_sum(normed_low, grad_query_pre),
            outer_sum(normed_low, grad_key_pre),
            outer_sum(normed_low, grad_value_low),
            outer_sum(grad_attn_low, mixed_low),
            gain_terms,
            padding,
        ],
        axis=1,
    )
    summed_terms = lax.psum_scatter(weight_terms, ("rows", "seq"), scatter_dimension=0, tiled=True)
    widths = [query_width, key_width, key_width, query_width]
    pieces_out = []
    column = 0
    for span_cols in widths:
        pieces_out.append(summed_terms[:, column : column + span_cols])
        column = column + span_cols
    return (
        layer_out,
        grad_tokens,
        pieces_out[0],
        pieces_out[1],
        pieces_out[2],
        pieces_out[3],
        column_sums[0],
        column_sums[1],
        column_sums[2],
        summed_terms[:, column],
        summed_terms[:, column + 1],
        summed_terms[:, column + 2],
        summed_terms[:, column + 3],
    )


def solution(mesh):
    placed = (
        P("rows", "seq", None),
        P("rows", "seq", None),
        P("rows", None),
        P(),
        P(("rows", "seq"), None),
        P(("rows", "seq"), None),
        P(("rows", "seq"), None),
        P(("rows", "seq"), None),
        P(("rows", "seq"), None),
        P(("rows", "seq"), None),
        P(("rows", "seq"), None),
        P(),
        P(),
        P(),
        P(),
    )
    return jax.shard_map(
        per_device,
        mesh=mesh,
        in_specs=placed,
        out_specs=(
            P("rows", "seq", None),
            P("rows", "seq", None),
            P(("rows", "seq"), None),
            P(("rows", "seq"), None),
            P(("rows", "seq"), None),
            P(("rows", "seq"), None),
            P(("rows", "seq"), None),
            P(("rows", "seq"), None),
            P(("rows", "seq"), None),
            P(("rows", "seq")),
            P(("rows", "seq")),
            P(("rows", "seq")),
            P(("rows", "seq")),
        ),
        check_vma=False,
    )
```

profile of v0, /device:TPU:20, one launch (start us, length us, event | category | flops | bytes accessed | tf_op | source)
XLA Modules:
  0.0 2724.8 jit_solution(16148281413889453011)
XLA Ops:
  32.4 46.7 %all-gather.14.cloned.1.call-done = bf16[2304,1024]{1,0:T(8,128)(2,1)} async-done(((bf16[72,1024]{1,0:T(8,128)(2,1)}), bf16[2304,1024]{1,0:T(8,128)(2,1)}) %all-gather.14.cloned.1.call-update) | async-done | bytes 4718608 | tf_op jit(solution)/shard_map/all_gather | solution.py:88
  90.8 54.2 %all-gather.10.cloned.1.call-done = bf16[2304,1024]{1,0:T(8,128)(2,1)} async-done(((bf16[72,1024]{1,0:T(8,128)(2,1)}), bf16[2304,1024]{1,0:T(8,128)(2,1)}) %all-gather.10.cloned.1.call-update) | async-done | bytes 4718608 | tf_op jit(solution)/shard_map/all_gather | solution.py:89
  165.0 27.3 %fusion.38 = bf16[72,9216]{1,0:T(8,128)(2,1)} fusion(s32[72,9216]{1,0:T(8,128)S(1)} %copy-done.13, s32[]{:T(128)S(6)} %select_n.149, s32[]{:T(128)} %bitcast.33, s32[]{:T(128)S(6)} %sign.73), kind=kLoop, calls=%fused_computation.56 | loop fusion | flops 8626176 | bytes 3981324 | tf_op jit(solution)/shard_map/convert_element_type | solution.py:83
  192.3 27.7 %fusion.48 = bf16[72,9216]{1,0:T(8,128)(2,1)} fusion(s32[72,9216]{1,0:T(8,128)S(1)} %copy-done.14, s32[]{:T(128)S(6)} %select_n.159, s32[]{:T(128)} %bitcast.35, s32[]{:T(128)S(6)} %sign.77), kind=kLoop, calls=%fused_computation.66 | loop fusion | flops 8626176 | bytes 3981324 | tf_op jit(solution)/shard_map/convert_element_type | solution.py:85
  229.1 12.8 copy.124
  249.0 32.0 %all-gather.16.cloned.1.call-done = bf16[1,2048,4,256]{3,1,2,0:T(8,128)(2,1)} async-done(((bf16[1,128,4,256]{3,1,2,0:T(8,128)(2,1)}), bf16[1,2048,4,256]{3,1,2,0:T(8,128)(2,1)}) %all-gather.16.cloned.1.call-update) | async-done | bytes 4194320 | tf_op jit(solution)/shard_map/all_gather | solution.py:139
  288.1 47.0 %all-gather.12.cloned.1.call-done = bf16[1,2048,4,256]{1,3,2,0:T(8,128)(2,1)} async-done(((bf16[1,128,4,256]{1,3,2,0:T(8,128)(2,1)}), bf16[1,2048,4,256]{1,3,2,0:T(8,128)(2,1)}) %all-gather.12.cloned.1.call-update) | async-done | bytes 4194320 | tf_op jit(solution)/shard_map/all_gather | solution.py:140
  343.5 75.5 %all-gather.20.cloned.1.call-done = bf16[2304,2048]{1,0:T(8,128)(2,1)} async-done(((bf16[72,2048]{1,0:T(8,128)(2,1)}), bf16[2304,2048]{1,0:T(8,128)(2,1)}) %all-gather.20.cloned.1.call-update) | async-done | bytes 9437200 | tf_op jit(solution)/shard_map/all_gather | solution.py:90
  427.5 29.0 %fusion.43 = bf16[72,9216]{1,0:T(8,128)(2,1)} fusion(s32[72,9216]{1,0:T(8,128)} %param.24, s32[]{:T(128)S(6)} %select_n.154, s32[]{:T(128)} %bitcast.34, s32[]{:T(128)S(6)} %sign.75), kind=kLoop, calls=%fused_computation.61 | loop fusion | flops 8626176 | bytes 3981324 | tf_op jit(solution)/shard_map/convert_element_type | solution.py:84
  487.1 206.9 %all_to_all.24 = bf16[3,72,32,576]{3,1,0,2:T(8,128)(2,1)S(1)} all-to-all(bf16[3,72,32,576]{3,1,0,2:T(8,128)(2,1)} %copy.126), channel_id=1, replica_groups=mesh['rows'=2,'seq'=16] {'rows','seq'}, dimensions={2} | all-to-all | bytes 15925248 | tf_op jit(solution)/shard_map/all_to_all | solution.py:99
  707.1 12.6 multiply_convert_fusion.1
  732.7 193.8 %reduce-scatter.6.cloned.1.call-done = f32[1,128,2304]{2,1,0:T(8,128)} async-done(((f32[1,2048,2304]{2,1,0:T(8,128)}), f32[1,128,2304]{2,1,0:T(8,128)}) %reduce-scatter.6.cloned.1.call-update) | async-done | bytes 1179664 | tf_op jit(solution)/shard_map/reduce_scatter | solution.py:160
  932.1 80.6 %all-gather.22.cloned.1.call-done = bf16[1,2048,2304]{2,1,0:T(8,128)(2,1)} async-done(((bf16[1,128,2304]{2,1,0:T(8,128)(2,1)}), bf16[1,2048,2304]{2,1,0:T(8,128)(2,1)}) %all-gather.22.cloned.1.call-update) | async-done | bytes 9437200 | tf_op jit(solution)/shard_map/all_gather | solution.py:168
  1012.7 16.0 multiply_convert_fusion
  1039.6 19.0 add_bitcast_fusion
  1058.7 193.2 %reduce-scatter.8.cloned.1.call-done = f32[1,128,2304]{2,1,0:T(8,128)} async-done(((f32[1,2048,2304]{2,1,0:T(8,128)}), f32[1,128,2304]{2,1,0:T(8,128)}) %reduce-scatter.8.cloned.1.call-update) | async-done | bytes 1179664 | tf_op jit(solution)/shard_map/reduce_scatter | solution.py:178
  1318.8 61.7 %reduce-scatter.10.cloned.1.call-done = f32[1,128,4,256]{3,1,2,0:T(8,128)} async-done(((f32[1,2048,4,256]{3,1,2,0:T(8,128)}), f32[1,128,4,256]{3,1,2,0:T(8,128)}) %reduce-scatter.10.cloned.1.call-update) | async-done | bytes 524304 | tf_op jit(solution)/shard_map/reduce_scatter | solution.py:244
  1381.9 107.3 %reduce-scatter.12.cloned.1.call-done = f32[1,128,4,256]{1,3,2,0:T(8,128)} async-done(((f32[1,2048,4,256]{1,3,2,0:T(8,128)}), f32[1,128,4,256]{1,3,2,0:T(8,128)}) %reduce-scatter.12.cloned.1.call-update) | async-done | bytes 524304 | tf_op jit(solution)/shard_map/reduce_scatter | solution.py:245
  1506.2 132.7 %concatenate.69 = f32[2304,6272]{0,1:T(8,128)} concatenate(f32[2304,2048]{0,1:T(8,128)} %fusion.111, f32[2304,1024]{0,1:T(8,128)} %fusion.113, f32[2304,1024]{0,1:T(8,128)} %fusion.109, f32[2304,2048]{0,1:T(8,128)} %fusion.158, f32[2304,1]{0,1:T(1,128)S(1)} %stack.40, f32[2304,1]{0,1:T(1,128)S(1)} %copy-done.29, f32[2304,1]{0,1:T(1,128)S(1)} %copy-done.28, ...), dimensions={1} | concatenate | bytes 115605504 | tf_op jit(solution)/shard_map/concatenate | solution.py:269
  1670.2 19.6 copy.140
  1694.8 380.7 %all-to-all-done.1 = bf16[3,2304,1,576]{3,0,2,1:T(4,128)(2,1)} async-done(((bf16[3,2304,1,576]{3,0,2,1:T(4,128)(2,1)}), bf16[3,2304,1,576]{3,0,2,1:T(4,128)(2,1)}, u32[]{:S(2)}, u32[]{:S(2)}) %all-to-all-start.1) | async-done | bytes 7962656 | tf_op jit(solution)/shard_map/all_to_all | solution.py:188
  2085.4 11.1 convert.36
  2096.5 12.1 reduce_sum.170
  2136.0 571.8 %all-reduce.3.cloned.1.call-done = f32[2304,6272]{0,1:T(8,128)} async-done(((f32[2304,6272]{0,1:T(8,128)}), f32[2304,6272]{0,1:T(8,128)}) %all-reduce.3.cloned.1.call-update) | async-done | bytes 57802768
  (239 shorter events, 329.3 us)
Async XLA Ops:
  7.2 71.9 %all-gather.14.cloned.1.call-start = ((), (), s32[]{:S(2)}) async-start(), calls=%async_computation.8 | async-start | bytes 4866048 | tf_op jit(solution)/shard_map/all_gather | solution.py:88
  14.6 130.4 %all-gather.10.cloned.1.call-start = ((), (), s32[]{:S(2)}) async-start(), calls=%async_computation.6 | async-start | bytes 4866048 | tf_op jit(solution)/shard_map/all_gather | solution.py:89
  20.6 208.5 %all-gather.18.cloned.1.call-start = ((), (), s32[]{:S(2)}) async-start(), calls=%async_computation.10 | async-start | bytes 9732096 | tf_op jit(solution)/shard_map/all_gather | solution.py:87
  30.1 251.0 %all-gather.16.cloned.1.call-start = ((), (), s32[]{:S(2)}) async-start(), calls=%async_computation.9 | async-start | bytes 4456448 | tf_op jit(solution)/shard_map/all_gather | solution.py:139
  31.4 54.5 %copy-start.38 = (f32[128]{0:T(128)}, f32[128]{0:T(128)S(1)}, u32[]{:S(2)}) copy-start(f32[128]{0:T(128)S(1)} %fusion.77) | copy-start | bytes 1540
  31.4 210.5 %copy-start.30 = (f32[128]{0:T(128)}, f32[128]{0:T(128)S(1)}, u32[]{:S(2)}) copy-start(f32[128]{0:T(128)S(1)} %fusion.132) | copy-start | bytes 1540
  31.4 210.5 %copy-start.22 = (f32[2304]{0:T(1024)}, f32[2304]{0:T(1024)S(1)}, u32[]{:S(2)}) copy-start(f32[2304]{0:T(1024)S(1)} %broadcast_add_fusion.3) | copy-start | bytes 27652
  32.4 216.5 %copy-start.17 = (f32[128,128]{1,0:T(8,128)}, f32[128,128]{1,0:T(8,128)S(1)}, u32[]{:S(2)}) copy-start(f32[128,128]{1,0:T(8,128)S(1)} %get-tuple-element.116) | copy-start | bytes 196612
  90.7 73.1 %copy-start.36 = (s32[1,2048]{1,0:T(1,128)S(1)}, s32[1,2048]{1,0:T(1,128)}, u32[]{:S(2)}) copy-start(s32[1,2048]{1,0:T(1,128)} %param.17) | copy-start | bytes 24580
  90.7 73.1 %copy-start.33 = (f32[2304]{0:T(1024)S(1)}, f32[2304]{0:T(1024)}, u32[]{:S(2)}) copy-start(f32[2304]{0:T(1024)} %param.27) | copy-start | bytes 27652
  90.7 73.2 %copy-start.34 = (f32[2304]{0:T(1024)S(1)}, f32[2304]{0:T(1024)}, u32[]{:S(2)}) copy-start(f32[2304]{0:T(1024)} %param.28) | copy-start | bytes 27652
  90.7 74.2 %copy-start.13 = (s32[72,9216]{1,0:T(8,128)S(1)}, s32[72,9216]{1,0:T(8,128)}, u32[]{:S(2)}) copy-start(s32[72,9216]{1,0:T(8,128)} %param.23) | copy-start | bytes 7962628
  90.8 244.3 %all-gather.12.cloned.1.call-start = ((), (), s32[]{:S(2)}) async-start(), calls=%async_computation.7 | async-start | bytes 4456448 | tf_op jit(solution)/shard_map/all_gather | solution.py:140
  150.7 268.4 %all-gather.20.cloned.1.call-start = ((), (), s32[]{:S(2)}) async-start(), calls=%async_computation.11 | async-start | bytes 9732096 | tf_op jit(solution)/shard_map/all_gather | solution.py:90
  159.9 537.8 %all-gather.24.cloned.1.call-start = ((), (), s32[]{:S(2)}) async-start(), calls=%async_computation.17 | async-start | bytes 10027008 | tf_op jit(solution)/shard_map/all_gather | solution.py:155
  343.5 82.5 %copy-start.15 = (bf16[1,128,4,2,256]{1,4,3,2,0:T(8,128)(2,1)}, bf16[1,128,4,2,256]{1,4,3,2,0:T(8,128)(2,1)S(1)}, u32[]{:S(2)}) copy-start(bf16[1,128,4,2,256]{1,4,3,2,0:T(8,128)(2,1)S(1)} %get-tuple-element.126) | copy-start | bytes 1572868
  427.4 499.1 %reduce-scatter.6.cloned.1.call-start = ((), (), s32[]{:S(2)}) async-start(), calls=%async_computation.12 | async-start | bytes 20054016 | tf_op jit(solution)/shard_map/reduce_scatter | solution.py:160
  732.0 196.1 %copy-start.6 = (bf16[1,128,2304]{2,1,0:T(8,128)(2,1)S(1)}, bf16[1,128,2304]{2,1,0:T(8,128)(2,1)}, u32[]{:S(2)}) copy-start(bf16[1,128,2304]{2,1,0:T(8,128)(2,1)} %param.16) | copy-start | bytes 1769476
  732.0 280.7 %all-gather.22.cloned.1.call-start = ((), (), s32[]{:S(2)}) async-start(), calls=%async_computation.13 | async-start | bytes 10027008 | tf_op jit(solution)/shard_map/all_gather | solution.py:168
  932.1 319.8 %reduce-scatter.8.cloned.1.call-start = ((), (), s32[]{:S(2)}) async-start(), calls=%async_computation.14 | async-start | bytes 20054016 | tf_op jit(solution)/shard_map/reduce_scatter | solution.py:178
  1058.6 321.9 %reduce-scatter.10.cloned.1.call-start = ((), (), s32[]{:S(2)}) async-start(), calls=%async_computation.15 | async-start | bytes 8912896 | tf_op jit(solution)/shard_map/reduce_scatter | solution.py:244
  1275.9 213.2 %reduce-scatter.12.cloned.1.call-start = ((), (), s32[]{:S(2)}) async-start(), calls=%async_computation.16 | async-start | bytes 8912896 | tf_op jit(solution)/shard_map/reduce_scatter | solution.py:245
  1285.8 1422.0 %all-reduce.3.cloned.1.call-start = ((), (), s32[]{:S(2)}) async-start(), calls=%async_computation.18 | async-start | bytes 115605504
  1689.9 385.7 %all-to-all-start.1 = ((bf16[3,2304,1,576]{3,0,2,1:T(4,128)(2,1)}), bf16[3,2304,1,576]{3,0,2,1:T(4,128)(2,1)}, u32[]{:S(2)}, u32[]{:S(2)}) async-start(bf16[3,2304,1,576]{3,0,2,1:T(4,128)(2,1)} %copy.140), calls=%async_computation.5 | async-start | bytes 23592960 | tf_op jit(solution)/shard_map/all_to_all | solution.py:188
  (44 other events, 431.1 us)
Sparse Core Ops, SparseCore 0:
  14.8 64.3 all-gather.13
  82.6 62.3 all-gather.9
  148.5 80.6 all-gather.17
  231.7 49.3 all-gather.15
  283.6 51.3 all-gather.11
  338.4 80.6 all-gather.19
  427.6 91.6 all-gather.23
  732.2 194.3 reduce-scatter.5
  932.2 80.4 all-gather.21
  1058.7 193.1 reduce-scatter.7
  1276.0 104.4 reduce-scatter.9
  1384.5 104.5 reduce-scatter.11
  1639.1 1068.6 all-reduce.2
where the time goes:
time: 2740 us; the launch traced here: 2720 us
  waiting for transfers between devices  1850 us (68%)
  local copies, waits for them, and re-layouts  256 us (9%)
  matrix products  216 us (8%)
  blocking collectives  207 us (8%)
  other arithmetic  163 us (6%)
    unnamed x14, waiting for transfers between devices  572 us
    all_to_all x1, waiting for transfers between devices, per_device(): lax.all_to_all(column_terms.reshape(3, D, 1, col_width).astype(jnp.bfloat...  381 us
    all_to_all x1, blocking collectives, per_device(): lax.all_to_all(spread, ('rows', 'seq'), split_axis=2, concat_axis=1, tile...  207 us
    reduce_scatter x1, waiting for transfers between devices, per_device(): lax.psum_scatter(ffn_terms, 'seq', scatter_dimension=1, tiled=True)  194 us
    reduce_scatter x1, waiting for transfers between devices, per_device(): lax.psum_scatter(mid_terms, 'seq', scatter_dimension=1, tiled=True)  193 us
    concatenate x1, local copies, waits for them, and re-layouts, per_device(): jnp.concatenate([outer_sum(normed_low, grad_query_pre), outer_sum(normed_...  133 us
    reduce_scatter x1, waiting for transfers between devices, per_device(): lax.psum_scatter(value_sums, 'seq', scatter_dimension=1, tiled=True)  107 us
    all_gather x1, waiting for transfers between devices, per_device(): lax.all_gather(grad_ffn_low.reshape(rows_here, seq_block, D), 'seq', axis...  80.6 us
  transfers between devices with their start and end apart: 14, of which 13 were waited for; matrix products, arithmetic and copies ran while one was open for 13% of the time, Pallas kernels for 0%

commit v1 on v0

--- a/solution.py
+++ b/solution.py
@@ -18,8 +18,9 @@
 
 
 def dequant(levels_int, level_idx, fan_in, boost):
-    stride = jnp.where(level_idx == 0, 1, jnp.where(level_idx == 1, 16, 64)).astype(jnp.int32)
-    sliced = levels_int // stride * stride + stride // 2
+    bits = jnp.where(level_idx == 0, 0, jnp.where(level_idx == 1, 4, 6)).astype(jnp.int32)
+    middle = jnp.where(level_idx == 0, 0, jnp.where(level_idx == 1, 8, 32)).astype(jnp.int32)
+    sliced = ((levels_int >> bits) << bits) + middle
     return sliced.astype(jnp.float32) * (boost / (74.0 * math.sqrt(fan_in)))
 
 
@@ -48,7 +49,7 @@
     return jax.nn.gelu(gate_vals, approximate=True) * up_vals
 
 
-def per_device(
+def per_device_plain(
     tokens,
     cotangent,
     doc_ids,
@@ -301,6 +302,460 @@
     )
 
 
+AXES = ("rows", "seq")
+LINE = 4
+
+
+def moves(places, rule):
+    found = []
+    for index in range(places):
+        y, rest = divmod(index, LINE * 4)
+        z, x, c = rest // 4, (rest // 2) % 2, rest % 2
+        target = rule(y, z, x, c)
+        if target is not None:
+            y_to, z_to, x_to, c_to = target
+            found.append((index, y_to * LINE * 4 + (z_to * 2 + x_to) * 2 + c_to))
+    return found
+
+
+def send(value, rule):
+    return lax.ppermute(value, AXES, moves(2 * LINE * 4, rule))
+
+
+def to_row(value):
+    return send(value, lambda y, z, x, c: (1 - y, z, x, c))
+
+
+def to_x(value):
+    return send(value, lambda y, z, x, c: (y, z, 1 - x, c))
+
+
+def to_core(value):
+    return send(value, lambda y, z, x, c: (y, z, x, 1 - c))
+
+
+def to_pair(value):
+    return send(value, lambda y, z, x, c: (y, z ^ 1, x, c))
+
+
+def across_middle(value):
+    return send(value, lambda y, z, x, c: (y, 3 - z, x, c) if z in (1, 2) else None)
+
+
+def to_ends(value):
+    return send(value, lambda y, z, x, c: (y, z ^ 1, x, c) if z in (1, 2) else None)
+
+
+def from_ends(value):
+    return send(value, lambda y, z, x, c: (y, z ^ 1, x, c) if z in (0, 3) else None)
+
+
+def up_line(value):
+    return send(value, lambda y, z, x, c: (y, z + 1, x, c) if z < LINE - 1 else None)
+
+
+def down_line(value):
+    return send(value, lambda y, z, x, c: (y, z - 1, x, c) if z > 0 else None)
+
+
+def to_chip(value, dz, dx):
+    return send(value, lambda y, z, x, c: (y, z ^ dz, x ^ dx, c))
+
+
+def low(value):
+    return value.astype(jnp.bfloat16)
+
+
+def wide(value):
+    return value.astype(jnp.float32)
+
+
+def pick(array, index, axis=0):
+    return lax.dynamic_index_in_dim(array, index, axis, keepdims=False)
+
+
+def place(array, piece, starts):
+    return lax.dynamic_update_slice(array, piece, starts)
+
+
+class Spot:
+    def __init__(self):
+        self.y = lax.axis_index("rows")
+        index = lax.axis_index("seq")
+        self.z = index // 4
+        self.x = (index // 2) % 2
+        self.c = index % 2
+        self.middle = (self.z == 1) | (self.z == 2)
+        upper = self.z >= 2
+        self.slots = [
+            self.z,
+            self.z ^ 1,
+            jnp.where(upper, 1, 2).astype(jnp.int32),
+            jnp.where(upper, 0, 3).astype(jnp.int32),
+        ]
+
+
+def gather_line(spot, own):
+    pair = to_pair(own)
+    near = across_middle(own)
+    far = across_middle(pair)
+    near_end = to_ends(near)
+    far_end = to_ends(far)
+    return [
+        own,
+        pair,
+        jnp.where(spot.middle, near, near_end),
+        jnp.where(spot.middle, far, far_end),
+    ]
+
+
+def reduce_line(parts):
+    far = parts[3] + wide(from_ends(low(parts[3])))
+    near = parts[2] + wide(from_ends(low(parts[2])))
+    pair = parts[1] + wide(across_middle(low(far)))
+    own = parts[0] + wide(across_middle(low(near)))
+    return own + wide(to_pair(low(pair)))
+
+
+def gather_group(own):
+    over_x = to_x(own)
+    return jnp.concatenate([own, to_core(own), over_x, to_core(over_x)], axis=0)
+
+
+def reduce_group(parts):
+    both = wide(parts[:, 0]) + wide(to_core(parts[:, 1]))
+    return both[0] + wide(to_x(low(both[1])))
+
+
+def gather_plane(spot, own):
+    return [
+        jnp.concatenate([block, to_x(block)], axis=0) for block in gather_line(spot, own)
+    ]
+
+
+def reduce_plane(chunks):
+    parts = [None] * LINE
+    for slot in (3, 2, 1, 0):
+        parts[slot] = wide(chunks[slot][0]) + wide(to_x(chunks[slot][1]))
+    return reduce_line(parts)
+
+
+def member(spot, dx, dc):
+    return (spot.x ^ dx) * 2 + (spot.c ^ dc)
+
+
+def exchange_group(spot, pieces):
+    own = pick(pieces, member(spot, 0, 0))
+    from_core = to_core(pick(pieces, member(spot, 0, 1)))
+    from_x = to_x(pick(pieces, member(spot, 1, 0)))
+    from_both = to_core(to_x(pick(pieces, member(spot, 1, 1))))
+    out = jnp.zeros_like(pieces)
+    for dx, dc, piece in ((0, 0, own), (0, 1, from_core), (1, 0, from_x), (1, 1, from_both)):
+        out = place(out, piece[None], (member(spot, dx, dc), 0, 0))
+    return out
+
+
+def gather_heads(spot, pieces):
+    group = exchange_group(spot, pieces)
+    rows, cols = pieces.shape[1:]
+    out = jnp.zeros((2, LINE, 4, rows, cols), pieces.dtype)
+    for slot, block in enumerate(gather_line(spot, group)):
+        z = spot.slots[slot]
+        out = place(out, block[None, None], (spot.y, z, 0, 0, 0))
+        out = place(out, to_row(block)[None, None], (1 - spot.y, z, 0, 0, 0))
+    return out.reshape(2 * LINE * 4 * rows, cols)
+
+
+def scatter_heads(spot, sums):
+    cols = sums.shape[1]
+    rows = sums.shape[0] // (2 * LINE * 4)
+    blocks = sums.reshape(2, LINE, 4, rows, cols)
+    mine = pick(blocks, spot.y)
+    other = pick(blocks, 1 - spot.y)
+    parts = [None] * LINE
+    for slot in (3, 2, 1, 0):
+        z = spot.slots[slot]
+        parts[slot] = wide(pick(mine, z)) + wide(to_row(pick(other, z)))
+    return exchange_group(spot, low(reduce_line(parts)))
+
+
+def gather_hidden(spot, pieces):
+    rows, width = pieces.shape[1:]
+    chip = spot.z * 2 + spot.x
+    plane = jnp.zeros_like(pieces)
+    for dz, dx in ((3, 0), (3, 1), (2, 0), (2, 1), (1, 0), (1, 1), (0, 1), (0, 0)):
+        there = (spot.z ^ dz) * 2 + (spot.x ^ dx)
+        piece = pick(pieces, there)
+        if dz or dx:
+            piece = to_chip(piece, dz, dx)
+        plane = place(plane, piece[None], (there, 0, 0))
+    across = to_row(plane)
+    out = jnp.zeros((2, LINE * 2, 2, rows, width), pieces.dtype)
+    for half, y in ((plane, spot.y), (across, 1 - spot.y)):
+        out = place(out, half[None, :, None], (y, 0, spot.c, 0, 0))
+        out = place(out, to_core(half)[None, :, None], (y, 0, 1 - spot.c, 0, 0))
+    return out.reshape(2 * LINE * 4 * rows, width)
+
+
+def scatter_hidden(spot, sums):
+    width = sums.shape[1]
+    rows = sums.shape[0] // (2 * LINE * 4)
+    blocks = sums.reshape(2, LINE * 2, 2, rows, width)
+    cores = low(
+        wide(pick(blocks, spot.c, 2)) + wide(to_core(pick(blocks, 1 - spot.c, 2)))
+    )
+    plane = low(wide(pick(cores, spot.y)) + wide(to_row(pick(cores, 1 - spot.y))))
+    out = jnp.zeros_like(plane)
+    for dz, dx in ((3, 0), (3, 1), (2, 0), (2, 1), (1, 0), (1, 1), (0, 1), (0, 0)):
+        there = (spot.z ^ dz) * 2 + (spot.x ^ dx)
+        piece = pick(plane, there)
+        if dz or dx:
+            piece = to_chip(piece, dz, dx)
+        out = place(out, piece[None], (there, 0, 0))
+    return wide(out).transpose(1, 0, 2).reshape(rows, LINE * 2 * width)
+
+
+def split_columns(matrix, count):
+    rows, cols = matrix.shape
+    return matrix.reshape(rows, count, cols // count).transpose(1, 0, 2)
+
+
+def join_columns(blocks):
+    count, rows, cols = blocks.shape
+    return wide(blocks).transpose(1, 0, 2).reshape(rows, count * cols)
+
+
+def turn(values, cosine, sine):
+    half_dim = HEAD_DIM // 2
+    front_half = values[..., :half_dim]
+    back_half = values[..., half_dim:]
+    return jnp.concatenate(
+        [front_half * cosine - back_half * sine, back_half * cosine + front_half * sine], axis=-1
+    )
+
+
+def dot(left_side, right_side):
+    return jnp.dot(left_side, right_side, preferred_element_type=jnp.float32)
+
+
+def dot_rows(left_side, right_side):
+    return jnp.einsum("tf,df->td", left_side, right_side, preferred_element_type=jnp.float32)
+
+
+def outer_sum(left_side, right_side):
+    return jnp.einsum("td,tf->df", left_side, right_side, preferred_element_type=jnp.float32)
+
+
+def per_device_line(
+    tokens,
+    cotangent,
+    doc_ids,
+    bit_levels,
+    w_query,
+    w_key,
+    w_value,
+    w_proj,
+    w_gate,
+    w_up,
+    w_down,
+    gain_first,
+    gain_second,
+    gain_third,
+    gain_fourth,
+):
+    spot = Spot()
+    count = tokens.shape[1]
+    local_rows = w_query.shape[0]
+    group_size = HEADS // KV_HEADS
+    query_width = HEADS * HEAD_DIM
+    score_scale = HEAD_DIM ** (-0.5)
+    span = 4 * count
+
+    heads_in = low(
+        jnp.concatenate(
+            [
+                split_columns(dequant(w_query, bit_levels[0], D, qk_boost), KV_HEADS),
+                split_columns(dequant(w_key, bit_levels[1], D, qk_boost), KV_HEADS),
+                split_columns(dequant(w_value, bit_levels[2], D, 1.0), KV_HEADS),
+            ],
+            axis=2,
+        )
+    )
+    proj_in = low(split_columns(dequant(w_proj, bit_levels[3], query_width, 1.0), KV_HEADS))
+    flat_tokens = wide(tokens).reshape(count, D)
+    normed_low = low(rmsnorm(flat_tokens, gain_first))
+    normed_all = gather_group(normed_low)
+    heads_w = gather_heads(spot, heads_in)
+    proj_w = gather_heads(spot, proj_in)
+    chips = LINE * 2
+    gate_w = gather_hidden(
+        spot, low(split_columns(dequant(w_gate, bit_levels[4], D, 1.0), chips))
+    )
+    up_w = gather_hidden(spot, low(split_columns(dequant(w_up, bit_levels[5], D, 1.0), chips)))
+    down_w = gather_hidden(
+        spot, low(split_columns(dequant(w_down, bit_levels[6], FF, 1.0), chips))
+    )
+
+    inner = jnp.arange(count, dtype=jnp.int32)
+    offsets = jnp.concatenate(
+        [member(spot, dx, dc) * count + inner for dx in range(2) for dc in range(2)]
+    )
+    positions = spot.z * span + offsets
+    half_dim = HEAD_DIM // 2
+    frequency = 10000.0 ** (-(2.0 / HEAD_DIM) * jnp.arange(half_dim, dtype=jnp.float32))
+    angles = positions.astype(jnp.float32)[:, None] * frequency[None, :]
+    cosine = jnp.cos(angles)
+    sine = jnp.sin(angles)
+    docs = doc_ids.reshape(LINE, 2, 2, count)
+    docs = jnp.where(spot.x == 1, docs[:, ::-1], docs)
+    docs = jnp.where(spot.c == 1, docs[:, :, ::-1], docs).reshape(LINE, span)
+    query_docs = pick(docs, spot.z)
+
+    pre = dot(normed_all, heads_w)
+    wide_q = group_size * HEAD_DIM
+    query_rot = low(
+        turn(
+            pre[:, :wide_q].reshape(span, group_size, HEAD_DIM),
+            cosine[:, None],
+            sine[:, None],
+        )
+    )
+    key_rot = low(turn(pre[:, wide_q : wide_q + HEAD_DIM], cosine, sine))
+    value_low = low(pre[:, wide_q + HEAD_DIM :])
+    key_value = [jnp.concatenate([key_rot, value_low], axis=1)]
+    for _ in range(1, LINE):
+        key_value.append(up_line(key_value[-1]))
+
+    totals = 0.0
+    summed = 0.0
+    saved = []
+    for back, block in enumerate(key_value):
+        key_piece, value_piece = block[:, :HEAD_DIM], block[:, HEAD_DIM:]
+        key_docs = pick(docs, jnp.maximum(spot.z - back, 0))
+        key_pos = positions - back * span
+        allowed = (
+            (key_pos[None, :] <= positions[:, None])
+            & (key_pos[None, :] >= 0)
+            & (key_docs[None, :] == query_docs[:, None])
+        )
+        raw_scores = (
+            jnp.einsum("qrd,kd->rqk", query_rot, key_piece, preferred_element_type=jnp.float32)
+            * score_scale
+        )
+        bent = jnp.tanh(raw_scores / softcap)
+        weights = jnp.where(allowed[None], jnp.exp(softcap * bent), 0.0)
+        totals = totals + jnp.sum(weights, axis=-1)
+        summed = summed + jnp.einsum(
+            "rqk,kd->qrd", low(weights), value_piece, preferred_element_type=jnp.float32
+        )
+        saved.append((key_piece, value_piece, weights, bent))
+    denominator = jnp.transpose(totals)[..., None]
+    mixed_out = summed / denominator
+    mixed_low = low(mixed_out).reshape(span, wide_q)
+    attn_out = reduce_group(low(dot_rows(mixed_low, proj_w)).reshape(2, 2, count, D))
+    hidden_one = flat_tokens + rmsnorm(attn_out, gain_second)
+    mid_low = low(rmsnorm(hidden_one, gain_third))
+
+    mid_chunks = gather_plane(spot, mid_low)
+    gates, acts, ffn_chunks = [], [], []
+    for chunk in mid_chunks:
+        gate_pre = dot(chunk, gate_w)
+        up_pre = dot(chunk, up_w)
+        activated = low(gelu_product(gate_pre, up_pre))
+        gates.append((gate_pre, up_pre))
+        acts.append(activated)
+        ffn_chunks.append(low(dot_rows(activated, down_w)).reshape(2, count, D))
+    ffn_out = reduce_plane(ffn_chunks)
+    result = hidden_one + rmsnorm(ffn_out, gain_fourth)
+    layer_out = low(result).reshape(1, count, D)
+
+    upstream = wide(cotangent).reshape(count, D)
+    grad_ffn, fourth_part = jax.vjp(rmsnorm, ffn_out, gain_fourth)[1](upstream)
+    grad_chunks = gather_plane(spot, low(grad_ffn))
+    gate_grads, up_grads, back_chunks = [], [], []
+    for chunk, (gate_pre, up_pre) in zip(grad_chunks, gates):
+        grad_act = dot(chunk, down_w)
+        grad_gate_pre, grad_up_pre = jax.vjp(gelu_product, gate_pre, up_pre)[1](grad_act)
+        gate_grads.append(low(grad_gate_pre))
+        up_grads.append(low(grad_up_pre))
+        back_chunks.append(
+            low(dot_rows(gate_grads[-1], gate_w) + dot_rows(up_grads[-1], up_w)).reshape(
+                2, count, D
+            )
+        )
+    grad_mid = reduce_plane(back_chunks)
+    mid_all = jnp.concatenate(mid_chunks, axis=0)
+    grad_gate = scatter_hidden(spot, low(outer_sum(mid_all, jnp.concatenate(gate_grads, axis=0))))
+    grad_up = scatter_hidden(spot, low(outer_sum(mid_all, jnp.concatenate(up_grads, axis=0))))
+    grad_down = scatter_hidden(
+        spot,
+        low(outer_sum(jnp.concatenate(grad_chunks, axis=0), jnp.concatenate(acts, axis=0))),
+    )
+
+    hidden_part, third_part = jax.vjp(rmsnorm, hidden_one, gain_third)[1](grad_mid)
+    grad_hidden = upstream + hidden_part
+    grad_attn, second_part = jax.vjp(rmsnorm, attn_out, gain_second)[1](grad_hidden)
+    grad_attn_all = gather_group(low(grad_attn))
+    proj_sums = scatter_heads(spot, low(outer_sum(grad_attn_all, mixed_low)))
+
+    grad_mixed = dot(grad_attn_all, proj_w).reshape(span, group_size, HEAD_DIM)
+    grad_summed = low(grad_mixed / denominator)
+    delta = jnp.transpose(jnp.sum(grad_mixed * mixed_out, axis=-1)) / totals
+    grad_query_rot = 0.0
+    passed = None
+    for back in range(LINE - 1, -1, -1):
+        key_piece, value_piece, weights, bent = saved[back]
+        grad_weights = (
+            jnp.einsum(
+                "qrd,kd->rqk", grad_summed, value_piece, preferred_element_type=jnp.float32
+            )
+            - delta[..., None]
+        )
+        grad_raw = low(weights * grad_weights * (1.0 - bent * bent))
+        grad_query_rot = grad_query_rot + jnp.einsum(
+            "rqk,kd->qrd", grad_raw, key_piece, preferred_element_type=jnp.float32
+        )
+        key_term = (
+            jnp.einsum("rqk,qrd->kd", grad_raw, query_rot, preferred_element_type=jnp.float32)
+            * score_scale
+        )
+        value_term = jnp.einsum(
+            "rqk,qrd->kd", low(weights), grad_summed, preferred_element_type=jnp.float32
+        )
+        sums = jnp.concatenate([key_term, value_term], axis=1)
+        if passed is not None:
+            sums = sums + wide(down_line(passed))
+        passed = low(sums)
+    grad_query_pre = low(
+        turn(grad_query_rot * score_scale, cosine[:, None], -sine[:, None])
+    ).reshape(span, wide_q)
+    grad_key_pre = low(turn(sums[:, :HEAD_DIM], cosine, -sine))
+    grad_pre = jnp.concatenate([grad_query_pre, grad_key_pre, low(sums[:, HEAD_DIM:])], axis=1)
+    head_sums = scatter_heads(spot, low(outer_sum(normed_all, grad_pre)))
+    grad_in = reduce_group(low(dot_rows(grad_pre, heads_w)).reshape(2, 2, count, D))
+    tokens_part, first_part = jax.vjp(rmsnorm, flat_tokens, gain_first)[1](grad_in)
+    grad_tokens = (grad_hidden + tokens_part).reshape(1, count, D)
+
+    gain_terms = lax.psum(jnp.stack([first_part, second_part, third_part, fourth_part]), AXES)
+    mine = (spot.y * (LINE * 4) + lax.axis_index("seq")) * local_rows
+    gains = lax.dynamic_slice_in_dim(gain_terms, mine, local_rows, 1)
+    return (
+        layer_out,
+        grad_tokens,
+        join_columns(head_sums[:, :, :wide_q]),
+        join_columns(head_sums[:, :, wide_q : wide_q + HEAD_DIM]),
+        join_columns(head_sums[:, :, wide_q + HEAD_DIM :]),
+        join_columns(proj_sums),
+        grad_gate,
+        grad_up,
+        grad_down,
+        gains[0],
+        gains[1],
+        gains[2],
+        gains[3],
+    )
+
+
 def solution(mesh):
     placed = (
         P("rows", "seq", None),
@@ -319,8 +774,10 @@
         P(),
         P(),
     )
+    sizes = dict(mesh.shape)
+    fits = sizes["rows"] == 2 and sizes["seq"] == LINE * 4
     return jax.shard_map(
-        per_device,
+        per_device_line if fits else per_device_plain,
         mesh=mesh,
         in_specs=placed,
         out_specs=(

time: 2740 us -> 1120 us (0.41)
  waiting for transfers between devices: 1850 us -> 508 us
  starting transfers between devices: 6.1 us -> 227 us
  blocking collectives: 207 us -> 43.2 us
  local copies, waits for them, and re-layouts: 256 us -> 132 us
  other arithmetic: 163 us -> 60.5 us
  matrix products: 216 us -> 127 us
    unnamed x14 -> x0, waiting for transfers between devices: 572 us -> none
    reduce_scatter x4 -> x0, waiting for transfers between devices: 556 us -> none  [the longest x1 194 us: per_device(): lax.psum_scatter(ffn_terms, 'seq', scatter_dimension=1, tiled=True)]
    ppermute x0 -> x161, waiting for transfers between devices: none -> 508 us  [send(): return lax.ppermute(value, AXES, moves(2 * LINE * 4, rule))]
    all_to_all x1 -> x0, waiting for transfers between devices: 381 us -> none  [per_device(): lax.all_to_all(column_terms.reshape(3, D, 1, col_width).astype(jnp.bfloat...]
    all_gather x8 -> x0, waiting for transfers between devices: 345 us -> none  [the longest x1 80.6 us: per_device(): lax.all_gather(grad_ffn_low.reshape(rows_here, seq_block, D), 'seq', axis...]
    ppermute x0 -> x161, starting transfers between devices: none -> 227 us  [send(): return lax.ppermute(value, AXES, moves(2 * LINE * 4, rule))]
    all_to_all x1 -> x0, blocking collectives: 207 us -> none  [per_device(): lax.all_to_all(spread, ('rows', 'seq'), split_axis=2, concat_axis=1, tile...]
    concatenate x2 -> x4, local copies, waits for them, and re-layouts: 143 us -> 4.03 us  [the longest x1 2.08 us: per_device_line(): mid_all = jnp.concatenate(mid_chunks, axis=0)]
  transfers between devices with their start and end apart: 14 -> 161, of which waited for: 13 -> 74; matrix products, arithmetic and copies ran while one was open for 13% -> 26% of each run, Pallas kernels for 0% -> 0%
where the time goes in v1:
time: 1120 us; the launch traced here: 1110 us
  waiting for transfers between devices  508 us (45%)
  starting transfers between devices  227 us (20%)
  local copies, waits for them, and re-layouts  132 us (12%)
  matrix products  127 us (11%)
  other arithmetic  60.5 us (5%)
  blocking collectives  43.2 us (4%)
  between operations  14.2 us (1%)
    ppermute x161, waiting for transfers between devices, send(): return lax.ppermute(value, AXES, moves(2 * LINE * 4, rule))  508 us
    ppermute x161, starting transfers between devices, send(): return lax.ppermute(value, AXES, moves(2 * LINE * 4, rule))  227 us
    psum x1, blocking collectives, per_device_line(): lax.psum(jnp.stack([first_part, second_part, third_part, fourth_part]), A...  43.2 us
    unnamed x417, local copies, waits for them, and re-layouts  38.8 us
    dot_general x14, matrix products, dot(): return jnp.dot(left_side, right_side, preferred_element_type=jnp.float32)  38.7 us
    dynamic_update_slice x86, local copies, waits for them, and re-layouts, place(): return lax.dynamic_update_slice(array, piece, starts)  32.7 us
    dot_general x5, matrix products, outer_sum(): jnp.einsum('td,tf->df', left_side, right_side, preferred_element_type=jnp...  32.2 us
    dot_general x14, matrix products, dot_rows(): jnp.einsum('tf,df->td', left_side, right_side, preferred_element_type=jnp...  31.9 us
  transfers between devices with their start and end apart: 161, of which 74 were waited for; matrix products, arithmetic and copies ran while one was open for 26% of the time, Pallas kernels for 0%

profile of v1, /device:TPU:20, one launch (start us, length us, event | category | flops | bytes accessed | tf_op | source)
XLA Modules:
  0.0 1110.6 jit_solution(799220039483455922)
XLA Ops:
  76.0 9.8 collective-permute-done.35
  110.5 10.6 collective-permute-done.45
  183.3 15.2 %collective-permute-done.25 = bf16[4,72,512]{2,1,0:T(8,128)(2,1)S(1)} collective-permute-done((bf16[4,72,512]{2,1,0:T(8,128)(2,1)S(1)}, bf16[4,72,512]{2,1,0:T(8,128)(2,1)S(1)}, u32[]{:S(2)}, u32[]{:S(2)}) %collective-permute-start.25) | collective-permute-done | bytes 294944 | tf_op jit(solution)/shard_map/ppermute | solution.py:322
  257.4 24.1 %collective-permute-done.43 = bf16[8,72,1152]{2,1,0:T(8,128)(2,1)S(1)} collective-permute-done((bf16[8,72,1152]{2,1,0:T(8,128)(2,1)S(1)}, bf16[8,72,1152]{2,1,0:T(8,128)(2,1)S(1)}, u32[]{:S(2)}, u32[]{:S(2)}) %collective-permute-start.43) | collective-permute-done | bytes 1327136 | tf_op jit(solution)/shard_map/ppermute | solution.py:322
  282.6 11.6 %collective-permute-done.15 = bf16[4,72,1024]{2,1,0:T(8,128)(2,1)S(1)} collective-permute-done((bf16[4,72,1024]{2,1,0:T(8,128)(2,1)S(1)}, bf16[4,72,1024]{2,1,0:T(8,128)(2,1)S(1)}, u32[]{:S(2)}, u32[]{:S(2)}) %collective-permute-start.15) | collective-permute-done | bytes 589856 | tf_op jit(solution)/shard_map/ppermute | solution.py:322
  313.8 9.2 collective-permute-done.16
  329.6 8.6 collective-permute-done.17
  366.4 13.2 %collective-permute-done.33 = bf16[128,2304]{1,0:T(8,128)(2,1)S(1)} collective-permute-done((bf16[128,2304]{1,0:T(8,128)(2,1)S(1)}, bf16[128,2304]{1,0:T(8,128)(2,1)S(1)}, u32[]{:S(2)}, u32[]{:S(2)}) %collective-permute-start.33) | collective-permute-done | bytes 589856 | tf_op jit(solution)/shard_map/ppermute | solution.py:322
  387.0 9.2 collective-permute-done.34
  409.9 19.4 %collective-permute-done.73 = bf16[128,2304]{1,0:T(8,128)(2,1)S(1)} collective-permute-done((bf16[128,2304]{1,0:T(8,128)(2,1)S(1)}, bf16[128,2304]{1,0:T(8,128)(2,1)S(1)}, u32[]{:S(2)}, u32[]{:S(2)}) %collective-permute-start.73) | collective-permute-done | bytes 589856 | tf_op jit(solution)/shard_map/ppermute | solution.py:322
  452.7 10.7 collective-permute-done.77
  476.4 12.2 %collective-permute-done.78 = bf16[128,2304]{1,0:T(8,128)(2,1)S(1)} collective-permute-done((bf16[128,2304]{1,0:T(8,128)(2,1)S(1)}, bf16[128,2304]{1,0:T(8,128)(2,1)S(1)}, u32[]{:S(2)}, u32[]{:S(2)}) %collective-permute-start.78) | collective-permute-done | bytes 589856 | tf_op jit(solution)/shard_map/ppermute | solution.py:322
  516.5 11.8 %collective-permute-done.71 = bf16[128,2304]{1,0:T(8,128)(2,1)S(1)} collective-permute-done((bf16[128,2304]{1,0:T(8,128)(2,1)S(1)}, bf16[128,2304]{1,0:T(8,128)(2,1)S(1)}, u32[]{:S(2)}, u32[]{:S(2)}) %collective-permute-start.71) | collective-permute-done | bytes 589856 | tf_op jit(solution)/shard_map/ppermute | solution.py:322
  563.6 16.1 %collective-permute-done.91 = bf16[128,2304]{1,0:T(8,128)(2,1)S(1)} collective-permute-done((bf16[128,2304]{1,0:T(8,128)(2,1)S(1)}, bf16[128,2304]{1,0:T(8,128)(2,1)S(1)}, u32[]{:S(2)}, u32[]{:S(2)}) %collective-permute-start.91) | collective-permute-done | bytes 589856 | tf_op jit(solution)/shard_map/ppermute | solution.py:322
  605.2 15.2 %collective-permute-done.95 = bf16[128,2304]{1,0:T(8,128)(2,1)S(1)} collective-permute-done((bf16[128,2304]{1,0:T(8,128)(2,1)S(1)}, bf16[128,2304]{1,0:T(8,128)(2,1)S(1)}, u32[]{:S(2)}, u32[]{:S(2)}) %collective-permute-start.95) | collective-permute-done | bytes 589856 | tf_op jit(solution)/shard_map/ppermute | solution.py:322
  623.7 9.4 convolution_convert_fusion.1
  680.9 12.1 %collective-permute-done.98 = bf16[128,2304]{1,0:T(8,128)(2,1)S(1)} collective-permute-done((bf16[128,2304]{1,0:T(8,128)(2,1)S(1)}, bf16[128,2304]{1,0:T(8,128)(2,1)S(1)}, u32[]{:S(2)}, u32[]{:S(2)}) %collective-permute-start.98) | collective-permute-done | bytes 589856 | tf_op jit(solution)/shard_map/ppermute | solution.py:322
  756.6 52.9 %collective-permute-done.122 = bf16[4,72,512]{2,1,0:T(8,128)(2,1)S(1)} collective-permute-done((bf16[4,72,512]{2,1,0:T(8,128)(2,1)}, bf16[4,72,512]{2,1,0:T(8,128)(2,1)S(1)}, u32[]{:S(2)}, u32[]{:S(2)}) %collective-permute-start.122) | collective-permute-done | bytes 294944 | tf_op jit(solution)/shard_map/ppermute | solution.py:322
  845.3 9.0 collective-permute-done.155
  871.4 8.7 collective-permute-done.145
  931.7 12.3 %collective-permute-done.128 = bf16[4,72,512]{2,1,0:T(8,128)(2,1)S(1)} collective-permute-done((bf16[4,72,512]{2,1,0:T(8,128)(2,1)S(1)}, bf16[4,72,512]{2,1,0:T(8,128)(2,1)S(1)}, u32[]{:S(2)}, u32[]{:S(2)}) %collective-permute-start.128) | collective-permute-done | bytes 294944 | tf_op jit(solution)/shard_map/ppermute | solution.py:322
  975.7 14.1 %collective-permute-done.109 = bf16[4,72,1024]{2,1,0:T(8,128)(2,1)S(1)} collective-permute-done((bf16[4,72,1024]{2,1,0:T(8,128)(2,1)S(1)}, bf16[4,72,1024]{2,1,0:T(8,128)(2,1)S(1)}, u32[]{:S(2)}, u32[]{:S(2)}) %collective-permute-start.109) | collective-permute-done | bytes 589856 | tf_op jit(solution)/shard_map/ppermute | solution.py:322
  989.8 9.1 collective-permute-done.113
  1048.9 43.2 %psum.7 = f32[4,2304]{1,0:T(4,128)} all-reduce(f32[4,2304]{1,0:T(4,128)} %pad_maximum_fusion.23), channel_id=1, replica_groups=mesh['rows'=2,'seq'=16] {'rows','seq'}, use_global_device_ids=true, to_apply=%region_17.18 | all-reduce | flops 9216 | bytes 73728 | tf_op jit(solution)/shard_map/psum | solution.py:739
  (1040 shorter events, 728.9 us)
Async XLA Ops:
  6.9 55.9 %collective-permute-start.19 = (bf16[72,512]{1,0:T(8,128)(2,1)}, bf16[72,512]{1,0:T(8,128)(2,1)}, u32[]{:S(2)}, u32[]{:S(2)}) collective-permute-start(bf16[72,512]{1,0:T(8,128)(2,1)} %bitcast.800), channel_id=1, source_target_pairs={{0,1},{1,0},{2,3},{3,2},{4,5},{5,4},{6,7},{7,6},{8,9},{9,8},{10,11... | collective-permute-start | bytes 221192 | tf_op jit(solution)/shard_map/ppermute | solution.py:322
  7.5 57.4 %collective-permute-start.20 = (bf16[72,512]{1,0:T(8,128)(2,1)}, bf16[72,512]{1,0:T(8,128)(2,1)}, u32[]{:S(2)}, u32[]{:S(2)}) collective-permute-start(bf16[72,512]{1,0:T(8,128)(2,1)} %bitcast.799), channel_id=1, source_target_pairs={{0,2},{1,3},{2,0},{3,1},{4,6},{5,7},{6,4},{7,5},{8,10},{9,11},{10,... | collective-permute-start | bytes 221192 | tf_op jit(solution)/shard_map/ppermute | solution.py:322
  9.6 56.7 %collective-permute-start.21 = (bf16[72,512]{1,0:T(8,128)(2,1)}, bf16[72,512]{1,0:T(8,128)(2,1)}, u32[]{:S(2)}, u32[]{:S(2)}) collective-permute-start(bf16[72,512]{1,0:T(8,128)(2,1)} %bitcast.798), channel_id=1, source_target_pairs={{0,2},{1,3},{2,0},{3,1},{4,6},{5,7},{6,4},{7,5},{8,10},{9,11},{10,... | collective-permute-start | bytes 221192 | tf_op jit(solution)/shard_map/ppermute | solution.py:322
  62.8 107.2 %collective-permute-start.5 = (bf16[72,1024]{1,0:T(8,128)(2,1)}, bf16[72,1024]{1,0:T(8,128)(2,1)S(1)}, u32[]{:S(2)}, u32[]{:S(2)}) collective-permute-start(bf16[72,1024]{1,0:T(8,128)(2,1)} %bitcast.795), channel_id=1, source_target_pairs={{0,2},{1,3},{2,0},{3,1},{4,6},{5,7},{6,4},{7,5},{8,10},{9,11},{10,... | collective-permute-start | bytes 442376 | tf_op jit(solution)/shard_map/ppermute | solution.py:322
  64.9 191.3 %collective-permute-start.1 = (bf16[128,2304]{1,0:T(8,128)(2,1)}, bf16[128,2304]{1,0:T(8,128)(2,1)S(1)}, u32[]{:S(2)}, u32[]{:S(2)}) collective-permute-start(bf16[128,2304]{1,0:T(8,128)(2,1)} %fusion.65), channel_id=1, source_target_pairs={{0,2},{1,3},{2,0},{3,1},{4,6},{5,7},{6,4},{7,5},{8,10},{9,11},{10,... | collective-permute-start | bytes 1769480 | tf_op jit(solution)/shard_map/ppermute | solution.py:322
  254.7 102.1 %collective-permute-start.52 = (bf16[8,72,1152]{2,1,0:T(8,128)(2,1)}, bf16[8,72,1152]{2,1,0:T(8,128)(2,1)}, u32[]{:S(2)}, u32[]{:S(2)}) collective-permute-start(bf16[8,72,1152]{2,1,0:T(8,128)(2,1)} %bitcast_dynamic-update-slice_fusion.29), channel_id=1, source_target_pairs={{0,1},{1,0},{2,3},{3,2},{4,5},{5,4},{6,7},{7,6},{8,9},{9,8},{10,11... | collective-permute-start | bytes 3981320 | tf_op jit(solution)/shard_map/ppermute | solution.py:322
  256.2 88.7 %collective-permute-start.53 = (bf16[8,72,1152]{2,1,0:T(8,128)(2,1)}, bf16[8,72,1152]{2,1,0:T(8,128)(2,1)}, u32[]{:S(2)}, u32[]{:S(2)}) collective-permute-start(bf16[8,72,1152]{2,1,0:T(8,128)(2,1)} %bitcast_dynamic-update-slice_fusion.29), channel_id=1, source_target_pairs={{0,16},{1,17},{2,18},{3,19},{4,20},{5,21},{6,22},{7,23},{8,24},{9,... | collective-permute-start | bytes 3981320 | tf_op jit(solution)/shard_map/ppermute | solution.py:322
  294.1 67.6 %collective-permute-start.62 = (bf16[8,72,1152]{2,1,0:T(8,128)(2,1)}, bf16[8,72,1152]{2,1,0:T(8,128)(2,1)}, u32[]{:S(2)}, u32[]{:S(2)}) collective-permute-start(bf16[8,72,1152]{2,1,0:T(8,128)(2,1)} %bitcast_dynamic-update-slice_fusion.28), channel_id=1, source_target_pairs={{0,1},{1,0},{2,3},{3,2},{4,5},{5,4},{6,7},{7,6},{8,9},{9,8},{10,11... | collective-permute-start | bytes 3981320 | tf_op jit(solution)/shard_map/ppermute | solution.py:322
  294.2 55.8 %collective-permute-start.63 = (bf16[8,72,1152]{2,1,0:T(8,128)(2,1)}, bf16[8,72,1152]{2,1,0:T(8,128)(2,1)}, u32[]{:S(2)}, u32[]{:S(2)}) collective-permute-start(bf16[8,72,1152]{2,1,0:T(8,128)(2,1)} %bitcast_dynamic-update-slice_fusion.28), channel_id=1, source_target_pairs={{0,16},{1,17},{2,18},{3,19},{4,20},{5,21},{6,22},{7,23},{8,24},{9,... | collective-permute-start | bytes 3981320 | tf_op jit(solution)/shard_map/ppermute | solution.py:322
  402.5 113.9 %collective-permute-start.65 = (bf16[128,2304]{1,0:T(8,128)(2,1)S(1)}, bf16[128,2304]{1,0:T(8,128)(2,1)S(1)}, u32[]{:S(2)}, u32[]{:S(2)}) collective-permute-start(bf16[128,2304]{1,0:T(8,128)(2,1)S(1)} %slice.263), channel_id=1, source_target_pairs={{0,2},{1,3},{2,0},{3,1},{4,6},{5,7},{6,4},{7,5},{8,10},{9,11},{10,... | collective-permute-start | bytes 1769480 | tf_op jit(solution)/shard_map/ppermute | solution.py:322
  450.1 65.3 %collective-permute-start.74 = (bf16[128,2304]{1,0:T(8,128)(2,1)S(1)}, bf16[128,2304]{1,0:T(8,128)(2,1)S(1)}, u32[]{:S(2)}, u32[]{:S(2)}) collective-permute-start(bf16[128,2304]{1,0:T(8,128)(2,1)S(1)} %slice.267), channel_id=1, source_target_pairs={{0,2},{1,3},{2,0},{3,1},{4,6},{5,7},{6,4},{7,5},{8,10},{9,11},{10,... | collective-permute-start | bytes 1769480 | tf_op jit(solution)/shard_map/ppermute | solution.py:322
  555.2 139.7 %collective-permute-start.83 = (bf16[128,2304]{1,0:T(8,128)(2,1)}, bf16[128,2304]{1,0:T(8,128)(2,1)S(1)}, u32[]{:S(2)}, u32[]{:S(2)}) collective-permute-start(bf16[128,2304]{1,0:T(8,128)(2,1)} %slice.271), channel_id=1, source_target_pairs={{0,2},{1,3},{2,0},{3,1},{4,6},{5,7},{6,4},{7,5},{8,10},{9,11},{10,... | collective-permute-start | bytes 1769480 | tf_op jit(solution)/shard_map/ppermute | solution.py:322
  590.6 90.2 %collective-permute-start.92 = (bf16[128,2304]{1,0:T(8,128)(2,1)}, bf16[128,2304]{1,0:T(8,128)(2,1)}, u32[]{:S(2)}, u32[]{:S(2)}) collective-permute-start(bf16[128,2304]{1,0:T(8,128)(2,1)} %slice.275), channel_id=1, source_target_pairs={{0,2},{1,3},{2,0},{3,1},{4,6},{5,7},{6,4},{7,5},{8,10},{9,11},{10,... | collective-permute-start | bytes 1769480 | tf_op jit(solution)/shard_map/ppermute | solution.py:322
  713.5 105.3 %collective-permute-start.153 = (bf16[8,72,1152]{2,1,0:T(8,128)(2,1)}, bf16[8,72,1152]{2,1,0:T(8,128)(2,1)}, u32[]{:S(2)}, u32[]{:S(2)}) collective-permute-start(bf16[8,72,1152]{2,1,0:T(8,128)(2,1)} %dynamic-slice_bitcast_fusion.3), channel_id=1, source_target_pairs={{0,16},{1,17},{2,18},{3,19},{4,20},{5,21},{6,22},{7,23},{8,24},{9,... | collective-permute-start | bytes 3981320 | tf_op jit(solution)/shard_map/ppermute | solution.py:322
  719.9 101.1 %collective-permute-start.144 = (bf16[8,72,1152]{2,1,0:T(8,128)(2,1)}, bf16[8,72,1152]{2,1,0:T(8,128)(2,1)}, u32[]{:S(2)}, u32[]{:S(2)}) collective-permute-start(bf16[8,72,1152]{2,1,0:T(8,128)(2,1)} %dynamic-slice_bitcast_fusion.4), channel_id=1, source_target_pairs={{0,16},{1,17},{2,18},{3,19},{4,20},{5,21},{6,22},{7,23},{8,24},{9,... | collective-permute-start | bytes 3981320 | tf_op jit(solution)/shard_map/ppermute | solution.py:322
  724.7 99.5 %collective-permute-start.135 = (bf16[8,72,1152]{2,1,0:T(8,128)(2,1)}, bf16[8,72,1152]{2,1,0:T(8,128)(2,1)}, u32[]{:S(2)}, u32[]{:S(2)}) collective-permute-start(bf16[8,72,1152]{2,1,0:T(8,128)(2,1)} %dynamic-slice_bitcast_fusion.5), channel_id=1, source_target_pairs={{0,16},{1,17},{2,18},{3,19},{4,20},{5,21},{6,22},{7,23},{8,24},{9,... | collective-permute-start | bytes 3981320 | tf_op jit(solution)/shard_map/ppermute | solution.py:322
  746.6 62.9 %collective-permute-start.122 = (bf16[4,72,512]{2,1,0:T(8,128)(2,1)}, bf16[4,72,512]{2,1,0:T(8,128)(2,1)S(1)}, u32[]{:S(2)}, u32[]{:S(2)}) collective-permute-start(bf16[4,72,512]{2,1,0:T(8,128)(2,1)} %get-tuple-element.59), channel_id=1, source_target_pairs={{0,16},{1,17},{2,18},{3,19},{4,20},{5,21},{6,22},{7,23},{8,24},{9,... | collective-permute-start | bytes 884744 | tf_op jit(solution)/shard_map/ppermute | solution.py:322
  747.6 68.1 %collective-permute-start.126 = (bf16[4,72,512]{2,1,0:T(8,128)(2,1)}, bf16[4,72,512]{2,1,0:T(8,128)(2,1)}, u32[]{:S(2)}, u32[]{:S(2)}) collective-permute-start(bf16[4,72,512]{2,1,0:T(8,128)(2,1)} %get-tuple-element.57), channel_id=1, source_target_pairs={{0,16},{1,17},{2,18},{3,19},{4,20},{5,21},{6,22},{7,23},{8,24},{9,... | collective-permute-start | bytes 884744 | tf_op jit(solution)/shard_map/ppermute | solution.py:322
  815.7 116.0 %collective-permute-start.125 = (bf16[4,72,512]{2,1,0:T(8,128)(2,1)}, bf16[4,72,512]{2,1,0:T(8,128)(2,1)S(1)}, u32[]{:S(2)}, u32[]{:S(2)}) collective-permute-start(bf16[4,72,512]{2,1,0:T(8,128)(2,1)} %get-tuple-element.58), channel_id=1, source_target_pairs={{0,16},{1,17},{2,18},{3,19},{4,20},{5,21},{6,22},{7,23},{8,24},{9,... | collective-permute-start | bytes 884744 | tf_op jit(solution)/shard_map/ppermute | solution.py:322
  818.8 130.2 %collective-permute-start.121 = (bf16[4,72,512]{2,1,0:T(8,128)(2,1)S(1)}, bf16[4,72,512]{2,1,0:T(8,128)(2,1)S(1)}, u32[]{:S(2)}, u32[]{:S(2)}) collective-permute-start(bf16[4,72,512]{2,1,0:T(8,128)(2,1)S(1)} %copy-done.73), channel_id=1, source_target_pairs={{0,16},{1,17},{2,18},{3,19},{4,20},{5,21},{6,22},{7,23},{8,24},{9,... | collective-permute-start | bytes 884744 | tf_op jit(solution)/shard_map/ppermute | solution.py:322
  952.5 56.5 %collective-permute-start.132 = (bf16[72,512]{1,0:T(8,128)(2,1)}, bf16[72,512]{1,0:T(8,128)(2,1)}, u32[]{:S(2)}, u32[]{:S(2)}) collective-permute-start(bf16[72,512]{1,0:T(8,128)(2,1)} %get-tuple-element.144), channel_id=1, source_target_pairs={{0,2},{1,3},{2,0},{3,1},{4,6},{5,7},{6,4},{7,5},{8,10},{9,11},{10,... | collective-permute-start | bytes 221192 | tf_op jit(solution)/shard_map/ppermute | solution.py:322
  975.7 56.2 %collective-permute-start.106 = (bf16[2,128,2304]{2,1,0:T(8,128)(2,1)S(1)}, bf16[2,128,2304]{2,1,0:T(8,128)(2,1)S(1)}, u32[]{:S(2)}, u32[]{:S(2)}) collective-permute-start(bf16[2,128,2304]{2,1,0:T(8,128)(2,1)S(1)} %slice_bitcast_fusion.1), channel_id=1, source_target_pairs={{0,1},{1,0},{2,3},{3,2},{4,5},{5,4},{6,7},{7,6},{8,9},{9,8},{10,11... | collective-permute-start | bytes 3538952 | tf_op jit(solution)/shard_map/ppermute | solution.py:322
  1034.9 61.4 %collective-permute-start.108 = (bf16[4,72,1024]{2,1,0:T(8,128)(2,1)}, bf16[4,72,1024]{2,1,0:T(8,128)(2,1)}, u32[]{:S(2)}, u32[]{:S(2)}) collective-permute-start(bf16[4,72,1024]{2,1,0:T(8,128)(2,1)} %get-tuple-element.48), channel_id=1, source_target_pairs={{0,16},{1,17},{2,18},{3,19},{4,20},{5,21},{6,22},{7,23},{8,24},{9,... | collective-permute-start | bytes 1769480 | tf_op jit(solution)/shard_map/ppermute | solution.py:322
  1036.6 59.6 %collective-permute-start.111 = (bf16[4,72,1024]{2,1,0:T(8,128)(2,1)}, bf16[4,72,1024]{2,1,0:T(8,128)(2,1)}, u32[]{:S(2)}, u32[]{:S(2)}) collective-permute-start(bf16[4,72,1024]{2,1,0:T(8,128)(2,1)} %get-tuple-element.52), channel_id=1, source_target_pairs={{4,8},{5,9},{6,10},{7,11},{8,4},{9,5},{10,6},{11,7},{20,24},{21,25... | collective-permute-start | bytes 1769480 | tf_op jit(solution)/shard_map/ppermute | solution.py:322
  (327 other events, 4770.8 us)

commit v2 on v1

--- a/solution.py
+++ b/solution.py
@@ -1,8 +1,11 @@
+import functools
 import math
 
 import jax
 import jax.numpy as jnp
 from jax import lax
+from jax.experimental import pallas as pl
+from jax.experimental.pallas import tpu as pltpu
 from jax.sharding import PartitionSpec as P
 
 D = 2304
@@ -444,75 +447,436 @@
     return (spot.x ^ dx) * 2 + (spot.c ^ dc)
 
 
-def exchange_group(spot, pieces):
-    own = pick(pieces, member(spot, 0, 0))
-    from_core = to_core(pick(pieces, member(spot, 0, 1)))
-    from_x = to_x(pick(pieces, member(spot, 1, 0)))
-    from_both = to_core(to_x(pick(pieces, member(spot, 1, 1))))
-    out = jnp.zeros_like(pieces)
-    for dx, dc, piece in ((0, 0, own), (0, 1, from_core), (1, 0, from_x), (1, 1, from_both)):
-        out = place(out, piece[None], (member(spot, dx, dc), 0, 0))
-    return out
-
-
-def gather_heads(spot, pieces):
-    group = exchange_group(spot, pieces)
-    rows, cols = pieces.shape[1:]
-    out = jnp.zeros((2, LINE, 4, rows, cols), pieces.dtype)
-    for slot, block in enumerate(gather_line(spot, group)):
-        z = spot.slots[slot]
-        out = place(out, block[None, None], (spot.y, z, 0, 0, 0))
-        out = place(out, to_row(block)[None, None], (1 - spot.y, z, 0, 0, 0))
-    return out.reshape(2 * LINE * 4 * rows, cols)
-
-
-def scatter_heads(spot, sums):
-    cols = sums.shape[1]
-    rows = sums.shape[0] // (2 * LINE * 4)
-    blocks = sums.reshape(2, LINE, 4, rows, cols)
-    mine = pick(blocks, spot.y)
-    other = pick(blocks, 1 - spot.y)
-    parts = [None] * LINE
-    for slot in (3, 2, 1, 0):
-        z = spot.slots[slot]
-        parts[slot] = wide(pick(mine, z)) + wide(to_row(pick(other, z)))
-    return exchange_group(spot, low(reduce_line(parts)))
-
-
-def gather_hidden(spot, pieces):
-    rows, width = pieces.shape[1:]
-    chip = spot.z * 2 + spot.x
-    plane = jnp.zeros_like(pieces)
-    for dz, dx in ((3, 0), (3, 1), (2, 0), (2, 1), (1, 0), (1, 1), (0, 1), (0, 0)):
-        there = (spot.z ^ dz) * 2 + (spot.x ^ dx)
-        piece = pick(pieces, there)
-        if dz or dx:
-            piece = to_chip(piece, dz, dx)
-        plane = place(plane, piece[None], (there, 0, 0))
-    across = to_row(plane)
-    out = jnp.zeros((2, LINE * 2, 2, rows, width), pieces.dtype)
-    for half, y in ((plane, spot.y), (across, 1 - spot.y)):
-        out = place(out, half[None, :, None], (y, 0, spot.c, 0, 0))
-        out = place(out, to_core(half)[None, :, None], (y, 0, 1 - spot.c, 0, 0))
-    return out.reshape(2 * LINE * 4 * rows, width)
-
-
-def scatter_hidden(spot, sums):
+def narrow_hidden(spot, sums):
     width = sums.shape[1]
     rows = sums.shape[0] // (2 * LINE * 4)
     blocks = sums.reshape(2, LINE * 2, 2, rows, width)
     cores = low(
         wide(pick(blocks, spot.c, 2)) + wide(to_core(pick(blocks, 1 - spot.c, 2)))
     )
-    plane = low(wide(pick(cores, spot.y)) + wide(to_row(pick(cores, 1 - spot.y))))
-    out = jnp.zeros_like(plane)
-    for dz, dx in ((3, 0), (3, 1), (2, 0), (2, 1), (1, 0), (1, 1), (0, 1), (0, 0)):
-        there = (spot.z ^ dz) * 2 + (spot.x ^ dx)
-        piece = pick(plane, there)
-        if dz or dx:
-            piece = to_chip(piece, dz, dx)
-        out = place(out, piece[None], (there, 0, 0))
-    return wide(out).transpose(1, 0, 2).reshape(rows, LINE * 2 * width)
+    return low(wide(pick(cores, spot.y)) + wide(to_row(pick(cores, 1 - spot.y))))
+
+
+GROUP = ((0, 0), (0, 1), (1, 0), (1, 1))
+PLANE = ((2, 0), (1, 0), (3, 0), (0, 1), (2, 1), (1, 1), (3, 1))
+
+
+def my_place():
+    index = lax.axis_index("seq")
+    return lax.axis_index("rows"), index // 4, (index // 2) % 2, index % 2
+
+
+def along_line(z, step):
+    return (z, z + 1 - 2 * (z % 2), (z + 2) % LINE, LINE - 1 - z)[step]
+
+
+def device_at(y, z, x, c):
+    return (y, (z * 2 + x) * 2 + c)
+
+
+def under(condition, action):
+    if condition is None:
+        action()
+    else:
+        pl.when(condition)(action)
+
+
+class Courier:
+    def __init__(self, send_sem, recv_sem):
+        self.send_sem = send_sem
+        self.recv_sem = recv_sem
+        self.names = {}
+        self.sent = []
+
+    def copy(self, source, target, device, name):
+        slot = self.names.setdefault(name, len(self.names))
+        return pltpu.make_async_remote_copy(
+            src_ref=source,
+            dst_ref=target,
+            send_sem=self.send_sem.at[slot],
+            recv_sem=self.recv_sem.at[slot],
+            device_id=device,
+            device_id_type=pl.DeviceIdType.MESH,
+        )
+
+    def send(self, source, target, device, name, condition=None):
+        copy = self.copy(source, target, device, name)
+        under(condition, copy.start)
+        self.sent.append((copy, condition))
+
+    def arrive(self, target, device, name, condition=None):
+        under(condition, self.copy(target, target, device, name).wait_recv)
+
+    def finish(self):
+        for copy, condition in self.sent:
+            under(condition, copy.wait_send)
+
+
+def greet(devices):
+    barrier = pltpu.get_barrier_semaphore()
+    for device in devices:
+        pl.semaphore_signal(
+            barrier, inc=1, device_id=device, device_id_type=pl.DeviceIdType.MESH
+        )
+    pl.semaphore_wait(barrier, len(devices))
+
+
+def gather_kernel(count, *refs):
+    heads_in, tokens_in = refs[:2]
+    hidden_in = refs[2 : 2 + count]
+    heads, tokens = refs[2 + count : 4 + count]
+    hidden = refs[4 + count : 4 + 2 * count]
+    send_sem, recv_sem, local_sem = refs[4 + 2 * count :]
+    y, z, x, c = my_place()
+    me = x * 2 + c
+    chip = z * 2 + x
+    chips = LINE * 2
+    group = {d: device_at(y, z, (x + d[0]) % 2, (c + d[1]) % 2) for d in GROUP[1:]}
+    plane = {d: device_at(y, along_line(z, d[0]), (x + d[1]) % 2, c) for d in PLANE}
+    row_peer = device_at(1 - y, z, x, c)
+    core_peer = group[(0, 1)]
+    up = device_at(y, jnp.minimum(z + 1, LINE - 1), x, c)
+    down = device_at(y, jnp.maximum(z - 1, 0), x, c)
+    can_up = z < LINE - 1
+    can_down = z > 0
+    greet([row_peer, core_peer, group[(1, 1)]] + list(plane.values()))
+    post = Courier(send_sem, recv_sem)
+
+    def member(d):
+        return ((x + d[0]) % 2) * 2 + (c + d[1]) % 2
+
+    def chip_of(d):
+        return along_line(z, d[0]) * 2 + (x + d[1]) % 2
+
+    def columns(ref, which):
+        width = ref.shape[1] // chips
+        return ref.at[:, pl.ds(pl.multiple_of(which * width, 128), width)]
+
+    for d, device in group.items():
+        post.send(heads_in.at[member(d)], heads.at[y, z, me], device, ("group", d))
+    local = [(heads_in.at[me], heads.at[y, z, me]), (tokens_in, tokens.at[0])]
+    local += [(columns(w, chip), out.at[y, chip, c]) for w, out in zip(hidden_in, hidden)]
+    kept = []
+    for slot, (source, target) in enumerate(local):
+        kept.append(pltpu.make_async_copy(source, target, local_sem.at[slot]))
+        kept[-1].start()
+    for d, device in group.items():
+        post.send(tokens_in, tokens.at[d[0] * 2 + d[1]], device, ("tokens", d))
+
+    def spread(source, which):
+        target = heads.at[y, z, member(which)]
+        post.send(source, target, up, ("up", 1, which), can_up)
+        post.send(source, target, down, ("down", 1, which), can_down)
+        post.send(source, target, row_peer, ("row", 0, 0, which))
+
+    def plane_out(m):
+        for d in PLANE:
+            post.send(
+                columns(hidden_in[m], chip_of(d)),
+                hidden[m].at[y, chip, c],
+                plane[d],
+                ("plane", m, d),
+            )
+        own = columns(hidden_in[m], chip)
+        post.send(own, hidden[m].at[y, chip, c], row_peer, ("far", m, (0, 0)))
+        post.send(own, hidden[m].at[y, chip, c], core_peer, ("core", 0, m, (0, 0)))
+
+    def plane_in(m):
+        for d in PLANE:
+            block = hidden[m].at[y, chip_of(d), c]
+            post.arrive(block, core_peer, ("plane", m, d))
+            post.send(block, block, row_peer, ("far", m, d))
+            post.send(block, block, core_peer, ("core", 0, m, d))
+
+    spread(heads_in.at[me], (0, 0))
+    if count:
+        plane_out(0)
+    for d in GROUP[1:]:
+        block = heads.at[y, z, member(d)]
+        post.arrive(block, core_peer, ("group", d))
+        spread(block, d)
+    sides = ((-1, "up", up, can_up), (1, "down", down, can_down))
+    for step in range(1, LINE):
+        for d in GROUP:
+            for sign, name, device, onward in sides:
+                here = z >= step if sign < 0 else z <= LINE - 1 - step
+                block = heads.at[y, jnp.clip(z + sign * step, 0, LINE - 1), member(d)]
+                post.arrive(block, core_peer, (name, step, d), here)
+                if step < LINE - 1:
+                    post.send(block, block, device, (name, step + 1, d), here & onward)
+                post.send(block, block, row_peer, ("row", sign, step, d), here)
+        if step == 1 and count:
+            plane_in(0)
+            if count > 1:
+                plane_out(1)
+    for m in range(1, count):
+        if m + 1 < count:
+            plane_out(m + 1)
+        plane_in(m)
+    for m in range(count):
+        for d in ((0, 0),) + PLANE:
+            block = hidden[m].at[1 - y, chip_of(d), c]
+            post.arrive(block, core_peer, ("far", m, d))
+            post.send(block, block, core_peer, ("core", 1, m, d))
+    for d in GROUP[1:]:
+        post.arrive(tokens.at[d[0] * 2 + d[1]], core_peer, ("tokens", d))
+    for d in GROUP:
+        post.arrive(heads.at[1 - y, z, member(d)], core_peer, ("row", 0, 0, d))
+        for step in range(1, LINE):
+            for sign, name, device, onward in sides:
+                here = z >= step if sign < 0 else z <= LINE - 1 - step
+                block = heads.at[1 - y, jnp.clip(z + sign * step, 0, LINE - 1), member(d)]
+                post.arrive(block, core_peer, ("row", sign, step, d), here)
+    for m in range(count):
+        for half in range(2):
+            for d in ((0, 0),) + PLANE:
+                block = hidden[m].at[y if half == 0 else 1 - y, chip_of(d), 1 - c]
+                post.arrive(block, core_peer, ("core", half, m, d))
+    post.finish()
+    for copy in kept:
+        copy.wait()
+
+
+def gather_weights(heads_in, tokens_in, hidden_in):
+    rows = heads_in.shape[1]
+    count = len(hidden_in)
+    anywhere = pl.BlockSpec(memory_space=pl.ANY)
+    copies = 44 + 4 * len(GROUP) + (7 + 24) * count
+    outs = [
+        jax.ShapeDtypeStruct((2, LINE, 4, rows, heads_in.shape[2]), jnp.bfloat16),
+        jax.ShapeDtypeStruct((4,) + tokens_in.shape, jnp.bfloat16),
+    ]
+    for matrix in hidden_in:
+        width = matrix.shape[1] // (LINE * 2)
+        outs.append(jax.ShapeDtypeStruct((2, LINE * 2, 2, rows, width), jnp.bfloat16))
+    found = pl.pallas_call(
+        functools.partial(gather_kernel, count),
+        out_shape=outs,
+        in_specs=[anywhere] * (2 + count),
+        out_specs=[anywhere] * (2 + count),
+        scratch_shapes=[
+            pltpu.SemaphoreType.DMA((copies,)),
+            pltpu.SemaphoreType.DMA((copies,)),
+            pltpu.SemaphoreType.DMA((2 + count,)),
+        ],
+        compiler_params=pltpu.CompilerParams(collective_id=0, has_side_effects=True),
+    )(heads_in, tokens_in, *hidden_in)
+    total = 2 * LINE * 4 * rows
+    heads = found[0].reshape(total, heads_in.shape[2])
+    tokens = found[1].reshape(4 * tokens_in.shape[0], tokens_in.shape[1])
+    return heads, tokens, [block.reshape(total, block.shape[-1]) for block in found[2:]]
+
+
+def scatter_kernel(parts, count, *refs):
+    heads_in = refs[:parts]
+    hidden_in = refs[parts : parts + count]
+    heads = refs[parts + count : 2 * parts + count]
+    hidden = refs[2 * parts + count : 2 * (parts + count)]
+    scratch = refs[2 * (parts + count) :]
+    own, across, above, below = (scratch[n * parts : (n + 1) * parts] for n in range(4))
+    send_sem, recv_sem, load_sem, head_send, head_recv, local_sem = scratch[4 * parts :]
+    y, z, x, c = my_place()
+    me = x * 2 + c
+    chip = z * 2 + x
+    chips = LINE * 2
+    group = {d: device_at(y, z, (x + d[0]) % 2, (c + d[1]) % 2) for d in GROUP[1:]}
+    plane = {d: device_at(y, along_line(z, d[0]), (x + d[1]) % 2, c) for d in PLANE}
+    row_peer = device_at(1 - y, z, x, c)
+    core_peer = group[(0, 1)]
+    up = device_at(y, jnp.minimum(z + 1, LINE - 1), x, c)
+    down = device_at(y, jnp.maximum(z - 1, 0), x, c)
+    greet([row_peer, core_peer, group[(1, 1)]] + list(plane.values()))
+    post = Courier(send_sem, recv_sem)
+
+    def member(d):
+        return ((x + d[0]) % 2) * 2 + (c + d[1]) % 2
+
+    def chip_of(d):
+        return along_line(z, d[0]) * 2 + (x + d[1]) % 2
+
+    order = [(0, 0, None)]
+    for step in range(1, LINE):
+        order = [(1, step, z <= LINE - 1 - step), (-1, step, z >= step)] + order
+
+    def head_copy(p, stage, source, target, device, place, m):
+        return pltpu.make_async_remote_copy(
+            src_ref=source,
+            dst_ref=target,
+            send_sem=head_send.at[p, stage, place, m],
+            recv_sem=head_recv.at[p, stage, place, m],
+            device_id=device,
+            device_id_type=pl.DeviceIdType.MESH,
+        )
+
+    def to_row_copy(p, place, m):
+        return head_copy(
+            p, 0, heads_in[p].at[1 - y, place, m], across[p].at[place, m], row_peer, place, m
+        )
+
+    def load_copy(p, place, m):
+        return pltpu.make_async_copy(
+            heads_in[p].at[y, place, m], own[p].at[place, m], load_sem.at[p, place, m]
+        )
+
+    def up_copy(p, place, m):
+        return head_copy(p, 1, own[p].at[place, m], below[p].at[place, m], up, place, m)
+
+    def down_copy(p, place, m):
+        return head_copy(p, 2, own[p].at[place, m], above[p].at[place, m], down, place, m)
+
+    def each(action):
+        lax.fori_loop(0, 4, lambda m, carry: (action(m), carry)[1], 0)
+
+    for sign, step, okay in order:
+        place = z + sign * step
+
+        def start(m, place=place):
+            for p in range(parts):
+                to_row_copy(p, place, m).start()
+                load_copy(p, place, m).start()
+
+        under(okay, lambda start=start: each(start))
+    kept = []
+    for m in range(count):
+        for d in PLANE:
+            width = hidden[m].shape[1] // chips
+            post.send(
+                hidden_in[m].at[chip_of(d)],
+                hidden[m].at[:, pl.ds(pl.multiple_of(chip * width, 128), width)],
+                plane[d],
+                ("plane", m, d),
+            )
+        kept.append(
+            pltpu.make_async_copy(
+                hidden_in[m].at[chip],
+                hidden[m].at[:, pl.ds(pl.multiple_of(chip * width, 128), width)],
+                local_sem.at[m],
+            )
+        )
+        kept[-1].start()
+
+    def ready(p, place, m):
+        to_row_copy(p, place, m).wait_recv()
+        load_copy(p, place, m).wait()
+        return wide(own[p][place, m]) + wide(across[p][place, m])
+
+    for sign, step, okay in order[:-1]:
+        place = z + sign * step
+
+        def relay(m, place=place, sign=sign):
+            for p in range(parts):
+                own[p][place, m] = low(ready(p, place, m))
+            if sign > 0:
+                @pl.when(z > 0)
+                def _():
+                    for p in range(parts):
+                        up_copy(p, place, m).wait_recv()
+                        own[p][place, m] = low(wide(own[p][place, m]) + wide(below[p][place, m]))
+            else:
+                @pl.when(z < LINE - 1)
+                def _():
+                    for p in range(parts):
+                        down_copy(p, place, m).wait_recv()
+                        own[p][place, m] = low(wide(own[p][place, m]) + wide(above[p][place, m]))
+            for p in range(parts):
+                (up_copy if sign > 0 else down_copy)(p, place, m).start()
+
+        under(okay, lambda relay=relay: each(relay))
+
+    def settle(m):
+        for p in range(parts):
+            own[p][z, m] = low(ready(p, z, m))
+
+        @pl.when(z > 0)
+        def _():
+            for p in range(parts):
+                up_copy(p, z, m).wait_recv()
+                own[p][z, m] = low(wide(own[p][z, m]) + wide(below[p][z, m]))
+
+        @pl.when(z < LINE - 1)
+        def _():
+            for p in range(parts):
+                down_copy(p, z, m).wait_recv()
+                own[p][z, m] = low(wide(own[p][z, m]) + wide(above[p][z, m]))
+
+    each(settle)
+    for p in range(parts):
+        kept.append(pltpu.make_async_copy(own[p].at[z, me], heads[p].at[me], local_sem.at[count + p]))
+        kept[-1].start()
+        for d, device in group.items():
+            post.send(own[p].at[z, member(d)], heads[p].at[me], device, ("group", p, d))
+    for p in range(parts):
+        for d in GROUP[1:]:
+            post.arrive(heads[p].at[member(d)], core_peer, ("group", p, d))
+    for m in range(count):
+        for d in PLANE:
+            width = hidden[m].shape[1] // chips
+            block = hidden[m].at[:, pl.ds(pl.multiple_of(chip_of(d) * width, 128), width)]
+            post.arrive(block, core_peer, ("plane", m, d))
+    for sign, step, okay in order:
+        place = z + sign * step
+
+        def drain(m, place=place, sign=sign):
+            for p in range(parts):
+                to_row_copy(p, place, m).wait_send()
+                if sign > 0:
+                    up_copy(p, place, m).wait_send()
+                if sign < 0:
+                    down_copy(p, place, m).wait_send()
+
+        under(okay, lambda drain=drain: each(drain))
+    post.finish()
+    for copy in kept:
+        copy.wait()
+
+
+def scatter_weights(head_sums, hidden_sums):
+    parts, count = len(head_sums), len(hidden_sums)
+    rows = head_sums[0].shape[0] // (2 * LINE * 4)
+    anywhere = pl.BlockSpec(memory_space=pl.ANY)
+    copies = 7 * count + 3 * parts
+    outs = [jax.ShapeDtypeStruct((4, rows, h.shape[1]), jnp.bfloat16) for h in head_sums]
+    outs += [
+        jax.ShapeDtypeStruct((rows, h.shape[0] * h.shape[2]), jnp.bfloat16) for h in hidden_sums
+    ]
+    found = pl.pallas_call(
+        functools.partial(scatter_kernel, parts, count),
+        out_shape=outs,
+        in_specs=[anywhere] * (parts + count),
+        out_specs=[anywhere] * (parts + count),
+        scratch_shapes=[
+            pltpu.VMEM((LINE, 4, rows, h.shape[1]), jnp.bfloat16) for _ in range(4) for h in head_sums
+        ]
+        + [
+            pltpu.SemaphoreType.DMA((copies,)),
+            pltpu.SemaphoreType.DMA((copies,)),
+            pltpu.SemaphoreType.DMA((parts, LINE, 4)),
+            pltpu.SemaphoreType.DMA((parts, 3, LINE, 4)),
+            pltpu.SemaphoreType.DMA((parts, 3, LINE, 4)),
+            pltpu.SemaphoreType.DMA((count + parts,)),
+        ],
+        compiler_params=pltpu.CompilerParams(
+            collective_id=1, has_side_effects=True, vmem_limit_bytes=40 << 20
+        ),
+    )(
+        *[h.reshape(2, LINE, 4, rows, h.shape[1]) for h in head_sums],
+        *hidden_sums,
+    )
+    return found[:parts], found[parts:]
+
+
+def scatter_gains(spot, gains):
+    count = gains.shape[0]
+    left = gains.reshape(count, 2, 2, 2, 2, 2, -1)
+    for bit, rule in (
+        (spot.y, to_row),
+        (spot.z // 2, lambda v: to_chip(v, 2, 0)),
+        (spot.z % 2, lambda v: to_chip(v, 1, 0)),
+        (spot.x, to_x),
+        (spot.c, to_core),
+    ):
+        left = pick(left, bit, 1) + rule(pick(left, 1 - bit, 1))
+    return left
 
 
 def split_columns(matrix, count):
@@ -565,7 +929,6 @@
 ):
     spot = Spot()
     count = tokens.shape[1]
-    local_rows = w_query.shape[0]
     group_size = HEADS // KV_HEADS
     query_width = HEADS * HEAD_DIM
     score_scale = HEAD_DIM ** (-0.5)
@@ -577,24 +940,25 @@
                 split_columns(dequant(w_query, bit_levels[0], D, qk_boost), KV_HEADS),
                 split_columns(dequant(w_key, bit_levels[1], D, qk_boost), KV_HEADS),
                 split_columns(dequant(w_value, bit_levels[2], D, 1.0), KV_HEADS),
+                split_columns(dequant(w_proj, bit_levels[3], query_width, 1.0), KV_HEADS),
             ],
             axis=2,
         )
     )
-    proj_in = low(split_columns(dequant(w_proj, bit_levels[3], query_width, 1.0), KV_HEADS))
     flat_tokens = wide(tokens).reshape(count, D)
     normed_low = low(rmsnorm(flat_tokens, gain_first))
-    normed_all = gather_group(normed_low)
-    heads_w = gather_heads(spot, heads_in)
-    proj_w = gather_heads(spot, proj_in)
-    chips = LINE * 2
-    gate_w = gather_hidden(
-        spot, low(split_columns(dequant(w_gate, bit_levels[4], D, 1.0), chips))
-    )
-    up_w = gather_hidden(spot, low(split_columns(dequant(w_up, bit_levels[5], D, 1.0), chips)))
-    down_w = gather_hidden(
-        spot, low(split_columns(dequant(w_down, bit_levels[6], FF, 1.0), chips))
-    )
+    all_heads, normed_all, (gate_w, up_w, down_w) = gather_weights(
+        heads_in,
+        normed_low,
+        [
+            low(dequant(w_gate, bit_levels[4], D, 1.0)),
+            low(dequant(w_up, bit_levels[5], D, 1.0)),
+            low(dequant(w_down, bit_levels[6], FF, 1.0)),
+        ],
+    )
+    head_width = (group_size + 2) * HEAD_DIM
+    heads_w = all_heads[:, :head_width]
+    proj_w = all_heads[:, head_width:]
 
     inner = jnp.arange(count, dtype=jnp.int32)
     offsets = jnp.concatenate(
@@ -685,9 +1049,9 @@
         )
     grad_mid = reduce_plane(back_chunks)
     mid_all = jnp.concatenate(mid_chunks, axis=0)
-    grad_gate = scatter_hidden(spot, low(outer_sum(mid_all, jnp.concatenate(gate_grads, axis=0))))
-    grad_up = scatter_hidden(spot, low(outer_sum(mid_all, jnp.concatenate(up_grads, axis=0))))
-    grad_down = scatter_hidden(
+    gate_sums = narrow_hidden(spot, low(outer_sum(mid_all, jnp.concatenate(gate_grads, axis=0))))
+    up_sums = narrow_hidden(spot, low(outer_sum(mid_all, jnp.concatenate(up_grads, axis=0))))
+    down_sums = narrow_hidden(
         spot,
         low(outer_sum(jnp.concatenate(grad_chunks, axis=0), jnp.concatenate(acts, axis=0))),
     )
@@ -696,7 +1060,8 @@
     grad_hidden = upstream + hidden_part
     grad_attn, second_part = jax.vjp(rmsnorm, attn_out, gain_second)[1](grad_hidden)
     grad_attn_all = gather_group(low(grad_attn))
-    proj_sums = scatter_heads(spot, low(outer_sum(grad_attn_all, mixed_low)))
+    proj_sums = low(outer_sum(grad_attn_all, mixed_low))
+    late_gains = scatter_gains(spot, jnp.stack([second_part, third_part, fourth_part]))
 
     grad_mixed = dot(grad_attn_all, proj_w).reshape(span, group_size, HEAD_DIM)
     grad_summed = low(grad_mixed / denominator)
@@ -731,28 +1096,28 @@
     ).reshape(span, wide_q)
     grad_key_pre = low(turn(sums[:, :HEAD_DIM], cosine, -sine))
     grad_pre = jnp.concatenate([grad_query_pre, grad_key_pre, low(sums[:, HEAD_DIM:])], axis=1)
-    head_sums = scatter_heads(spot, low(outer_sum(normed_all, grad_pre)))
+    (head_rows, proj_rows), (grad_gate, grad_up, grad_down) = scatter_weights(
+        [low(outer_sum(normed_all, grad_pre)), proj_sums], [gate_sums, up_sums, down_sums]
+    )
     grad_in = reduce_group(low(dot_rows(grad_pre, heads_w)).reshape(2, 2, count, D))
     tokens_part, first_part = jax.vjp(rmsnorm, flat_tokens, gain_first)[1](grad_in)
     grad_tokens = (grad_hidden + tokens_part).reshape(1, count, D)
 
-    gain_terms = lax.psum(jnp.stack([first_part, second_part, third_part, fourth_part]), AXES)
-    mine = (spot.y * (LINE * 4) + lax.axis_index("seq")) * local_rows
-    gains = lax.dynamic_slice_in_dim(gain_terms, mine, local_rows, 1)
+    first_gain = scatter_gains(spot, first_part[None])
     return (
         layer_out,
         grad_tokens,
-        join_columns(head_sums[:, :, :wide_q]),
-        join_columns(head_sums[:, :, wide_q : wide_q + HEAD_DIM]),
-        join_columns(head_sums[:, :, wide_q + HEAD_DIM :]),
-        join_columns(proj_sums),
-        grad_gate,
-        grad_up,
-        grad_down,
-        gains[0],
-        gains[1],
-        gains[2],
-        gains[3],
+        join_columns(head_rows[:, :, :wide_q]),
+        join_columns(head_rows[:, :, wide_q : wide_q + HEAD_DIM]),
+        join_columns(head_rows[:, :, wide_q + HEAD_DIM :]),
+        join_columns(proj_rows),
+        wide(grad_gate),
+        wide(grad_up),
+        wide(grad_down),
+        first_gain[0],
+        late_gains[0],
+        late_gains[1],
+        late_gains[2],
     )
 
 

time: 1120 us -> 922 us (0.82)
  Pallas kernels: 0 us -> 318 us
  waiting for transfers between devices: 508 us -> 261 us
  starting transfers between devices: 227 us -> 69.1 us
  local copies, waits for them, and re-layouts: 132 us -> 43.1 us
  blocking collectives: 43.2 us -> 0 us
  matrix products: 127 us -> 149 us
    pallas_call x0 -> x2, Pallas kernels: none -> 318 us  [the longest x1 177 us: gather_weights(): pl.pallas_call(functools.partial(gather_kernel, count), out_shape=outs, i...]
    ppermute x161 -> x65, waiting for transfers between devices: 508 us -> 261 us  [send(): return lax.ppermute(value, AXES, moves(2 * LINE * 4, rule))]
    ppermute x161 -> x65, starting transfers between devices: 227 us -> 69.1 us  [send(): return lax.ppermute(value, AXES, moves(2 * LINE * 4, rule))]
    psum x1 -> x0, blocking collectives: 43.2 us -> none  [per_device_line(): lax.psum(jnp.stack([first_part, second_part, third_part, fourth_part]), A...]
    dynamic_update_slice x86 -> x0, local copies, waits for them, and re-layouts: 32.7 us -> none  [place(): return lax.dynamic_update_slice(array, piece, starts)]
    unnamed x417 -> x357, local copies, waits for them, and re-layouts: 38.8 us -> 16.5 us
    another operation x19 -> x6, local copies, waits for them, and re-layouts: 19.8 us -> 4.64 us  [the longest x3 3.01 us: per_device_line(): jnp.stack([second_part, third_part, fourth_part])]
    dot_general x14, matrix products: 38.7 us -> 53.6 us  [dot(): return jnp.dot(left_side, right_side, preferred_element_type=jnp.float32)]
  transfers between devices with their start and end apart: 161 -> 65, of which waited for: 74 -> 35; matrix products, arithmetic and copies ran while one was open for 26% -> 21% of each run, Pallas kernels for 0% -> 16%
where the time goes in v2:
time: 922 us; the launch traced here: 908 us
  Pallas kernels  318 us (34%)
  waiting for transfers between devices  261 us (28%)
  matrix products  149 us (16%)
  starting transfers between devices  69.1 us (7%)
  other arithmetic  54.6 us (6%)
  local copies, waits for them, and re-layouts  43.1 us (5%)
  between operations  13.4 us (1%)
    ppermute x65, waiting for transfers between devices, send(): return lax.ppermute(value, AXES, moves(2 * LINE * 4, rule))  261 us
    pallas_call x1, Pallas kernels, gather_weights(): pl.pallas_call(functools.partial(gather_kernel, count), out_shape=outs, i...  177 us
    pallas_call x1, Pallas kernels, scatter_weights(): pl.pallas_call(functools.partial(scatter_kernel, parts, count), out_shape...  141 us
    ppermute x65, starting transfers between devices, send(): return lax.ppermute(value, AXES, moves(2 * LINE * 4, rule))  69.1 us
    dot_general x14, matrix products, dot(): return jnp.dot(left_side, right_side, preferred_element_type=jnp.float32)  53.6 us
    dot_general x14, matrix products, dot_rows(): jnp.einsum('tf,df->td', left_side, right_side, preferred_element_type=jnp...  34.8 us
    dot_general x5, matrix products, outer_sum(): jnp.einsum('td,tf->df', left_side, right_side, preferred_element_type=jnp...  33.7 us
  transfers between devices with their start and end apart: 65, of which 35 were waited for; matrix products, arithmetic and copies ran while one was open for 21% of the time, Pallas kernels for 16%

profile of v2, /device:TPU:20, one launch (start us, length us, event | category | flops | bytes accessed | tf_op | source)
XLA Modules:
  0.0 908.4 jit_solution(10456253682975193473)
XLA Ops:
  25.8 176.7 %shard_map.246 = (bf16[2,4,4,72,1536]{4,3,2,1,0:T(8,128)(2,1)}, bf16[4,128,2304]{2,1,0:T(8,128)(2,1)}, bf16[2,8,2,72,1152]{4,3,2,1,0:T(8,128)(2,1)}, bf16[2,8,2,...) custom-call(bf16[4,72,1536]{2,1,0:T(8,128)(2,1)} %pad_maximum_fusion.5.refs_0_, bf16[128,2304]{1,0:T(8,128)(2,1)} %fusion.69.refs_1_, ...), custom_call_target="tpu_custom_call" | custom-call | tf_op jit(solution)/shard_map/pallas_call | solution.py:652
  219.3 7.9 collective-permute-done
  233.1 9.8 %collective-permute-done.1 = bf16[512,512]{1,0:T(8,128)(2,1)S(1)} collective-permute-done((bf16[512,512]{1,0:T(8,128)(2,1)}, bf16[512,512]{1,0:T(8,128)(2,1)S(1)}, u32[]{:S(2)}, u32[]{:S(2)}) %collective-permute-start.1) | collective-permute-done | bytes 524320 | tf_op jit(solution)/shard_map/ppermute | solution.py:325
  247.7 9.9 %collective-permute-done.2 = bf16[512,512]{1,0:T(8,128)(2,1)S(1)} collective-permute-done((bf16[512,512]{1,0:T(8,128)(2,1)S(1)}, bf16[512,512]{1,0:T(8,128)(2,1)S(1)}, u32[]{:S(2)}, u32[]{:S(2)}) %collective-permute-start.2) | collective-permute-done | bytes 524320 | tf_op jit(solution)/shard_map/ppermute | solution.py:325
  267.6 14.8 %collective-permute-done.4 = bf16[128,2304]{1,0:T(8,128)(2,1)S(1)} collective-permute-done((bf16[128,2304]{1,0:T(8,128)(2,1)S(1)}, bf16[128,2304]{1,0:T(8,128)(2,1)S(1)}, u32[]{:S(2)}, u32[]{:S(2)}) %collective-permute-start.4) | collective-permute-done | bytes 589856 | tf_op jit(solution)/shard_map/ppermute | solution.py:325
  288.1 11.7 %collective-permute-done.5 = bf16[128,2304]{1,0:T(8,128)(2,1)} collective-permute-done((bf16[128,2304]{1,0:T(8,128)(2,1)}, bf16[128,2304]{1,0:T(8,128)(2,1)}, u32[]{:S(2)}, u32[]{:S(2)}) %collective-permute-start.5) | collective-permute-done | bytes 589856 | tf_op jit(solution)/shard_map/ppermute | solution.py:325
  320.8 18.0 %collective-permute-done.14 = bf16[128,2304]{1,0:T(8,128)(2,1)S(1)} collective-permute-done((bf16[128,2304]{1,0:T(8,128)(2,1)S(1)}, bf16[128,2304]{1,0:T(8,128)(2,1)S(1)}, u32[]{:S(2)}, u32[]{:S(2)}) %collective-permute-start.14) | collective-permute-done | bytes 589856 | tf_op jit(solution)/shard_map/ppermute | solution.py:325
  362.0 10.7 %collective-permute-done.18 = bf16[128,2304]{1,0:T(8,128)(2,1)S(1)} collective-permute-done((bf16[128,2304]{1,0:T(8,128)(2,1)S(1)}, bf16[128,2304]{1,0:T(8,128)(2,1)S(1)}, u32[]{:S(2)}, u32[]{:S(2)}) %collective-permute-start.18) | collective-permute-done | bytes 589856 | tf_op jit(solution)/shard_map/ppermute | solution.py:325
  385.7 12.3 %collective-permute-done.19 = bf16[128,2304]{1,0:T(8,128)(2,1)S(1)} collective-permute-done((bf16[128,2304]{1,0:T(8,128)(2,1)S(1)}, bf16[128,2304]{1,0:T(8,128)(2,1)S(1)}, u32[]{:S(2)}, u32[]{:S(2)}) %collective-permute-start.19) | collective-permute-done | bytes 589856 | tf_op jit(solution)/shard_map/ppermute | solution.py:325
  399.4 6.4 collective-permute-done.10
  415.9 6.6 collective-permute-done.11
  428.2 10.2 %collective-permute-done.12 = bf16[128,2304]{1,0:T(8,128)(2,1)S(1)} collective-permute-done((bf16[128,2304]{1,0:T(8,128)(2,1)S(1)}, bf16[128,2304]{1,0:T(8,128)(2,1)S(1)}, u32[]{:S(2)}, u32[]{:S(2)}) %collective-permute-start.12) | collective-permute-done | bytes 589856 | tf_op jit(solution)/shard_map/ppermute | solution.py:325
  449.3 6.2 collective-permute-done.23
  478.2 16.7 %collective-permute-done.32 = bf16[128,2304]{1,0:T(8,128)(2,1)S(1)} collective-permute-done((bf16[128,2304]{1,0:T(8,128)(2,1)}, bf16[128,2304]{1,0:T(8,128)(2,1)S(1)}, u32[]{:S(2)}, u32[]{:S(2)}) %collective-permute-start.32) | collective-permute-done | bytes 589856 | tf_op jit(solution)/shard_map/ppermute | solution.py:325
  525.4 11.8 %collective-permute-done.36 = bf16[128,2304]{1,0:T(8,128)(2,1)S(1)} collective-permute-done((bf16[128,2304]{1,0:T(8,128)(2,1)S(1)}, bf16[128,2304]{1,0:T(8,128)(2,1)S(1)}, u32[]{:S(2)}, u32[]{:S(2)}) %collective-permute-start.36) | collective-permute-done | bytes 589856 | tf_op jit(solution)/shard_map/ppermute | solution.py:325
  546.5 9.5 %convolution_convert_fusion.1 = bf16[2304,1152]{1,0:T(8,128)(2,1)} fusion(bf16[1024,2304]{1,0:T(8,128)(2,1)S(1)} %bitcast.509, bf16[256,1152]{1,0:T(8,128)(2,1)} %copy-done.123, bf16[256,1152]{1,0:T(8,128)(2,1)} %copy-done.122, bf16[256,1152]{1,0:T(8,128)(2,1)S(1)} %get-tuple-element.64, bf16[256,1152]{1,0:T(8,128)(2,1)S(1)} %get-tuple-element.60), kind=kOutput, calls=%fused_computation.1 | convolution fusion | flops 5447909376 | bytes 12386304 | tf_op jit(solution)/shard_map/td,tf->df/dot_general | solution.py:910
  556.0 8.1 convolution_convert_fusion.2
  567.1 13.3 %collective-permute-done.38 = bf16[128,2304]{1,0:T(8,128)(2,1)S(1)} collective-permute-done((bf16[128,2304]{1,0:T(8,128)(2,1)S(1)}, bf16[128,2304]{1,0:T(8,128)(2,1)S(1)}, u32[]{:S(2)}, u32[]{:S(2)}) %collective-permute-start.38) | collective-permute-done | bytes 589856 | tf_op jit(solution)/shard_map/ppermute | solution.py:325
  582.7 7.2 collective-permute-done.29
  596.1 8.5 convolution_convert_fusion
  672.9 11.3 %collective-permute-done.44 = bf16[512,512]{1,0:T(8,128)(2,1)S(1)} collective-permute-done((bf16[512,512]{1,0:T(8,128)(2,1)S(1)}, bf16[512,512]{1,0:T(8,128)(2,1)S(1)}, u32[]{:S(2)}, u32[]{:S(2)}) %collective-permute-start.44) | collective-permute-done | bytes 524320 | tf_op jit(solution)/shard_map/ppermute | solution.py:325
  687.6 12.0 %collective-permute-done.45 = bf16[512,512]{1,0:T(8,128)(2,1)S(1)} collective-permute-done((bf16[512,512]{1,0:T(8,128)(2,1)S(1)}, bf16[512,512]{1,0:T(8,128)(2,1)S(1)}, u32[]{:S(2)}, u32[]{:S(2)}) %collective-permute-start.45) | collective-permute-done | bytes 524320 | tf_op jit(solution)/shard_map/ppermute | solution.py:325
  702.9 11.2 %collective-permute-done.46 = bf16[512,512]{1,0:T(8,128)(2,1)S(1)} collective-permute-done((bf16[512,512]{1,0:T(8,128)(2,1)S(1)}, bf16[512,512]{1,0:T(8,128)(2,1)S(1)}, u32[]{:S(2)}, u32[]{:S(2)}) %collective-permute-start.46) | collective-permute-done | bytes 524320 | tf_op jit(solution)/shard_map/ppermute | solution.py:325
  739.3 141.3 %shard_map.247 = (bf16[4,72,1024]{2,1,0:T(8,128)(2,1)S(1)}, bf16[4,72,512]{2,1,0:T(8,128)(2,1)S(1)}, bf16[72,9216]{1,0:T(8,128)(2,1)S(1)}, bf16[72,9216]{1,0:T(8,128)(2,1)S(1)}, bf16[72,9216]{1,0:T(8,128)(2,1)S(1)}) custom-call(bf16[2,4,4,72,1024]{4,3,2,1,0:T(8,128)(2,1)} %bitcast.490, bf16[2,4,4,72,512]{4,3,2,1,0:T(8,128)(2,1)S(1)} %bitcast.477, ...), custom_call_target="tpu_custom_call" | custom-call | tf_op jit(solution)/shard_map/pallas_call | solution.py:842
  (682 shorter events, 343.0 us)
Async XLA Ops:
  285.4 27.6 %collective-permute-start.13 = (bf16[128,2304]{1,0:T(8,128)(2,1)}, bf16[128,2304]{1,0:T(8,128)(2,1)S(1)}, u32[]{:S(2)}, u32[]{:S(2)}) collective-permute-start(bf16[128,2304]{1,0:T(8,128)(2,1)} %get-tuple-element.52), channel_id=1, source_target_pairs={{0,4},{1,5},{2,6},{3,7},{4,0},{5,1},{6,2},{7,3},{8,12},{9,13},{10,... | collective-permute-start | bytes 1769480 | tf_op jit(solution)/shard_map/ppermute | solution.py:325
  286.1 30.4 %collective-permute-start.7 = (bf16[128,2304]{1,0:T(8,128)(2,1)}, bf16[128,2304]{1,0:T(8,128)(2,1)S(1)}, u32[]{:S(2)}, u32[]{:S(2)}) collective-permute-start(bf16[128,2304]{1,0:T(8,128)(2,1)} %get-tuple-element.52), channel_id=1, source_target_pairs={{4,8},{5,9},{6,10},{7,11},{8,4},{9,5},{10,6},{11,7},{20,24},{21,25... | collective-permute-start | bytes 1769480 | tf_op jit(solution)/shard_map/ppermute | solution.py:325
  312.4 115.8 %collective-permute-start.6 = (bf16[128,2304]{1,0:T(8,128)(2,1)S(1)}, bf16[128,2304]{1,0:T(8,128)(2,1)S(1)}, u32[]{:S(2)}, u32[]{:S(2)}) collective-permute-start(bf16[128,2304]{1,0:T(8,128)(2,1)S(1)} %slice.269), channel_id=1, source_target_pairs={{0,2},{1,3},{2,0},{3,1},{4,6},{5,7},{6,4},{7,5},{8,10},{9,11},{10,... | collective-permute-start | bytes 1769480 | tf_op jit(solution)/shard_map/ppermute | solution.py:325
  313.0 29.9 %collective-permute-start.16 = (bf16[128,2304]{1,0:T(8,128)(2,1)S(1)}, bf16[128,2304]{1,0:T(8,128)(2,1)S(1)}, u32[]{:S(2)}, u32[]{:S(2)}) collective-permute-start(bf16[128,2304]{1,0:T(8,128)(2,1)S(1)} %collective-permute-done.13), channel_id=1, source_target_pairs={{4,8},{5,9},{6,10},{7,11},{8,4},{9,5},{10,6},{11,7},{20,24},{21,25... | collective-permute-start | bytes 1769480 | tf_op jit(solution)/shard_map/ppermute | solution.py:325
  315.0 23.8 %collective-permute-start.14 = (bf16[128,2304]{1,0:T(8,128)(2,1)S(1)}, bf16[128,2304]{1,0:T(8,128)(2,1)S(1)}, u32[]{:S(2)}, u32[]{:S(2)}) collective-permute-start(bf16[128,2304]{1,0:T(8,128)(2,1)S(1)} %collective-permute-done.13), channel_id=1, source_target_pairs={{0,2},{1,3},{2,0},{3,1},{4,6},{5,7},{6,4},{7,5},{8,10},{9,11},{10,... | collective-permute-start | bytes 1769480 | tf_op jit(solution)/shard_map/ppermute | solution.py:325
  316.5 23.1 %collective-permute-start.8 = (bf16[128,2304]{1,0:T(8,128)(2,1)S(1)}, bf16[128,2304]{1,0:T(8,128)(2,1)S(1)}, u32[]{:S(2)}, u32[]{:S(2)}) collective-permute-start(bf16[128,2304]{1,0:T(8,128)(2,1)S(1)} %collective-permute-done.7), channel_id=1, source_target_pairs={{4,0},{5,1},{6,2},{7,3},{8,12},{9,13},{10,14},{11,15},{20,16},{21,... | collective-permute-start | bytes 1769480 | tf_op jit(solution)/shard_map/ppermute | solution.py:325
  359.7 65.0 %collective-permute-start.15 = (bf16[128,2304]{1,0:T(8,128)(2,1)S(1)}, bf16[128,2304]{1,0:T(8,128)(2,1)S(1)}, u32[]{:S(2)}, u32[]{:S(2)}) collective-permute-start(bf16[128,2304]{1,0:T(8,128)(2,1)S(1)} %slice.273), channel_id=1, source_target_pairs={{0,2},{1,3},{2,0},{3,1},{4,6},{5,7},{6,4},{7,5},{8,10},{9,11},{10,... | collective-permute-start | bytes 1769480 | tf_op jit(solution)/shard_map/ppermute | solution.py:325
  379.0 19.0 %collective-permute-start.19 = (bf16[128,2304]{1,0:T(8,128)(2,1)S(1)}, bf16[128,2304]{1,0:T(8,128)(2,1)S(1)}, u32[]{:S(2)}, u32[]{:S(2)}) collective-permute-start(bf16[128,2304]{1,0:T(8,128)(2,1)S(1)} %slice.275), channel_id=1, source_target_pairs={{0,2},{1,3},{2,0},{3,1},{4,6},{5,7},{6,4},{7,5},{8,10},{9,11},{10,... | collective-permute-start | bytes 1769480 | tf_op jit(solution)/shard_map/ppermute | solution.py:325
  385.0 20.8 %collective-permute-start.10 = (bf16[128,2304]{1,0:T(8,128)(2,1)S(1)}, bf16[128,2304]{1,0:T(8,128)(2,1)S(1)}, u32[]{:S(2)}, u32[]{:S(2)}) collective-permute-start(bf16[128,2304]{1,0:T(8,128)(2,1)S(1)} %slice.271), channel_id=1, source_target_pairs={{0,2},{1,3},{2,0},{3,1},{4,6},{5,7},{6,4},{7,5},{8,10},{9,11},{10,... | collective-permute-start | bytes 1769480 | tf_op jit(solution)/shard_map/ppermute | solution.py:325
  445.8 25.9 %collective-permute-start.31 = (bf16[128,2304]{1,0:T(8,128)(2,1)}, bf16[128,2304]{1,0:T(8,128)(2,1)}, u32[]{:S(2)}, u32[]{:S(2)}) collective-permute-start(bf16[128,2304]{1,0:T(8,128)(2,1)} %get-tuple-element.46), channel_id=1, source_target_pairs={{0,4},{1,5},{2,6},{3,7},{4,0},{5,1},{6,2},{7,3},{8,12},{9,13},{10,... | collective-permute-start | bytes 1769480 | tf_op jit(solution)/shard_map/ppermute | solution.py:325
  445.8 28.5 %collective-permute-start.25 = (bf16[128,2304]{1,0:T(8,128)(2,1)}, bf16[128,2304]{1,0:T(8,128)(2,1)}, u32[]{:S(2)}, u32[]{:S(2)}) collective-permute-start(bf16[128,2304]{1,0:T(8,128)(2,1)} %get-tuple-element.46), channel_id=1, source_target_pairs={{4,8},{5,9},{6,10},{7,11},{8,4},{9,5},{10,6},{11,7},{20,24},{21,25... | collective-permute-start | bytes 1769480 | tf_op jit(solution)/shard_map/ppermute | solution.py:325
  470.2 134.5 %collective-permute-start.24 = (bf16[128,2304]{1,0:T(8,128)(2,1)S(1)}, bf16[128,2304]{1,0:T(8,128)(2,1)S(1)}, u32[]{:S(2)}, u32[]{:S(2)}) collective-permute-start(bf16[128,2304]{1,0:T(8,128)(2,1)S(1)} %slice.277), channel_id=1, source_target_pairs={{0,2},{1,3},{2,0},{3,1},{4,6},{5,7},{6,4},{7,5},{8,10},{9,11},{10,... | collective-permute-start | bytes 1769480 | tf_op jit(solution)/shard_map/ppermute | solution.py:325
  471.7 33.1 %collective-permute-start.34 = (bf16[128,2304]{1,0:T(8,128)(2,1)}, bf16[128,2304]{1,0:T(8,128)(2,1)S(1)}, u32[]{:S(2)}, u32[]{:S(2)}) collective-permute-start(bf16[128,2304]{1,0:T(8,128)(2,1)} %collective-permute-done.31), channel_id=1, source_target_pairs={{4,8},{5,9},{6,10},{7,11},{8,4},{9,5},{10,6},{11,7},{20,24},{21,25... | collective-permute-start | bytes 1769480 | tf_op jit(solution)/shard_map/ppermute | solution.py:325
  473.6 21.3 %collective-permute-start.32 = (bf16[128,2304]{1,0:T(8,128)(2,1)}, bf16[128,2304]{1,0:T(8,128)(2,1)S(1)}, u32[]{:S(2)}, u32[]{:S(2)}) collective-permute-start(bf16[128,2304]{1,0:T(8,128)(2,1)} %collective-permute-done.31), channel_id=1, source_target_pairs={{0,2},{1,3},{2,0},{3,1},{4,6},{5,7},{6,4},{7,5},{8,10},{9,11},{10,... | collective-permute-start | bytes 1769480 | tf_op jit(solution)/shard_map/ppermute | solution.py:325
  474.3 20.7 %collective-permute-start.26 = (bf16[128,2304]{1,0:T(8,128)(2,1)}, bf16[128,2304]{1,0:T(8,128)(2,1)S(1)}, u32[]{:S(2)}, u32[]{:S(2)}) collective-permute-start(bf16[128,2304]{1,0:T(8,128)(2,1)} %collective-permute-done.25), channel_id=1, source_target_pairs={{4,0},{5,1},{6,2},{7,3},{8,12},{9,13},{10,14},{11,15},{20,16},{21,... | collective-permute-start | bytes 1769480 | tf_op jit(solution)/shard_map/ppermute | solution.py:325
  508.2 83.8 %collective-permute-start.33 = (bf16[128,2304]{1,0:T(8,128)(2,1)S(1)}, bf16[128,2304]{1,0:T(8,128)(2,1)S(1)}, u32[]{:S(2)}, u32[]{:S(2)}) collective-permute-start(bf16[128,2304]{1,0:T(8,128)(2,1)S(1)} %slice.281), channel_id=1, source_target_pairs={{0,2},{1,3},{2,0},{3,1},{4,6},{5,7},{6,4},{7,5},{8,10},{9,11},{10,... | collective-permute-start | bytes 1769480 | tf_op jit(solution)/shard_map/ppermute | solution.py:325
  514.6 22.6 %collective-permute-start.36 = (bf16[128,2304]{1,0:T(8,128)(2,1)S(1)}, bf16[128,2304]{1,0:T(8,128)(2,1)S(1)}, u32[]{:S(2)}, u32[]{:S(2)}) collective-permute-start(bf16[128,2304]{1,0:T(8,128)(2,1)S(1)} %get-tuple-element.42), channel_id=1, source_target_pairs={{0,2},{1,3},{2,0},{3,1},{4,6},{5,7},{6,4},{7,5},{8,10},{9,11},{10,... | collective-permute-start | bytes 1769480 | tf_op jit(solution)/shard_map/ppermute | solution.py:325
  523.8 41.8 %collective-permute-start.28 = (bf16[128,2304]{1,0:T(8,128)(2,1)S(1)}, bf16[128,2304]{1,0:T(8,128)(2,1)S(1)}, u32[]{:S(2)}, u32[]{:S(2)}) collective-permute-start(bf16[128,2304]{1,0:T(8,128)(2,1)S(1)} %slice.279), channel_id=1, source_target_pairs={{0,2},{1,3},{2,0},{3,1},{4,6},{5,7},{6,4},{7,5},{8,10},{9,11},{10,... | collective-permute-start | bytes 1769480 | tf_op jit(solution)/shard_map/ppermute | solution.py:325
  565.8 24.1 %collective-permute-start.29 = (bf16[128,2304]{1,0:T(8,128)(2,1)S(1)}, bf16[128,2304]{1,0:T(8,128)(2,1)S(1)}, u32[]{:S(2)}, u32[]{:S(2)}) collective-permute-start(bf16[128,2304]{1,0:T(8,128)(2,1)S(1)} %fusion.127), channel_id=1, source_target_pairs={{0,4},{1,5},{2,6},{3,7},{12,8},{13,9},{14,10},{15,11},{16,20},{17,... | collective-permute-start | bytes 1769480 | tf_op jit(solution)/shard_map/ppermute | solution.py:325
  624.0 20.4 %collective-permute-start.51 = (bf16[2,8,72,1152]{3,2,1,0:T(8,128)(2,1)S(1)}, bf16[2,8,72,1152]{3,2,1,0:T(8,128)(2,1)S(1)}, u32[]{:S(2)}, u32[]{:S(2)}) collective-permute-start(bf16[2,8,72,1152]{3,2,1,0:T(8,128)(2,1)S(1)} %dynamic-slice_bitcast_fusion.1), channel_id=1, source_target_pairs={{0,1},{1,0},{2,3},{3,2},{4,5},{5,4},{6,7},{7,6},{8,9},{9,8},{10,11... | collective-permute-start | bytes 7962632 | tf_op jit(solution)/shard_map/ppermute | solution.py:325
  635.3 90.0 %collective-permute-start.54 = (bf16[8,72,1152]{2,1,0:T(8,128)(2,1)}, bf16[8,72,1152]{2,1,0:T(8,128)(2,1)}, u32[]{:S(2)}, u32[]{:S(2)}) collective-permute-start(bf16[8,72,1152]{2,1,0:T(8,128)(2,1)} %dynamic-slice_bitcast_fusion.3), channel_id=1, source_target_pairs={{0,16},{1,17},{2,18},{3,19},{4,20},{5,21},{6,22},{7,23},{8,24},{9,... | collective-permute-start | bytes 3981320 | tf_op jit(solution)/shard_map/ppermute | solution.py:325
  638.7 88.4 %collective-permute-start.50 = (bf16[8,72,1152]{2,1,0:T(8,128)(2,1)}, bf16[8,72,1152]{2,1,0:T(8,128)(2,1)}, u32[]{:S(2)}, u32[]{:S(2)}) collective-permute-start(bf16[8,72,1152]{2,1,0:T(8,128)(2,1)} %dynamic-slice_bitcast_fusion.5), channel_id=1, source_target_pairs={{0,16},{1,17},{2,18},{3,19},{4,20},{5,21},{6,22},{7,23},{8,24},{9,... | collective-permute-start | bytes 3981320 | tf_op jit(solution)/shard_map/ppermute | solution.py:325
  646.3 83.6 %collective-permute-start.52 = (bf16[8,72,1152]{2,1,0:T(8,128)(2,1)}, bf16[8,72,1152]{2,1,0:T(8,128)(2,1)}, u32[]{:S(2)}, u32[]{:S(2)}) collective-permute-start(bf16[8,72,1152]{2,1,0:T(8,128)(2,1)} %dynamic-slice_bitcast_fusion.4), channel_id=1, source_target_pairs={{0,16},{1,17},{2,18},{3,19},{4,20},{5,21},{6,22},{7,23},{8,24},{9,... | collective-permute-start | bytes 3981320 | tf_op jit(solution)/shard_map/ppermute | solution.py:325
  729.5 152.2 %collective-permute-start.48 = (bf16[128,2304]{1,0:T(8,128)(2,1)S(1)}, bf16[128,2304]{1,0:T(8,128)(2,1)S(1)}, u32[]{:S(2)}, u32[]{:S(2)}) collective-permute-start(bf16[128,2304]{1,0:T(8,128)(2,1)S(1)} %fusion.139), channel_id=1, source_target_pairs={{0,2},{1,3},{2,0},{3,1},{4,6},{5,7},{6,4},{7,5},{8,10},{9,11},{10,... | collective-permute-start | bytes 1769480 | tf_op jit(solution)/shard_map/ppermute | solution.py:325
  (216 other events, 2467.7 us)

commit v3 on v2

--- a/solution.py
+++ b/solution.py
@@ -439,6 +439,10 @@
 def reduce_plane(chunks):
     parts = [None] * LINE
     for slot in (3, 2, 1, 0):
+        if slot == 1:
+            parts[3], chunks[1], chunks[0] = lax.optimization_barrier(
+                (parts[3], chunks[1], chunks[0])
+            )
         parts[slot] = wide(chunks[slot][0]) + wide(to_x(chunks[slot][1]))
     return reduce_line(parts)
 
@@ -865,20 +869,6 @@
     return found[:parts], found[parts:]
 
 
-def scatter_gains(spot, gains):
-    count = gains.shape[0]
-    left = gains.reshape(count, 2, 2, 2, 2, 2, -1)
-    for bit, rule in (
-        (spot.y, to_row),
-        (spot.z // 2, lambda v: to_chip(v, 2, 0)),
-        (spot.z % 2, lambda v: to_chip(v, 1, 0)),
-        (spot.x, to_x),
-        (spot.c, to_core),
-    ):
-        left = pick(left, bit, 1) + rule(pick(left, 1 - bit, 1))
-    return left
-
-
 def split_columns(matrix, count):
     rows, cols = matrix.shape
     return matrix.reshape(rows, count, cols // count).transpose(1, 0, 2)
@@ -1029,7 +1019,7 @@
         gates.append((gate_pre, up_pre))
         acts.append(activated)
         ffn_chunks.append(low(dot_rows(activated, down_w)).reshape(2, count, D))
-    ffn_out = reduce_plane(ffn_chunks)
+    ffn_out = reduce_plane(lax.optimization_barrier(ffn_chunks))
     result = hidden_one + rmsnorm(ffn_out, gain_fourth)
     layer_out = low(result).reshape(1, count, D)
 
@@ -1047,6 +1037,9 @@
                 2, count, D
             )
         )
+    back_chunks, mid_chunks, gate_grads, up_grads, grad_chunks, acts = lax.optimization_barrier(
+        (back_chunks, mid_chunks, gate_grads, up_grads, grad_chunks, acts)
+    )
     grad_mid = reduce_plane(back_chunks)
     mid_all = jnp.concatenate(mid_chunks, axis=0)
     gate_sums = narrow_hidden(spot, low(outer_sum(mid_all, jnp.concatenate(gate_grads, axis=0))))
@@ -1061,7 +1054,6 @@
     grad_attn, second_part = jax.vjp(rmsnorm, attn_out, gain_second)[1](grad_hidden)
     grad_attn_all = gather_group(low(grad_attn))
     proj_sums = low(outer_sum(grad_attn_all, mixed_low))
-    late_gains = scatter_gains(spot, jnp.stack([second_part, third_part, fourth_part]))
 
     grad_mixed = dot(grad_attn_all, proj_w).reshape(span, group_size, HEAD_DIM)
     grad_summed = low(grad_mixed / denominator)
@@ -1096,28 +1088,35 @@
     ).reshape(span, wide_q)
     grad_key_pre = low(turn(sums[:, :HEAD_DIM], cosine, -sine))
     grad_pre = jnp.concatenate([grad_query_pre, grad_key_pre, low(sums[:, HEAD_DIM:])], axis=1)
+    grad_shares = dot_rows(grad_pre, heads_w)
+    first_part = jnp.sum(wide(normed_all) * grad_shares, axis=0) / (1.0 + gain_first)
+    gain_sums = jnp.stack([first_part, second_part, third_part, fourth_part], axis=1)
+    gain_sums = low(jnp.pad(gain_sums, ((0, 0), (0, 124))))
     (head_rows, proj_rows), (grad_gate, grad_up, grad_down) = scatter_weights(
-        [low(outer_sum(normed_all, grad_pre)), proj_sums], [gate_sums, up_sums, down_sums]
-    )
-    grad_in = reduce_group(low(dot_rows(grad_pre, heads_w)).reshape(2, 2, count, D))
-    tokens_part, first_part = jax.vjp(rmsnorm, flat_tokens, gain_first)[1](grad_in)
+        [
+            low(outer_sum(normed_all, grad_pre)),
+            jnp.concatenate([proj_sums, gain_sums], axis=1),
+        ],
+        [gate_sums, up_sums, down_sums],
+    )
+    grad_in = reduce_group(low(grad_shares).reshape(2, 2, count, D))
+    tokens_part = jax.vjp(lambda v: rmsnorm(v, gain_first), flat_tokens)[1](grad_in)[0]
     grad_tokens = (grad_hidden + tokens_part).reshape(1, count, D)
-
-    first_gain = scatter_gains(spot, first_part[None])
+    gains = jnp.sum(wide(proj_rows[:, :, wide_q:]), axis=0)
     return (
         layer_out,
         grad_tokens,
         join_columns(head_rows[:, :, :wide_q]),
         join_columns(head_rows[:, :, wide_q : wide_q + HEAD_DIM]),
         join_columns(head_rows[:, :, wide_q + HEAD_DIM :]),
-        join_columns(proj_rows),
+        join_columns(proj_rows[:, :, :wide_q]),
         wide(grad_gate),
         wide(grad_up),
         wide(grad_down),
-        first_gain[0],
-        late_gains[0],
-        late_gains[1],
-        late_gains[2],
+        gains[:, 0],
+        gains[:, 1],
+        gains[:, 2],
+        gains[:, 3],
     )
 
 

time: 922 us -> 878 us (0.952)
  waiting for transfers between devices: 261 us -> 210 us
    ppermute x65 -> x55, waiting for transfers between devices: 261 us -> 210 us  [send(): return lax.ppermute(value, AXES, moves(2 * LINE * 4, rule))]
    convert_element_type x23 -> x25, other arithmetic: 14.8 us -> 26.3 us  [low(): return value.astype(jnp.bfloat16)]
    dot_general x14, matrix products: 53.6 us -> 42.8 us  [dot(): return jnp.dot(left_side, right_side, preferred_element_type=jnp.float32)]
    ppermute x65 -> x55, starting transfers between devices: 69.1 us -> 75.8 us  [send(): return lax.ppermute(value, AXES, moves(2 * LINE * 4, rule))]
  transfers between devices with their start and end apart: 65 -> 55, of which waited for: 35 -> 30; matrix products, arithmetic and copies ran while one was open for 21% -> 20% of each run, Pallas kernels for 16% -> 17%
where the time goes in v3:
time: 878 us; the launch traced here: 866 us
  Pallas kernels  325 us (37%)
  waiting for transfers between devices  210 us (24%)
  matrix products  146 us (17%)
  starting transfers between devices  75.8 us (9%)
  other arithmetic  61.6 us (7%)
  local copies, waits for them, and re-layouts  34.8 us (4%)
  between operations  12.9 us (1%)
    ppermute x55, waiting for transfers between devices, send(): return lax.ppermute(value, AXES, moves(2 * LINE * 4, rule))  210 us
    pallas_call x1, Pallas kernels, gather_weights(): pl.pallas_call(functools.partial(gather_kernel, count), out_shape=outs, i...  177 us
    pallas_call x1, Pallas kernels, scatter_weights(): pl.pallas_call(functools.partial(scatter_kernel, parts, count), out_shape...  148 us
    ppermute x55, starting transfers between devices, send(): return lax.ppermute(value, AXES, moves(2 * LINE * 4, rule))  75.8 us
    dot_general x14, matrix products, dot(): return jnp.dot(left_side, right_side, preferred_element_type=jnp.float32)  42.8 us
    dot_general x14, matrix products, dot_rows(): jnp.einsum('tf,df->td', left_side, right_side, preferred_element_type=jnp...  39.8 us
    dot_general x5, matrix products, outer_sum(): jnp.einsum('td,tf->df', left_side, right_side, preferred_element_type=jnp...  35.2 us
    convert_element_type x25, other arithmetic, low(): return value.astype(jnp.bfloat16)  26.3 us
  transfers between devices with their start and end apart: 55, of which 30 were waited for; matrix products, arithmetic and copies ran while one was open for 20% of the time, Pallas kernels for 17%

profile of v3, /device:TPU:20, one launch (start us, length us, event | category | flops | bytes accessed | tf_op | source)
XLA Modules:
  0.0 866.5 jit_solution(15791067629390853086)
XLA Ops:
  23.8 176.7 %shard_map.246 = (bf16[2,4,4,72,1536]{4,3,2,1,0:T(8,128)(2,1)}, bf16[4,128,2304]{2,1,0:T(8,128)(2,1)}, bf16[2,8,2,72,1152]{4,3,2,1,0:T(8,128)(2,1)}, bf16[2,8,2,...) custom-call(bf16[4,72,1536]{2,1,0:T(8,128)(2,1)} %pad_maximum_fusion.9.refs_0_, bf16[128,2304]{1,0:T(8,128)(2,1)} %fusion.111.refs_1_, ...), custom_call_target="tpu_custom_call" | custom-call | tf_op jit(solution)/shard_map/pallas_call | solution.py:656
  217.8 7.4 collective-permute-done
  231.1 9.8 %collective-permute-done.1 = bf16[512,512]{1,0:T(8,128)(2,1)S(1)} collective-permute-done((bf16[512,512]{1,0:T(8,128)(2,1)}, bf16[512,512]{1,0:T(8,128)(2,1)S(1)}, u32[]{:S(2)}, u32[]{:S(2)}) %collective-permute-start.1) | collective-permute-done | bytes 524320 | tf_op jit(solution)/shard_map/ppermute | solution.py:325
  246.1 9.4 %collective-permute-done.2 = bf16[512,512]{1,0:T(8,128)(2,1)S(1)} collective-permute-done((bf16[512,512]{1,0:T(8,128)(2,1)S(1)}, bf16[512,512]{1,0:T(8,128)(2,1)S(1)}, u32[]{:S(2)}, u32[]{:S(2)}) %collective-permute-start.2) | collective-permute-done | bytes 524320 | tf_op jit(solution)/shard_map/ppermute | solution.py:325
  265.6 14.8 %collective-permute-done.4 = bf16[128,2304]{1,0:T(8,128)(2,1)S(1)} collective-permute-done((bf16[128,2304]{1,0:T(8,128)(2,1)S(1)}, bf16[128,2304]{1,0:T(8,128)(2,1)S(1)}, u32[]{:S(2)}, u32[]{:S(2)}) %collective-permute-start.4) | collective-permute-done | bytes 589856 | tf_op jit(solution)/shard_map/ppermute | solution.py:325
  285.8 11.6 %collective-permute-done.6 = bf16[128,2304]{1,0:T(8,128)(2,1)} collective-permute-done((bf16[128,2304]{1,0:T(8,128)(2,1)}, bf16[128,2304]{1,0:T(8,128)(2,1)}, u32[]{:S(2)}, u32[]{:S(2)}) %collective-permute-start.6) | collective-permute-done | bytes 589856 | tf_op jit(solution)/shard_map/ppermute | solution.py:325
  326.8 10.2 %collective-permute-done.10 = bf16[128,2304]{1,0:T(8,128)(2,1)S(1)} collective-permute-done((bf16[128,2304]{1,0:T(8,128)(2,1)S(1)}, bf16[128,2304]{1,0:T(8,128)(2,1)S(1)}, u32[]{:S(2)}, u32[]{:S(2)}) %collective-permute-start.10) | collective-permute-done | bytes 589856 | tf_op jit(solution)/shard_map/ppermute | solution.py:325
  354.6 14.1 %collective-permute-done.14 = bf16[128,2304]{1,0:T(8,128)(2,1)S(1)} collective-permute-done((bf16[128,2304]{1,0:T(8,128)(2,1)S(1)}, bf16[128,2304]{1,0:T(8,128)(2,1)S(1)}, u32[]{:S(2)}, u32[]{:S(2)}) %collective-permute-start.14) | collective-permute-done | bytes 589856 | tf_op jit(solution)/shard_map/ppermute | solution.py:325
  371.8 9.6 %collective-permute-done.16 = bf16[128,2304]{1,0:T(8,128)(2,1)S(1)} collective-permute-done((bf16[128,2304]{1,0:T(8,128)(2,1)S(1)}, bf16[128,2304]{1,0:T(8,128)(2,1)S(1)}, u32[]{:S(2)}, u32[]{:S(2)}) %collective-permute-start.16) | collective-permute-done | bytes 589856 | tf_op jit(solution)/shard_map/ppermute | solution.py:325
  403.0 6.3 collective-permute-done.18
  419.5 7.2 collective-permute-done.24
  471.7 7.0 collective-permute-done.31
  491.3 6.8 convolution_convert_fusion.2
  500.7 8.3 convolution_convert_fusion.1
  514.7 14.3 %collective-permute-done.38 = bf16[128,2304]{1,0:T(8,128)(2,1)S(1)} collective-permute-done((bf16[128,2304]{1,0:T(8,128)(2,1)S(1)}, bf16[128,2304]{1,0:T(8,128)(2,1)S(1)}, u32[]{:S(2)}, u32[]{:S(2)}) %collective-permute-start.38) | collective-permute-done | bytes 589856 | tf_op jit(solution)/shard_map/ppermute | solution.py:325
  529.1 12.1 %collective-permute-done.35 = bf16[128,2304]{1,0:T(8,128)(2,1)S(1)} collective-permute-done((bf16[128,2304]{1,0:T(8,128)(2,1)S(1)}, bf16[128,2304]{1,0:T(8,128)(2,1)S(1)}, u32[]{:S(2)}, u32[]{:S(2)}) %collective-permute-start.35) | collective-permute-done | bytes 589856 | tf_op jit(solution)/shard_map/ppermute | solution.py:325
  548.4 11.0 %collective-permute-done.39 = bf16[128,2304]{1,0:T(8,128)(2,1)S(1)} collective-permute-done((bf16[128,2304]{1,0:T(8,128)(2,1)S(1)}, bf16[128,2304]{1,0:T(8,128)(2,1)S(1)}, u32[]{:S(2)}, u32[]{:S(2)}) %collective-permute-start.39) | collective-permute-done | bytes 589856 | tf_op jit(solution)/shard_map/ppermute | solution.py:325
  560.4 8.7 %convolution_convert_fusion = bf16[2304,1152]{1,0:T(8,128)(2,1)S(1)} fusion(bf16[256,2304]{1,0:T(8,128)(2,1)} %pad_maximum_fusion.7, bf16[256,2304]{1,0:T(8,128)(2,1)S(1)} %pad_maximum_fusion.6, bf16[256,2304]{1,0:T(8,128)(2,1)} %copy-done.56, bf16[256,2304]{1,0:T(8,128)(2,1)S(1)} %copy-done.30, bf16[256,1152]{1,0:T(8,128)(2,1)} %copy-done.132, ...), kind=kOutput, calls=%fused_computation | convolution fusion | flops 5466783744 | bytes 12386304 | tf_op jit(solution)/shard_map/td,tf->df/dot_general | solution.py:900
  635.9 8.1 collective-permute-done.52
  652.0 19.8 %collective-permute-done.54 = bf16[8,72,1152]{2,1,0:T(8,128)(2,1)} collective-permute-done((bf16[8,72,1152]{2,1,0:T(8,128)(2,1)}, bf16[8,72,1152]{2,1,0:T(8,128)(2,1)}, u32[]{:S(2)}, u32[]{:S(2)}) %collective-permute-start.54) | collective-permute-done | bytes 1327136 | tf_op jit(solution)/shard_map/ppermute | solution.py:325
  676.8 5.8 multiply_reduce_fusion
  691.6 6.7 convolution_convert_fusion.3
  698.4 148.3 %shard_map.247 = (bf16[4,72,1024]{2,1,0:T(8,128)(2,1)S(1)}, bf16[4,72,640]{2,1,0:T(8,128)(2,1)S(1)}, bf16[72,9216]{1,0:T(8,128)(2,1)S(1)}, bf16[72,9216]{1,0:T(8,128)(2,1)S(1)}, bf16[72,9216]{1,0:T(8,128)(2,1)S(1)}) custom-call(bf16[2,4,4,72,1024]{4,3,2,1,0:T(8,128)(2,1)} %bitcast.475, bf16[2,4,4,72,640]{4,3,2,1,0:T(8,128)(2,1)S(1)} %bitcast.468, ...), custom_call_target="tpu_custom_call" | custom-call | tf_op jit(solution)/shard_map/pallas_call | solution.py:846
  858.5 5.9 collective-permute-done.48
  (571 shorter events, 313.7 us)
Async XLA Ops:
  325.3 20.5 %collective-permute-start.13 = (bf16[128,2304]{1,0:T(8,128)(2,1)S(1)}, bf16[128,2304]{1,0:T(8,128)(2,1)S(1)}, u32[]{:S(2)}, u32[]{:S(2)}) collective-permute-start(bf16[128,2304]{1,0:T(8,128)(2,1)S(1)} %broadcast_select_fusion.2), channel_id=1, source_target_pairs={{0,2},{1,3},{2,0},{3,1},{4,6},{5,7},{6,4},{7,5},{8,10},{9,11},{10,... | collective-permute-start | bytes 1769480 | tf_op jit(solution)/shard_map/ppermute | solution.py:325
  353.9 27.4 %collective-permute-start.16 = (bf16[128,2304]{1,0:T(8,128)(2,1)S(1)}, bf16[128,2304]{1,0:T(8,128)(2,1)S(1)}, u32[]{:S(2)}, u32[]{:S(2)}) collective-permute-start(bf16[128,2304]{1,0:T(8,128)(2,1)S(1)} %slice_bitcast_fusion.11), channel_id=1, source_target_pairs={{0,2},{1,3},{2,0},{3,1},{4,6},{5,7},{6,4},{7,5},{8,10},{9,11},{10,... | collective-permute-start | bytes 1769480 | tf_op jit(solution)/shard_map/ppermute | solution.py:325
  370.2 27.8 %collective-permute-start.19 = (bf16[128,2304]{1,0:T(8,128)(2,1)S(1)}, bf16[128,2304]{1,0:T(8,128)(2,1)S(1)}, u32[]{:S(2)}, u32[]{:S(2)}) collective-permute-start(bf16[128,2304]{1,0:T(8,128)(2,1)S(1)} %slice_bitcast_fusion.10), channel_id=1, source_target_pairs={{0,2},{1,3},{2,0},{3,1},{4,6},{5,7},{6,4},{7,5},{8,10},{9,11},{10,... | collective-permute-start | bytes 1769480 | tf_op jit(solution)/shard_map/ppermute | solution.py:325
  382.8 20.2 %collective-permute-start.15 = (bf16[128,2304]{1,0:T(8,128)(2,1)S(1)}, bf16[128,2304]{1,0:T(8,128)(2,1)S(1)}, u32[]{:S(2)}, u32[]{:S(2)}) collective-permute-start(bf16[128,2304]{1,0:T(8,128)(2,1)S(1)} %slice_bitcast_fusion.12), channel_id=1, source_target_pairs={{0,2},{1,3},{2,0},{3,1},{4,6},{5,7},{6,4},{7,5},{8,10},{9,11},{10,... | collective-permute-start | bytes 1769480 | tf_op jit(solution)/shard_map/ppermute | solution.py:325
  417.0 19.4 %collective-permute-start.26 = (bf16[128,2304]{1,0:T(8,128)(2,1)S(1)}, bf16[128,2304]{1,0:T(8,128)(2,1)S(1)}, u32[]{:S(2)}, u32[]{:S(2)}) collective-permute-start(bf16[128,2304]{1,0:T(8,128)(2,1)S(1)} %get-tuple-element.134), channel_id=1, source_target_pairs={{4,8},{5,9},{6,10},{7,11},{8,4},{9,5},{10,6},{11,7},{20,24},{21,25... | collective-permute-start | bytes 1769480 | tf_op jit(solution)/shard_map/ppermute | solution.py:325
  426.7 20.5 %collective-permute-start.25 = (bf16[128,2304]{1,0:T(8,128)(2,1)S(1)}, bf16[128,2304]{1,0:T(8,128)(2,1)S(1)}, u32[]{:S(2)}, u32[]{:S(2)}) collective-permute-start(bf16[128,2304]{1,0:T(8,128)(2,1)S(1)} %collective-permute-done.24), channel_id=1, source_target_pairs={{0,2},{1,3},{2,0},{3,1},{4,6},{5,7},{6,4},{7,5},{8,10},{9,11},{10,... | collective-permute-start | bytes 1769480 | tf_op jit(solution)/shard_map/ppermute | solution.py:325
  426.7 26.1 %collective-permute-start.29 = (bf16[128,2304]{1,0:T(8,128)(2,1)S(1)}, bf16[128,2304]{1,0:T(8,128)(2,1)S(1)}, u32[]{:S(2)}, u32[]{:S(2)}) collective-permute-start(bf16[128,2304]{1,0:T(8,128)(2,1)S(1)} %collective-permute-done.24), channel_id=1, source_target_pairs={{4,8},{5,9},{6,10},{7,11},{8,4},{9,5},{10,6},{11,7},{20,24},{21,25... | collective-permute-start | bytes 1769480 | tf_op jit(solution)/shard_map/ppermute | solution.py:325
  487.3 23.4 %collective-permute-start.32 = (bf16[128,2304]{1,0:T(8,128)(2,1)S(1)}, bf16[128,2304]{1,0:T(8,128)(2,1)S(1)}, u32[]{:S(2)}, u32[]{:S(2)}) collective-permute-start(bf16[128,2304]{1,0:T(8,128)(2,1)S(1)} %slice_bitcast_fusion.9), channel_id=1, source_target_pairs={{0,2},{1,3},{2,0},{3,1},{4,6},{5,7},{6,4},{7,5},{8,10},{9,11},{10,... | collective-permute-start | bytes 1769480 | tf_op jit(solution)/shard_map/ppermute | solution.py:325
  487.5 24.9 %collective-permute-start.34 = (bf16[128,2304]{1,0:T(8,128)(2,1)S(1)}, bf16[128,2304]{1,0:T(8,128)(2,1)S(1)}, u32[]{:S(2)}, u32[]{:S(2)}) collective-permute-start(bf16[128,2304]{1,0:T(8,128)(2,1)S(1)} %slice_bitcast_fusion.7), channel_id=1, source_target_pairs={{0,2},{1,3},{2,0},{3,1},{4,6},{5,7},{6,4},{7,5},{8,10},{9,11},{10,... | collective-permute-start | bytes 1769480 | tf_op jit(solution)/shard_map/ppermute | solution.py:325
  499.9 79.4 %collective-permute-start.49 = (bf16[2,8,72,1152]{3,2,1,0:T(8,128)(2,1)}, bf16[2,8,72,1152]{3,2,1,0:T(8,128)(2,1)}, u32[]{:S(2)}, u32[]{:S(2)}) collective-permute-start(bf16[2,8,72,1152]{3,2,1,0:T(8,128)(2,1)} %dynamic-slice_bitcast_fusion.2), channel_id=1, source_target_pairs={{0,1},{1,0},{2,3},{3,2},{4,5},{5,4},{6,7},{7,6},{8,9},{9,8},{10,11... | collective-permute-start | bytes 7962632 | tf_op jit(solution)/shard_map/ppermute | solution.py:325
  510.8 73.9 %collective-permute-start.51 = (bf16[2,8,72,1152]{3,2,1,0:T(8,128)(2,1)}, bf16[2,8,72,1152]{3,2,1,0:T(8,128)(2,1)}, u32[]{:S(2)}, u32[]{:S(2)}) collective-permute-start(bf16[2,8,72,1152]{3,2,1,0:T(8,128)(2,1)} %dynamic-slice_bitcast_fusion.1), channel_id=1, source_target_pairs={{0,1},{1,0},{2,3},{3,2},{4,5},{5,4},{6,7},{7,6},{8,9},{9,8},{10,11... | collective-permute-start | bytes 7962632 | tf_op jit(solution)/shard_map/ppermute | solution.py:325
  511.0 18.0 %collective-permute-start.38 = (bf16[128,2304]{1,0:T(8,128)(2,1)S(1)}, bf16[128,2304]{1,0:T(8,128)(2,1)S(1)}, u32[]{:S(2)}, u32[]{:S(2)}) collective-permute-start(bf16[128,2304]{1,0:T(8,128)(2,1)S(1)} %convert_element_type.538), channel_id=1, source_target_pairs={{0,4},{1,5},{2,6},{3,7},{12,8},{13,9},{14,10},{15,11},{16,20},{17,... | collective-permute-start | bytes 1769480 | tf_op jit(solution)/shard_map/ppermute | solution.py:325
  512.3 32.9 %collective-permute-start.37 = (bf16[128,2304]{1,0:T(8,128)(2,1)S(1)}, bf16[128,2304]{1,0:T(8,128)(2,1)S(1)}, u32[]{:S(2)}, u32[]{:S(2)}) collective-permute-start(bf16[128,2304]{1,0:T(8,128)(2,1)S(1)} %slice_bitcast_fusion.6), channel_id=1, source_target_pairs={{0,2},{1,3},{2,0},{3,1},{4,6},{5,7},{6,4},{7,5},{8,10},{9,11},{10,... | collective-permute-start | bytes 1769480 | tf_op jit(solution)/shard_map/ppermute | solution.py:325
  512.6 28.7 %collective-permute-start.35 = (bf16[128,2304]{1,0:T(8,128)(2,1)S(1)}, bf16[128,2304]{1,0:T(8,128)(2,1)S(1)}, u32[]{:S(2)}, u32[]{:S(2)}) collective-permute-start(bf16[128,2304]{1,0:T(8,128)(2,1)S(1)} %fusion.129), channel_id=1, source_target_pairs={{0,4},{1,5},{2,6},{3,7},{12,8},{13,9},{14,10},{15,11},{16,20},{17,... | collective-permute-start | bytes 1769480 | tf_op jit(solution)/shard_map/ppermute | solution.py:325
  529.0 40.4 %collective-permute-start.33 = (bf16[128,2304]{1,0:T(8,128)(2,1)}, bf16[128,2304]{1,0:T(8,128)(2,1)}, u32[]{:S(2)}, u32[]{:S(2)}) collective-permute-start(bf16[128,2304]{1,0:T(8,128)(2,1)} %slice_bitcast_fusion.8), channel_id=1, source_target_pairs={{0,2},{1,3},{2,0},{3,1},{4,6},{5,7},{6,4},{7,5},{8,10},{9,11},{10,... | collective-permute-start | bytes 1769480 | tf_op jit(solution)/shard_map/ppermute | solution.py:325
  541.2 18.1 %collective-permute-start.39 = (bf16[128,2304]{1,0:T(8,128)(2,1)S(1)}, bf16[128,2304]{1,0:T(8,128)(2,1)S(1)}, u32[]{:S(2)}, u32[]{:S(2)}) collective-permute-start(bf16[128,2304]{1,0:T(8,128)(2,1)S(1)} %add_convert_fusion), channel_id=1, source_target_pairs={{4,8},{5,9},{6,10},{7,11},{8,4},{9,5},{10,6},{11,7},{20,24},{21,25... | collective-permute-start | bytes 1769480 | tf_op jit(solution)/shard_map/ppermute | solution.py:325
  545.3 25.7 %collective-permute-start.36 = (bf16[128,2304]{1,0:T(8,128)(2,1)}, bf16[128,2304]{1,0:T(8,128)(2,1)}, u32[]{:S(2)}, u32[]{:S(2)}) collective-permute-start(bf16[128,2304]{1,0:T(8,128)(2,1)} %add_convert_fusion.1), channel_id=1, source_target_pairs={{4,8},{5,9},{6,10},{7,11},{8,4},{9,5},{10,6},{11,7},{20,24},{21,25... | collective-permute-start | bytes 1769480 | tf_op jit(solution)/shard_map/ppermute | solution.py:325
  569.4 22.0 %collective-permute-start.53 = (bf16[2,8,72,1152]{3,2,1,0:T(8,128)(2,1)S(1)}, bf16[2,8,72,1152]{3,2,1,0:T(8,128)(2,1)S(1)}, u32[]{:S(2)}, u32[]{:S(2)}) collective-permute-start(bf16[2,8,72,1152]{3,2,1,0:T(8,128)(2,1)S(1)} %dynamic-slice_bitcast_fusion), channel_id=1, source_target_pairs={{0,1},{1,0},{2,3},{3,2},{4,5},{5,4},{6,7},{7,6},{8,9},{9,8},{10,11... | collective-permute-start | bytes 7962632 | tf_op jit(solution)/shard_map/ppermute | solution.py:325
  583.2 45.1 %collective-permute-start.50 = (bf16[8,72,1152]{2,1,0:T(8,128)(2,1)}, bf16[8,72,1152]{2,1,0:T(8,128)(2,1)}, u32[]{:S(2)}, u32[]{:S(2)}) collective-permute-start(bf16[8,72,1152]{2,1,0:T(8,128)(2,1)} %dynamic-slice_bitcast_fusion.5), channel_id=1, source_target_pairs={{0,16},{1,17},{2,18},{3,19},{4,20},{5,21},{6,22},{7,23},{8,24},{9,... | collective-permute-start | bytes 3981320 | tf_op jit(solution)/shard_map/ppermute | solution.py:325
  588.5 55.4 %collective-permute-start.52 = (bf16[8,72,1152]{2,1,0:T(8,128)(2,1)}, bf16[8,72,1152]{2,1,0:T(8,128)(2,1)}, u32[]{:S(2)}, u32[]{:S(2)}) collective-permute-start(bf16[8,72,1152]{2,1,0:T(8,128)(2,1)} %dynamic-slice_bitcast_fusion.4), channel_id=1, source_target_pairs={{0,16},{1,17},{2,18},{3,19},{4,20},{5,21},{6,22},{7,23},{8,24},{9,... | collective-permute-start | bytes 3981320 | tf_op jit(solution)/shard_map/ppermute | solution.py:325
  593.3 78.5 %collective-permute-start.54 = (bf16[8,72,1152]{2,1,0:T(8,128)(2,1)}, bf16[8,72,1152]{2,1,0:T(8,128)(2,1)}, u32[]{:S(2)}, u32[]{:S(2)}) collective-permute-start(bf16[8,72,1152]{2,1,0:T(8,128)(2,1)} %dynamic-slice_bitcast_fusion.3), channel_id=1, source_target_pairs={{0,16},{1,17},{2,18},{3,19},{4,20},{5,21},{6,22},{7,23},{8,24},{9,... | collective-permute-start | bytes 3981320 | tf_op jit(solution)/shard_map/ppermute | solution.py:325
  613.7 17.5 %collective-permute-start.44 = (bf16[512,512]{1,0:T(8,128)(2,1)}, bf16[512,512]{1,0:T(8,128)(2,1)}, u32[]{:S(2)}, u32[]{:S(2)}) collective-permute-start(bf16[512,512]{1,0:T(8,128)(2,1)} %pad_maximum_fusion.13), channel_id=1, source_target_pairs={{4,0},{5,1},{6,2},{7,3},{8,4},{9,5},{10,6},{11,7},{12,8},{13,9},{1... | collective-permute-start | bytes 1572872 | tf_op jit(solution)/shard_map/ppermute | solution.py:325
  648.4 26.1 %collective-permute-start.46 = (bf16[512,512]{1,0:T(8,128)(2,1)S(1)}, bf16[512,512]{1,0:T(8,128)(2,1)S(1)}, u32[]{:S(2)}, u32[]{:S(2)}) collective-permute-start(bf16[512,512]{1,0:T(8,128)(2,1)S(1)} %fusion.130), channel_id=1, source_target_pairs={{4,0},{5,1},{6,2},{7,3},{8,4},{9,5},{10,6},{11,7},{12,8},{13,9},{1... | collective-permute-start | bytes 1572872 | tf_op jit(solution)/shard_map/ppermute | solution.py:325
  683.9 162.9 %collective-permute-start.47 = (bf16[2,128,2304]{2,1,0:T(8,128)(2,1)}, bf16[2,128,2304]{2,1,0:T(8,128)(2,1)}, u32[]{:S(2)}, u32[]{:S(2)}) collective-permute-start(bf16[2,128,2304]{2,1,0:T(8,128)(2,1)} %slice_bitcast_fusion.1), channel_id=1, source_target_pairs={{0,1},{1,0},{2,3},{3,2},{4,5},{5,4},{6,7},{7,6},{8,9},{9,8},{10,11... | collective-permute-start | bytes 3538952 | tf_op jit(solution)/shard_map/ppermute | solution.py:325
  (170 other events, 1778.6 us)

commit v4 on v3

--- a/solution.py
+++ b/solution.py
@@ -432,7 +432,7 @@
 
 def gather_plane(spot, own):
     return [
-        jnp.concatenate([block, to_x(block)], axis=0) for block in gather_line(spot, own)
+        jnp.concatenate([block, to_row(block)], axis=0) for block in gather_line(spot, own)
     ]
 
 
@@ -443,7 +443,7 @@
             parts[3], chunks[1], chunks[0] = lax.optimization_barrier(
                 (parts[3], chunks[1], chunks[0])
             )
-        parts[slot] = wide(chunks[slot][0]) + wide(to_x(chunks[slot][1]))
+        parts[slot] = wide(chunks[slot][0]) + wide(to_row(chunks[slot][1]))
     return reduce_line(parts)
 
 
@@ -451,18 +451,9 @@
     return (spot.x ^ dx) * 2 + (spot.c ^ dc)
 
 
-def narrow_hidden(spot, sums):
-    width = sums.shape[1]
-    rows = sums.shape[0] // (2 * LINE * 4)
-    blocks = sums.reshape(2, LINE * 2, 2, rows, width)
-    cores = low(
-        wide(pick(blocks, spot.c, 2)) + wide(to_core(pick(blocks, 1 - spot.c, 2)))
-    )
-    return low(wide(pick(cores, spot.y)) + wide(to_row(pick(cores, 1 - spot.y))))
-
-
 GROUP = ((0, 0), (0, 1), (1, 0), (1, 1))
 PLANE = ((2, 0), (1, 0), (3, 0), (0, 1), (2, 1), (1, 1), (3, 1))
+PLANE_FAR = ((2, 0), (3, 0), (2, 1), (3, 1), (1, 0), (1, 1), (0, 1))
 
 
 def my_place():
@@ -533,24 +524,25 @@
     send_sem, recv_sem, local_sem = refs[4 + 2 * count :]
     y, z, x, c = my_place()
     me = x * 2 + c
-    chip = z * 2 + x
+    chip = z * 2 + y
     chips = LINE * 2
     group = {d: device_at(y, z, (x + d[0]) % 2, (c + d[1]) % 2) for d in GROUP[1:]}
-    plane = {d: device_at(y, along_line(z, d[0]), (x + d[1]) % 2, c) for d in PLANE}
+    plane = {d: device_at((y + d[1]) % 2, along_line(z, d[0]), x, c) for d in PLANE}
     row_peer = device_at(1 - y, z, x, c)
     core_peer = group[(0, 1)]
+    chip_peer = group[(1, 0)]
     up = device_at(y, jnp.minimum(z + 1, LINE - 1), x, c)
     down = device_at(y, jnp.maximum(z - 1, 0), x, c)
     can_up = z < LINE - 1
     can_down = z > 0
-    greet([row_peer, core_peer, group[(1, 1)]] + list(plane.values()))
+    greet(list(group.values()) + list(plane.values()))
     post = Courier(send_sem, recv_sem)
 
     def member(d):
         return ((x + d[0]) % 2) * 2 + (c + d[1]) % 2
 
     def chip_of(d):
-        return along_line(z, d[0]) * 2 + (x + d[1]) % 2
+        return along_line(z, d[0]) * 2 + (y + d[1]) % 2
 
     def columns(ref, which):
         width = ref.shape[1] // chips
@@ -559,7 +551,7 @@
     for d, device in group.items():
         post.send(heads_in.at[member(d)], heads.at[y, z, me], device, ("group", d))
     local = [(heads_in.at[me], heads.at[y, z, me]), (tokens_in, tokens.at[0])]
-    local += [(columns(w, chip), out.at[y, chip, c]) for w, out in zip(hidden_in, hidden)]
+    local += [(columns(w, chip), out.at[y, z, x, c]) for w, out in zip(hidden_in, hidden)]
     kept = []
     for slot, (source, target) in enumerate(local):
         kept.append(pltpu.make_async_copy(source, target, local_sem.at[slot]))
@@ -577,19 +569,22 @@
         for d in PLANE:
             post.send(
                 columns(hidden_in[m], chip_of(d)),
-                hidden[m].at[y, chip, c],
+                hidden[m].at[y, z, x, c],
                 plane[d],
                 ("plane", m, d),
             )
         own = columns(hidden_in[m], chip)
-        post.send(own, hidden[m].at[y, chip, c], row_peer, ("far", m, (0, 0)))
-        post.send(own, hidden[m].at[y, chip, c], core_peer, ("core", 0, m, (0, 0)))
+        post.send(own, hidden[m].at[y, z, x, c], chip_peer, ("far", m, (0, 0)))
+        post.send(own, hidden[m].at[y, z, x, c], core_peer, ("core", 0, m, (0, 0)))
+
+    def rows_of(m, d, x_from, c_from):
+        return hidden[m].at[(y + d[1]) % 2, along_line(z, d[0]), x_from, c_from]
 
     def plane_in(m):
         for d in PLANE:
-            block = hidden[m].at[y, chip_of(d), c]
+            block = rows_of(m, d, x, c)
             post.arrive(block, core_peer, ("plane", m, d))
-            post.send(block, block, row_peer, ("far", m, d))
+            post.send(block, block, chip_peer, ("far", m, d))
             post.send(block, block, core_peer, ("core", 0, m, d))
 
     spread(heads_in.at[me], (0, 0))
@@ -619,7 +614,7 @@
         plane_in(m)
     for m in range(count):
         for d in ((0, 0),) + PLANE:
-            block = hidden[m].at[1 - y, chip_of(d), c]
+            block = rows_of(m, d, 1 - x, c)
             post.arrive(block, core_peer, ("far", m, d))
             post.send(block, block, core_peer, ("core", 1, m, d))
     for d in GROUP[1:]:
@@ -634,7 +629,7 @@
     for m in range(count):
         for half in range(2):
             for d in ((0, 0),) + PLANE:
-                block = hidden[m].at[y if half == 0 else 1 - y, chip_of(d), 1 - c]
+                block = rows_of(m, d, x if half == 0 else 1 - x, 1 - c)
                 post.arrive(block, core_peer, ("core", half, m, d))
     post.finish()
     for copy in kept:
@@ -652,7 +647,7 @@
     ]
     for matrix in hidden_in:
         width = matrix.shape[1] // (LINE * 2)
-        outs.append(jax.ShapeDtypeStruct((2, LINE * 2, 2, rows, width), jnp.bfloat16))
+        outs.append(jax.ShapeDtypeStruct((2, LINE, 2, 2, rows, width), jnp.bfloat16))
     found = pl.pallas_call(
         functools.partial(gather_kernel, count),
         out_shape=outs,
@@ -678,25 +673,28 @@
     hidden = refs[2 * parts + count : 2 * (parts + count)]
     scratch = refs[2 * (parts + count) :]
     own, across, above, below = (scratch[n * parts : (n + 1) * parts] for n in range(4))
-    send_sem, recv_sem, load_sem, head_send, head_recv, local_sem = scratch[4 * parts :]
+    share, other_core, other_chip = scratch[4 * parts : 4 * parts + 3]
+    send_sem, recv_sem, load_sem, head_send, head_recv, local_sem = scratch[4 * parts + 3 :]
     y, z, x, c = my_place()
     me = x * 2 + c
-    chip = z * 2 + x
+    chip = z * 2 + y
     chips = LINE * 2
     group = {d: device_at(y, z, (x + d[0]) % 2, (c + d[1]) % 2) for d in GROUP[1:]}
-    plane = {d: device_at(y, along_line(z, d[0]), (x + d[1]) % 2, c) for d in PLANE}
+    plane = {d: device_at((y + d[1]) % 2, along_line(z, d[0]), x, c) for d in PLANE}
     row_peer = device_at(1 - y, z, x, c)
     core_peer = group[(0, 1)]
+    chip_peer = group[(1, 0)]
     up = device_at(y, jnp.minimum(z + 1, LINE - 1), x, c)
     down = device_at(y, jnp.maximum(z - 1, 0), x, c)
-    greet([row_peer, core_peer, group[(1, 1)]] + list(plane.values()))
+    greet(list(group.values()) + list(plane.values()))
     post = Courier(send_sem, recv_sem)
+    everyone = PLANE_FAR + ((0, 0),)
 
     def member(d):
         return ((x + d[0]) % 2) * 2 + (c + d[1]) % 2
 
-    def chip_of(d):
-        return along_line(z, d[0]) * 2 + (x + d[1]) % 2
+    def owner(d):
+        return (y + d[1]) % 2, along_line(z, d[0])
 
     order = [(0, 0, None)]
     for step in range(1, LINE):
@@ -741,30 +739,75 @@
 
         under(okay, lambda start=start: each(start))
     kept = []
-    for m in range(count):
-        for d in PLANE:
-            width = hidden[m].shape[1] // chips
-            post.send(
-                hidden_in[m].at[chip_of(d)],
-                hidden[m].at[:, pl.ds(pl.multiple_of(chip * width, 128), width)],
-                plane[d],
-                ("plane", m, d),
-            )
-        kept.append(
-            pltpu.make_async_copy(
-                hidden_in[m].at[chip],
-                hidden[m].at[:, pl.ds(pl.multiple_of(chip * width, 128), width)],
-                local_sem.at[m],
-            )
-        )
-        kept[-1].start()
+    loads = {}
+    for d in everyone:
+        y_to, z_to = owner(d)
+        for m in range(count):
+            for side, x_to in ((0, 1 - x), (1, x)):
+                post.send(
+                    hidden_in[m].at[y_to, z_to, x_to, 1 - c],
+                    other_core.at[m, y_to, z_to, x_to],
+                    core_peer,
+                    ("core", m, d, side),
+                )
+                loads[m, d, side] = pltpu.make_async_copy(
+                    hidden_in[m].at[y_to, z_to, x_to, c],
+                    share.at[m, y_to, z_to, x_to],
+                    local_sem.at[count + parts + len(loads)],
+                )
+                loads[m, d, side].start()
+
+    def add_up(target, terms):
+        rows, width = target.shape
+
+        def add(k, carry):
+            lanes = pl.ds(pl.multiple_of(k * 128, 128), 128)
+            total = wide(target[:, lanes])
+            for term in terms:
+                total = total + wide(term[:, lanes])
+            target[:, lanes] = low(total)
+            return carry
+
+        lax.fori_loop(0, width // 128, add, 0)
+
+    def over_chip(d):
+        y_to, z_to = owner(d)
+        for m in range(count):
+            block = share.at[m, y_to, z_to, 1 - x]
+            arrived = other_core.at[m, y_to, z_to, 1 - x]
+            loads[m, d, 0].wait()
+            post.arrive(arrived, core_peer, ("core", m, d, 0))
+            add_up(block, [arrived])
+            post.send(block, other_chip.at[m, y_to, z_to], chip_peer, ("chip", m, d))
+
+    def landing(m, which):
+        width = hidden[m].shape[1] // chips
+        return hidden[m].at[:, pl.ds(pl.multiple_of(which * width, 128), width)]
+
+    def over_plane(d):
+        y_to, z_to = owner(d)
+        for m in range(count):
+            block = share.at[m, y_to, z_to, x]
+            loads[m, d, 1].wait()
+            post.arrive(other_core.at[m, y_to, z_to, x], core_peer, ("core", m, d, 1))
+            post.arrive(other_chip.at[m, y_to, z_to], core_peer, ("chip", m, d))
+            add_up(block, [other_core.at[m, y_to, z_to, x], other_chip.at[m, y_to, z_to]])
+            if d == (0, 0):
+                kept.append(pltpu.make_async_copy(block, landing(m, chip), local_sem.at[m]))
+                kept[-1].start()
+            else:
+                post.send(block, landing(m, chip), plane[d], ("plane", m, d))
+
+    for d in everyone:
+        over_chip(d)
 
     def ready(p, place, m):
         to_row_copy(p, place, m).wait_recv()
         load_copy(p, place, m).wait()
         return wide(own[p][place, m]) + wide(across[p][place, m])
 
-    for sign, step, okay in order[:-1]:
+    planned = [everyone[:1], everyone[1:2], everyone[2:3], everyone[3:4], everyone[4:6], everyone[6:]]
+    for (sign, step, okay), hidden_now in zip(order[:-1], planned):
         place = z + sign * step
 
         def relay(m, place=place, sign=sign):
@@ -786,6 +829,8 @@
                 (up_copy if sign > 0 else down_copy)(p, place, m).start()
 
         under(okay, lambda relay=relay: each(relay))
+        for d in hidden_now:
+            over_plane(d)
 
     def settle(m):
         for p in range(parts):
@@ -814,9 +859,8 @@
             post.arrive(heads[p].at[member(d)], core_peer, ("group", p, d))
     for m in range(count):
         for d in PLANE:
-            width = hidden[m].shape[1] // chips
-            block = hidden[m].at[:, pl.ds(pl.multiple_of(chip_of(d) * width, 128), width)]
-            post.arrive(block, core_peer, ("plane", m, d))
+            y_from, z_from = owner(d)
+            post.arrive(landing(m, z_from * 2 + y_from), core_peer, ("plane", m, d))
     for sign, step, okay in order:
         place = z + sign * step
 
@@ -837,12 +881,11 @@
 def scatter_weights(head_sums, hidden_sums):
     parts, count = len(head_sums), len(hidden_sums)
     rows = head_sums[0].shape[0] // (2 * LINE * 4)
+    width = hidden_sums[0].shape[1]
     anywhere = pl.BlockSpec(memory_space=pl.ANY)
-    copies = 7 * count + 3 * parts
+    copies = (32 + 8 + 7) * count + 3 * parts
     outs = [jax.ShapeDtypeStruct((4, rows, h.shape[1]), jnp.bfloat16) for h in head_sums]
-    outs += [
-        jax.ShapeDtypeStruct((rows, h.shape[0] * h.shape[2]), jnp.bfloat16) for h in hidden_sums
-    ]
+    outs += [jax.ShapeDtypeStruct((rows, LINE * 2 * width), jnp.bfloat16)] * count
     found = pl.pallas_call(
         functools.partial(scatter_kernel, parts, count),
         out_shape=outs,
@@ -852,19 +895,22 @@
             pltpu.VMEM((LINE, 4, rows, h.shape[1]), jnp.bfloat16) for _ in range(4) for h in head_sums
         ]
         + [
+            pltpu.VMEM((count, 2, LINE, 2, rows, width), jnp.bfloat16),
+            pltpu.VMEM((count, 2, LINE, 2, rows, width), jnp.bfloat16),
+            pltpu.VMEM((count, 2, LINE, rows, width), jnp.bfloat16),
             pltpu.SemaphoreType.DMA((copies,)),
             pltpu.SemaphoreType.DMA((copies,)),
             pltpu.SemaphoreType.DMA((parts, LINE, 4)),
             pltpu.SemaphoreType.DMA((parts, 3, LINE, 4)),
             pltpu.SemaphoreType.DMA((parts, 3, LINE, 4)),
-            pltpu.SemaphoreType.DMA((count + parts,)),
+            pltpu.SemaphoreType.DMA((count + parts + 16 * count,)),
         ],
         compiler_params=pltpu.CompilerParams(
-            collective_id=1, has_side_effects=True, vmem_limit_bytes=40 << 20
+            collective_id=1, has_side_effects=True, vmem_limit_bytes=56 << 20
         ),
     )(
         *[h.reshape(2, LINE, 4, rows, h.shape[1]) for h in head_sums],
-        *hidden_sums,
+        *[h.reshape(2, LINE, 2, 2, rows, width) for h in hidden_sums],
     )
     return found[:parts], found[parts:]
 
@@ -1037,16 +1083,15 @@
                 2, count, D
             )
         )
-    back_chunks, mid_chunks, gate_grads, up_grads, grad_chunks, acts = lax.optimization_barrier(
-        (back_chunks, mid_chunks, gate_grads, up_grads, grad_chunks, acts)
-    )
-    grad_mid = reduce_plane(back_chunks)
+    grad_mid = reduce_plane(lax.optimization_barrier(back_chunks))
+    grad_mid, mid_chunks, gate_grads, up_grads, grad_chunks, acts = lax.optimization_barrier(
+        (grad_mid, mid_chunks, gate_grads, up_grads, grad_chunks, acts)
+    )
     mid_all = jnp.concatenate(mid_chunks, axis=0)
-    gate_sums = narrow_hidden(spot, low(outer_sum(mid_all, jnp.concatenate(gate_grads, axis=0))))
-    up_sums = narrow_hidden(spot, low(outer_sum(mid_all, jnp.concatenate(up_grads, axis=0))))
-    down_sums = narrow_hidden(
-        spot,
-        low(outer_sum(jnp.concatenate(grad_chunks, axis=0), jnp.concatenate(acts, axis=0))),
+    gate_sums = low(outer_sum(mid_all, jnp.concatenate(gate_grads, axis=0)))
+    up_sums = low(outer_sum(mid_all, jnp.concatenate(up_grads, axis=0)))
+    down_sums = low(
+        outer_sum(jnp.concatenate(grad_chunks, axis=0), jnp.concatenate(acts, axis=0))
     )
 
     hidden_part, third_part = jax.vjp(rmsnorm, hidden_one, gain_third)[1](grad_mid)

time: 878 us -> 845 us (0.962)
  other arithmetic: 61.6 us -> 40.1 us
  starting transfers between devices: 75.8 us -> 91.5 us
  Pallas kernels: 325 us -> 316 us
    pallas_call x1, Pallas kernels: 177 us -> 147 us  [gather_weights(): pl.pallas_call(functools.partial(gather_kernel, count), out_shape=outs, i...]
    pallas_call x1, Pallas kernels: 148 us -> 169 us  [scatter_weights(): pl.pallas_call(functools.partial(scatter_kernel, parts, count), out_shape...]
    convert_element_type x25 -> x19, other arithmetic: 26.3 us -> 10.4 us  [low(): return value.astype(jnp.bfloat16)]
    ppermute x55 -> x49, starting transfers between devices: 75.8 us -> 91.5 us  [send(): return lax.ppermute(value, AXES, moves(2 * LINE * 4, rule))]
    ppermute x55 -> x49, waiting for transfers between devices: 210 us -> 209 us  [send(): return lax.ppermute(value, AXES, moves(2 * LINE * 4, rule))]
  transfers between devices with their start and end apart: 55 -> 49, of which waited for: 30 -> 31; matrix products, arithmetic and copies ran while one was open for 20% -> 14% of each run, Pallas kernels for 17% -> 20%
where the time goes in v4:
time: 845 us; the launch traced here: 835 us
  Pallas kernels  316 us (37%)
  waiting for transfers between devices  209 us (25%)
  matrix products  138 us (16%)
  starting transfers between devices  91.5 us (11%)
  other arithmetic  40.1 us (5%)
  local copies, waits for them, and re-layouts  27.9 us (3%)
  between operations  12.9 us (2%)
    ppermute x49, waiting for transfers between devices, send(): return lax.ppermute(value, AXES, moves(2 * LINE * 4, rule))  209 us
    pallas_call x1, Pallas kernels, scatter_weights(): pl.pallas_call(functools.partial(scatter_kernel, parts, count), out_shape...  169 us
    pallas_call x1, Pallas kernels, gather_weights(): pl.pallas_call(functools.partial(gather_kernel, count), out_shape=outs, i...  147 us
    ppermute x49, starting transfers between devices, send(): return lax.ppermute(value, AXES, moves(2 * LINE * 4, rule))  91.5 us
    dot_general x14, matrix products, dot(): return jnp.dot(left_side, right_side, preferred_element_type=jnp.float32)  45.2 us
    dot_general x5, matrix products, outer_sum(): jnp.einsum('td,tf->df', left_side, right_side, preferred_element_type=jnp...  35.5 us
    dot_general x14, matrix products, dot_rows(): jnp.einsum('tf,df->td', left_side, right_side, preferred_element_type=jnp...  33.4 us
  transfers between devices with their start and end apart: 49, of which 31 were waited for; matrix products, arithmetic and copies ran while one was open for 14% of the time, Pallas kernels for 20%

profile of v4, /device:TPU:20, one launch (start us, length us, event | category | flops | bytes accessed | tf_op | source)
XLA Modules:
  0.0 835.4 jit_solution(9274984072879013179)
XLA Ops:
  24.7 147.2 %shard_map.246 = (bf16[2,4,4,72,1536]{4,3,2,1,0:T(8,128)(2,1)}, bf16[4,128,2304]{2,1,0:T(8,128)(2,1)}, bf16[2,4,2,2,72,1152]{5,4,3,2,1,0:T(8,128)(2,1)}, bf16[2,...) custom-call(bf16[4,72,1536]{2,1,0:T(8,128)(2,1)} %pad_maximum_fusion.9.refs_0_, ...), custom_call_target="tpu_custom_call" | custom-call | tf_op jit(solution)/shard_map/pallas_call | solution.py:651
  180.6 19.0 %collective-permute-start = (bf16[512,512]{1,0:T(8,128)(2,1)}, bf16[512,512]{1,0:T(8,128)(2,1)}, u32[]{:S(2)}, u32[]{:S(2)}) collective-permute-start(bf16[512,512]{1,0:T(8,128)(2,1)} %pad_maximum_fusion.11), channel_id=1, source_target_pairs={{0,4},{1,5},{2,6},{3,7},{4,8},{5,9},{6,10},{7,11},{8,12},{9,13},{1... | collective-permute-start | bytes 1572872 | tf_op jit(solution)/shard_map/ppermute | solution.py:325
  219.9 8.9 %collective-permute-done.1 = bf16[512,512]{1,0:T(8,128)(2,1)S(1)} collective-permute-done((bf16[512,512]{1,0:T(8,128)(2,1)}, bf16[512,512]{1,0:T(8,128)(2,1)S(1)}, u32[]{:S(2)}, u32[]{:S(2)}) %collective-permute-start.1) | collective-permute-done | bytes 524320 | tf_op jit(solution)/shard_map/ppermute | solution.py:325
  234.4 9.6 %collective-permute-done.2 = bf16[512,512]{1,0:T(8,128)(2,1)S(1)} collective-permute-done((bf16[512,512]{1,0:T(8,128)(2,1)S(1)}, bf16[512,512]{1,0:T(8,128)(2,1)S(1)}, u32[]{:S(2)}, u32[]{:S(2)}) %collective-permute-start.2) | collective-permute-done | bytes 524320 | tf_op jit(solution)/shard_map/ppermute | solution.py:325
  256.1 13.6 %collective-permute-done.4 = bf16[128,2304]{1,0:T(8,128)(2,1)S(1)} collective-permute-done((bf16[128,2304]{1,0:T(8,128)(2,1)S(1)}, bf16[128,2304]{1,0:T(8,128)(2,1)S(1)}, u32[]{:S(2)}, u32[]{:S(2)}) %collective-permute-start.4) | collective-permute-done | bytes 589856 | tf_op jit(solution)/shard_map/ppermute | solution.py:325
  276.2 11.0 %collective-permute-done.6 = bf16[128,2304]{1,0:T(8,128)(2,1)} collective-permute-done((bf16[128,2304]{1,0:T(8,128)(2,1)}, bf16[128,2304]{1,0:T(8,128)(2,1)}, u32[]{:S(2)}, u32[]{:S(2)}) %collective-permute-start.6) | collective-permute-done | bytes 589856 | tf_op jit(solution)/shard_map/ppermute | solution.py:325
  318.0 9.6 %collective-permute-done.10 = bf16[128,2304]{1,0:T(8,128)(2,1)S(1)} collective-permute-done((bf16[128,2304]{1,0:T(8,128)(2,1)S(1)}, bf16[128,2304]{1,0:T(8,128)(2,1)S(1)}, u32[]{:S(2)}, u32[]{:S(2)}) %collective-permute-start.10) | collective-permute-done | bytes 589856 | tf_op jit(solution)/shard_map/ppermute | solution.py:325
  345.9 14.1 %collective-permute-done.14 = bf16[128,2304]{1,0:T(8,128)(2,1)S(1)} collective-permute-done((bf16[128,2304]{1,0:T(8,128)(2,1)S(1)}, bf16[128,2304]{1,0:T(8,128)(2,1)S(1)}, u32[]{:S(2)}, u32[]{:S(2)}) %collective-permute-start.14) | collective-permute-done | bytes 589856 | tf_op jit(solution)/shard_map/ppermute | solution.py:325
  363.4 9.3 %collective-permute-done.16 = bf16[128,2304]{1,0:T(8,128)(2,1)S(1)} collective-permute-done((bf16[128,2304]{1,0:T(8,128)(2,1)S(1)}, bf16[128,2304]{1,0:T(8,128)(2,1)S(1)}, u32[]{:S(2)}, u32[]{:S(2)}) %collective-permute-start.16) | collective-permute-done | bytes 589856 | tf_op jit(solution)/shard_map/ppermute | solution.py:325
  378.8 6.4 collective-permute-done.17
  394.2 6.3 collective-permute-done.18
  409.5 7.0 collective-permute-done.24
  432.1 7.4 collective-permute-done.27
  478.1 14.1 %collective-permute-done.32 = bf16[128,2304]{1,0:T(8,128)(2,1)S(1)} collective-permute-done((bf16[128,2304]{1,0:T(8,128)(2,1)S(1)}, bf16[128,2304]{1,0:T(8,128)(2,1)S(1)}, u32[]{:S(2)}, u32[]{:S(2)}) %collective-permute-start.32) | collective-permute-done | bytes 589856 | tf_op jit(solution)/shard_map/ppermute | solution.py:325
  494.3 8.2 collective-permute-done.34
  521.2 5.9 collective-permute-done.36
  536.9 8.1 convolution_convert_fusion.2
  545.0 8.1 convolution_convert_fusion.1
  553.7 8.4 %convolution_convert_fusion = bf16[2304,1152]{1,0:T(8,128)(2,1)} fusion(bf16[256,2304]{1,0:T(8,128)(2,1)S(1)} %pad_maximum_fusion.7, bf16[256,2304]{1,0:T(8,128)(2,1)S(1)} %pad_maximum_fusion.6, bf16[256,2304]{1,0:T(8,128)(2,1)S(1)} %constant_dynamic-update-slice_fusion.2, bf16[256,2304]{1,0:T(8,128)(2,1)S(1)} %pad_maximum_fusion.5, ...), kind=kOutput, calls=%fused_computation | convolution fusion | flops 5466783744 | bytes 12386304 | tf_op jit(solution)/shard_map/td,tf->df/dot_general | solution.py:946
  585.7 9.0 %collective-permute-done.44 = bf16[512,512]{1,0:T(8,128)(2,1)S(1)} collective-permute-done((bf16[512,512]{1,0:T(8,128)(2,1)S(1)}, bf16[512,512]{1,0:T(8,128)(2,1)S(1)}, u32[]{:S(2)}, u32[]{:S(2)}) %collective-permute-start.44) | collective-permute-done | bytes 524320 | tf_op jit(solution)/shard_map/ppermute | solution.py:325
  598.1 11.5 %collective-permute-done.45 = bf16[512,512]{1,0:T(8,128)(2,1)S(1)} collective-permute-done((bf16[512,512]{1,0:T(8,128)(2,1)S(1)}, bf16[512,512]{1,0:T(8,128)(2,1)S(1)}, u32[]{:S(2)}, u32[]{:S(2)}) %collective-permute-start.45) | collective-permute-done | bytes 524320 | tf_op jit(solution)/shard_map/ppermute | solution.py:325
  618.1 6.6 collective-permute-done.46
  639.1 6.6 convolution_convert_fusion.3
  645.7 169.0 %shard_map.247 = (bf16[4,72,1024]{2,1,0:T(8,128)(2,1)}, bf16[4,72,640]{2,1,0:T(8,128)(2,1)}, bf16[72,9216]{1,0:T(8,128)(2,1)}, bf16[72,9216]{1,0:T(8,128)(2,1)}, bf16[72,9216]{1,0:T(8,128)(2,1)}) custom-call(bf16[2,4,4,72,1024]{4,3,2,1,0:T(8,128)(2,1)} %bitcast.429, bf16[2,4,4,72,640]{4,3,2,1,0:T(8,128)(2,1)} %bitcast.425, ...), custom_call_target="tpu_custom_call" | custom-call | tf_op jit(solution)/shard_map/pallas_call | solution.py:889
  (532 shorter events, 297.6 us)
Async XLA Ops:
  180.6 31.3 %collective-permute-start = (bf16[512,512]{1,0:T(8,128)(2,1)}, bf16[512,512]{1,0:T(8,128)(2,1)}, u32[]{:S(2)}, u32[]{:S(2)}) collective-permute-start(bf16[512,512]{1,0:T(8,128)(2,1)} %pad_maximum_fusion.11), channel_id=1, source_target_pairs={{0,4},{1,5},{2,6},{3,7},{4,8},{5,9},{6,10},{7,11},{8,12},{9,13},{1... | collective-permute-start | bytes 1572872 | tf_op jit(solution)/shard_map/ppermute | solution.py:325
  211.8 16.9 %collective-permute-start.1 = (bf16[512,512]{1,0:T(8,128)(2,1)}, bf16[512,512]{1,0:T(8,128)(2,1)S(1)}, u32[]{:S(2)}, u32[]{:S(2)}) collective-permute-start(bf16[512,512]{1,0:T(8,128)(2,1)} %collective-permute-done), channel_id=1, source_target_pairs={{0,4},{1,5},{2,6},{3,7},{4,8},{5,9},{6,10},{7,11},{8,12},{9,13},{1... | collective-permute-start | bytes 1572872 | tf_op jit(solution)/shard_map/ppermute | solution.py:325
  253.2 16.5 %collective-permute-start.4 = (bf16[128,2304]{1,0:T(8,128)(2,1)S(1)}, bf16[128,2304]{1,0:T(8,128)(2,1)S(1)}, u32[]{:S(2)}, u32[]{:S(2)}) collective-permute-start(bf16[128,2304]{1,0:T(8,128)(2,1)S(1)} %fusion.127), channel_id=1, source_target_pairs={{0,2},{1,3},{2,0},{3,1},{4,6},{5,7},{6,4},{7,5},{8,10},{9,11},{10,... | collective-permute-start | bytes 1769480 | tf_op jit(solution)/shard_map/ppermute | solution.py:325
  272.3 18.7 %collective-permute-start.8 = (bf16[128,2304]{1,0:T(8,128)(2,1)}, bf16[128,2304]{1,0:T(8,128)(2,1)}, u32[]{:S(2)}, u32[]{:S(2)}) collective-permute-start(bf16[128,2304]{1,0:T(8,128)(2,1)} %multiply_convert_fusion.11), channel_id=1, source_target_pairs={{4,8},{5,9},{6,10},{7,11},{8,4},{9,5},{10,6},{11,7},{20,24},{21,25... | collective-permute-start | bytes 1769480 | tf_op jit(solution)/shard_map/ppermute | solution.py:325
  275.4 18.2 %collective-permute-start.5 = (bf16[128,2304]{1,0:T(8,128)(2,1)}, bf16[128,2304]{1,0:T(8,128)(2,1)}, u32[]{:S(2)}, u32[]{:S(2)}) collective-permute-start(bf16[128,2304]{1,0:T(8,128)(2,1)} %multiply_convert_fusion.11), channel_id=1, source_target_pairs={{0,16},{1,17},{2,18},{3,19},{4,20},{5,21},{6,22},{7,23},{8,24},{9,... | collective-permute-start | bytes 1769480 | tf_op jit(solution)/shard_map/ppermute | solution.py:325
  287.2 18.0 %collective-permute-start.7 = (bf16[128,2304]{1,0:T(8,128)(2,1)}, bf16[128,2304]{1,0:T(8,128)(2,1)S(1)}, u32[]{:S(2)}, u32[]{:S(2)}) collective-permute-start(bf16[128,2304]{1,0:T(8,128)(2,1)} %collective-permute-done.6), channel_id=1, source_target_pairs={{0,16},{1,17},{2,18},{3,19},{4,20},{5,21},{6,22},{7,23},{8,24},{9,... | collective-permute-start | bytes 1769480 | tf_op jit(solution)/shard_map/ppermute | solution.py:325
  311.4 16.3 %collective-permute-start.10 = (bf16[128,2304]{1,0:T(8,128)(2,1)S(1)}, bf16[128,2304]{1,0:T(8,128)(2,1)S(1)}, u32[]{:S(2)}, u32[]{:S(2)}) collective-permute-start(bf16[128,2304]{1,0:T(8,128)(2,1)S(1)} %broadcast_select_fusion.3), channel_id=1, source_target_pairs={{0,16},{1,17},{2,18},{3,19},{4,20},{5,21},{6,22},{7,23},{8,24},{9,... | collective-permute-start | bytes 1769480 | tf_op jit(solution)/shard_map/ppermute | solution.py:325
  316.2 21.0 %collective-permute-start.13 = (bf16[128,2304]{1,0:T(8,128)(2,1)S(1)}, bf16[128,2304]{1,0:T(8,128)(2,1)S(1)}, u32[]{:S(2)}, u32[]{:S(2)}) collective-permute-start(bf16[128,2304]{1,0:T(8,128)(2,1)S(1)} %broadcast_select_fusion.2), channel_id=1, source_target_pairs={{0,16},{1,17},{2,18},{3,19},{4,20},{5,21},{6,22},{7,23},{8,24},{9,... | collective-permute-start | bytes 1769480 | tf_op jit(solution)/shard_map/ppermute | solution.py:325
  343.7 16.3 %collective-permute-start.14 = (bf16[128,2304]{1,0:T(8,128)(2,1)S(1)}, bf16[128,2304]{1,0:T(8,128)(2,1)S(1)}, u32[]{:S(2)}, u32[]{:S(2)}) collective-permute-start(bf16[128,2304]{1,0:T(8,128)(2,1)S(1)} %slice_bitcast_fusion.13), channel_id=1, source_target_pairs={{0,16},{1,17},{2,18},{3,19},{4,20},{5,21},{6,22},{7,23},{8,24},{9,... | collective-permute-start | bytes 1769480 | tf_op jit(solution)/shard_map/ppermute | solution.py:325
  345.6 27.1 %collective-permute-start.16 = (bf16[128,2304]{1,0:T(8,128)(2,1)S(1)}, bf16[128,2304]{1,0:T(8,128)(2,1)S(1)}, u32[]{:S(2)}, u32[]{:S(2)}) collective-permute-start(bf16[128,2304]{1,0:T(8,128)(2,1)S(1)} %slice_bitcast_fusion.11), channel_id=1, source_target_pairs={{0,16},{1,17},{2,18},{3,19},{4,20},{5,21},{6,22},{7,23},{8,24},{9,... | collective-permute-start | bytes 1769480 | tf_op jit(solution)/shard_map/ppermute | solution.py:325
  361.6 26.1 %collective-permute-start.19 = (bf16[128,2304]{1,0:T(8,128)(2,1)S(1)}, bf16[128,2304]{1,0:T(8,128)(2,1)S(1)}, u32[]{:S(2)}, u32[]{:S(2)}) collective-permute-start(bf16[128,2304]{1,0:T(8,128)(2,1)S(1)} %slice_bitcast_fusion.10), channel_id=1, source_target_pairs={{0,16},{1,17},{2,18},{3,19},{4,20},{5,21},{6,22},{7,23},{8,24},{9,... | collective-permute-start | bytes 1769480 | tf_op jit(solution)/shard_map/ppermute | solution.py:325
  374.2 20.0 %collective-permute-start.15 = (bf16[128,2304]{1,0:T(8,128)(2,1)S(1)}, bf16[128,2304]{1,0:T(8,128)(2,1)S(1)}, u32[]{:S(2)}, u32[]{:S(2)}) collective-permute-start(bf16[128,2304]{1,0:T(8,128)(2,1)S(1)} %slice_bitcast_fusion.12), channel_id=1, source_target_pairs={{0,16},{1,17},{2,18},{3,19},{4,20},{5,21},{6,22},{7,23},{8,24},{9,... | collective-permute-start | bytes 1769480 | tf_op jit(solution)/shard_map/ppermute | solution.py:325
  376.1 16.4 %collective-permute-start.21 = (bf16[128,2304]{1,0:T(8,128)(2,1)S(1)}, bf16[128,2304]{1,0:T(8,128)(2,1)S(1)}, u32[]{:S(2)}, u32[]{:S(2)}) collective-permute-start(bf16[128,2304]{1,0:T(8,128)(2,1)S(1)} %add_convert_fusion.3), channel_id=1, source_target_pairs={{4,8},{5,9},{6,10},{7,11},{8,4},{9,5},{10,6},{11,7},{20,24},{21,25... | collective-permute-start | bytes 1769480 | tf_op jit(solution)/shard_map/ppermute | solution.py:325
  406.8 20.4 %collective-permute-start.26 = (bf16[128,2304]{1,0:T(8,128)(2,1)S(1)}, bf16[128,2304]{1,0:T(8,128)(2,1)S(1)}, u32[]{:S(2)}, u32[]{:S(2)}) collective-permute-start(bf16[128,2304]{1,0:T(8,128)(2,1)S(1)} %get-tuple-element.136), channel_id=1, source_target_pairs={{4,8},{5,9},{6,10},{7,11},{8,4},{9,5},{10,6},{11,7},{20,24},{21,25... | collective-permute-start | bytes 1769480 | tf_op jit(solution)/shard_map/ppermute | solution.py:325
  416.5 23.1 %collective-permute-start.25 = (bf16[128,2304]{1,0:T(8,128)(2,1)S(1)}, bf16[128,2304]{1,0:T(8,128)(2,1)S(1)}, u32[]{:S(2)}, u32[]{:S(2)}) collective-permute-start(bf16[128,2304]{1,0:T(8,128)(2,1)S(1)} %collective-permute-done.24), channel_id=1, source_target_pairs={{0,16},{1,17},{2,18},{3,19},{4,20},{5,21},{6,22},{7,23},{8,24},{9,... | collective-permute-start | bytes 1769480 | tf_op jit(solution)/shard_map/ppermute | solution.py:325
  418.5 23.5 %collective-permute-start.29 = (bf16[128,2304]{1,0:T(8,128)(2,1)S(1)}, bf16[128,2304]{1,0:T(8,128)(2,1)S(1)}, u32[]{:S(2)}, u32[]{:S(2)}) collective-permute-start(bf16[128,2304]{1,0:T(8,128)(2,1)S(1)} %collective-permute-done.24), channel_id=1, source_target_pairs={{4,8},{5,9},{6,10},{7,11},{8,4},{9,5},{10,6},{11,7},{20,24},{21,25... | collective-permute-start | bytes 1769480 | tf_op jit(solution)/shard_map/ppermute | solution.py:325
  475.9 16.3 %collective-permute-start.32 = (bf16[128,2304]{1,0:T(8,128)(2,1)S(1)}, bf16[128,2304]{1,0:T(8,128)(2,1)S(1)}, u32[]{:S(2)}, u32[]{:S(2)}) collective-permute-start(bf16[128,2304]{1,0:T(8,128)(2,1)S(1)} %slice_bitcast_fusion.9), channel_id=1, source_target_pairs={{0,16},{1,17},{2,18},{3,19},{4,20},{5,21},{6,22},{7,23},{8,24},{9,... | collective-permute-start | bytes 1769480 | tf_op jit(solution)/shard_map/ppermute | solution.py:325
  476.1 26.5 %collective-permute-start.34 = (bf16[128,2304]{1,0:T(8,128)(2,1)S(1)}, bf16[128,2304]{1,0:T(8,128)(2,1)S(1)}, u32[]{:S(2)}, u32[]{:S(2)}) collective-permute-start(bf16[128,2304]{1,0:T(8,128)(2,1)S(1)} %slice_bitcast_fusion.7), channel_id=1, source_target_pairs={{0,16},{1,17},{2,18},{3,19},{4,20},{5,21},{6,22},{7,23},{8,24},{9,... | collective-permute-start | bytes 1769480 | tf_op jit(solution)/shard_map/ppermute | solution.py:325
  492.5 16.3 %collective-permute-start.38 = (bf16[128,2304]{1,0:T(8,128)(2,1)S(1)}, bf16[128,2304]{1,0:T(8,128)(2,1)S(1)}, u32[]{:S(2)}, u32[]{:S(2)}) collective-permute-start(bf16[128,2304]{1,0:T(8,128)(2,1)S(1)} %convert_element_type.466), channel_id=1, source_target_pairs={{0,4},{1,5},{2,6},{3,7},{12,8},{13,9},{14,10},{15,11},{16,20},{17,... | collective-permute-start | bytes 1769480 | tf_op jit(solution)/shard_map/ppermute | solution.py:325
  494.3 23.8 %collective-permute-start.37 = (bf16[128,2304]{1,0:T(8,128)(2,1)S(1)}, bf16[128,2304]{1,0:T(8,128)(2,1)S(1)}, u32[]{:S(2)}, u32[]{:S(2)}) collective-permute-start(bf16[128,2304]{1,0:T(8,128)(2,1)S(1)} %slice_bitcast_fusion.6), channel_id=1, source_target_pairs={{0,16},{1,17},{2,18},{3,19},{4,20},{5,21},{6,22},{7,23},{8,24},{9,... | collective-permute-start | bytes 1769480 | tf_op jit(solution)/shard_map/ppermute | solution.py:325
  504.1 17.1 %collective-permute-start.33 = (bf16[128,2304]{1,0:T(8,128)(2,1)S(1)}, bf16[128,2304]{1,0:T(8,128)(2,1)S(1)}, u32[]{:S(2)}, u32[]{:S(2)}) collective-permute-start(bf16[128,2304]{1,0:T(8,128)(2,1)S(1)} %slice_bitcast_fusion.8), channel_id=1, source_target_pairs={{0,16},{1,17},{2,18},{3,19},{4,20},{5,21},{6,22},{7,23},{8,24},{9,... | collective-permute-start | bytes 1769480 | tf_op jit(solution)/shard_map/ppermute | solution.py:325
  534.1 19.0 %collective-permute-start.42 = (bf16[128,2304]{1,0:T(8,128)(2,1)S(1)}, bf16[128,2304]{1,0:T(8,128)(2,1)S(1)}, u32[]{:S(2)}, u32[]{:S(2)}) collective-permute-start(bf16[128,2304]{1,0:T(8,128)(2,1)S(1)} %fusion.99), channel_id=1, source_target_pairs={{0,2},{1,3},{2,0},{3,1},{4,6},{5,7},{6,4},{7,5},{8,10},{9,11},{10,... | collective-permute-start | bytes 1769480 | tf_op jit(solution)/shard_map/ppermute | solution.py:325
  535.1 27.0 %collective-permute-start.41 = (bf16[128,2304]{1,0:T(8,128)(2,1)S(1)}, bf16[128,2304]{1,0:T(8,128)(2,1)S(1)}, u32[]{:S(2)}, u32[]{:S(2)}) collective-permute-start(bf16[128,2304]{1,0:T(8,128)(2,1)S(1)} %fusion.99), channel_id=1, source_target_pairs={{0,1},{1,0},{2,3},{3,2},{4,5},{5,4},{6,7},{7,6},{8,9},{9,8},{10,11... | collective-permute-start | bytes 1769480 | tf_op jit(solution)/shard_map/ppermute | solution.py:325
  633.6 182.1 %collective-permute-start.47 = (bf16[2,128,2304]{2,1,0:T(8,128)(2,1)}, bf16[2,128,2304]{2,1,0:T(8,128)(2,1)}, u32[]{:S(2)}, u32[]{:S(2)}) collective-permute-start(bf16[2,128,2304]{2,1,0:T(8,128)(2,1)} %slice_bitcast_fusion.1), channel_id=1, source_target_pairs={{0,1},{1,0},{2,3},{3,2},{4,5},{5,4},{6,7},{7,6},{8,9},{9,8},{10,11... | collective-permute-start | bytes 3538952 | tf_op jit(solution)/shard_map/ppermute | solution.py:325
  (156 other events, 1433.5 us)
